TPU v7x, 32 devices: a whole 2x2x4 slice. The times are simulated.
32 devices in a mesh: wide: 8 (over z, y), narrow: 4 (over x, core).
Axes of the slice: x: 2, y: 2, z: 4, core: 2. Of those that a mesh axis runs over, the one named last changes fastest.
Arguments:
- coefficients: bfloat16 [100, 131072], P(None, ('wide', 'narrow')), may hold values from -6 to 6
- neighbours: int32 [4, 131072], P(None, ('wide', 'narrow')), may hold values from 0 to 5119
- halo_blocks: int32 [32, 4, 2], P(('wide', 'narrow')), may hold values from 0 to 31, as said below
- recon_weight: bfloat16 [5, 75, 100], replicated, may hold values from -0.25 to 0.25
- owner_device: int32 [1024], P(('wide', 'narrow')), may hold values from 0 to 31, as said below
- work_count: int32 [1024], P(('wide', 'narrow')), may hold values from 1 to 4
Outputs:
- migrated_modal: bfloat16 [100, 131072], P(None, ('wide', 'narrow'))
- migrated_metric: float32 [6, 131072], P(None, ('wide', 'narrow'))
- migrated_work: float32 [131072], P(('wide', 'narrow'))
Inputs may be any that keep to these rules, and one draw needn't show every extreme that they name: `halo_blocks`: each device's list for one direction holds 2 different block numbers of that device. `owner_device`: every device receives exactly 32 blocks. Of one device's blocks, either exactly 4 or none go to devices of any one wide index. Two devices of the same wide index with narrow indices 2j and 2j + 1 together send either exactly 8 or none of their blocks to devices of any one wide index. For every wide index w and narrow indices a and c, exactly 8 of the blocks that devices of narrow index a send to wide index w go to the device of wide index w and narrow index c.
All inputs are finite; a program needn't handle non-finite values.
Results may differ from a plain program's by a relative error of at most 0.0004.
Values may be sent and summed in bfloat16 or wider, within the bound.
No kernel may reach another device: no remote copies, remote signals or barrier semaphores. Data moves between devices by JAX's collectives and lax.ppermute only.
A program may use at most 64 MiB of HBM per device.

v0:
```python
import jax
import jax.numpy as jnp
from jax import lax
from jax.sharding import PartitionSpec as P


def passed_along(value, axis, steps):
    count = lax.axis_size(axis)
    pairs = [(source, (source + steps) % count) for source in range(count)]
    return lax.ppermute(value, axis, pairs)


def metric_rows(derivs):
    vectors = derivs.reshape(derivs.shape[0] // 3, 3, derivs.shape[1])
    inverse = 1.0 / vectors.shape[0]
    along_x = vectors[:, 0]
    along_y = vectors[:, 1]
    along_z = vectors[:, 2]
    return jnp.stack(
        [
            1.0 + inverse * jnp.sum(along_x * along_x, axis=0),
            1.0 + inverse * jnp.sum(along_y * along_y, axis=0),
            1.0 + inverse * jnp.sum(along_z * along_z, axis=0),
            inverse * jnp.sum(along_x * along_y, axis=0),
            inverse * jnp.sum(along_x * along_z, axis=0),
            inverse * jnp.sum(along_y * along_z, axis=0),
        ]
    )


def determinant(components):
    metric_xx = components[0]
    metric_yy = components[1]
    metric_zz = components[2]
    metric_xy = components[3]
    metric_xz = components[4]
    metric_yz = components[5]
    return (
        metric_xx * (metric_yy * metric_zz - metric_yz * metric_yz)
        - metric_xy * (metric_xy * metric_zz - metric_yz * metric_xz)
        + metric_xz * (metric_xy * metric_yz - metric_yy * metric_xz)
    )


def first_slots(slot_of, slot_total, position):
    slot_ids = jnp.arange(slot_total, dtype=jnp.int32)
    matches = slot_of[None, :] == slot_ids[:, None]
    filled = jnp.any(matches, axis=1)
    picked = jnp.sum(jnp.where(matches, position[None, :], 0), axis=1)
    return (filled, picked)


def per_device(coefficients, neighbours, halo_blocks, recon_weight, owner_device, work_count):
    coeff_count, elem_count = coefficients.shape
    block_count = owner_device.shape[0]
    block_len = elem_count // block_count
    halo_count = halo_blocks.shape[2]
    wide_size = lax.axis_size("wide")
    narrow_size = lax.axis_size("narrow")
    blocked = coefficients.reshape(coeff_count, block_count, block_len)
    sending = halo_blocks[0]

    def outgoing(direction):
        return jnp.take(blocked, sending[direction], axis=1)

    def from_wide(block_set, offset):
        return passed_along(block_set, "wide", offset)

    def from_narrow(block_set, offset):
        return passed_along(block_set, "narrow", offset)

    arrived = [
        from_wide(outgoing(1), 1),
        from_wide(outgoing(0), -1),
        from_narrow(outgoing(3), 1),
        from_narrow(outgoing(2), -1),
    ]
    halo_cols = jnp.concatenate(arrived, axis=1).reshape(coeff_count, 4 * halo_count * block_len)
    derivs = jnp.dot(recon_weight[0], coefficients, preferred_element_type=jnp.float32)
    extended = jnp.concatenate([coefficients, halo_cols], axis=1)
    for face_index in range(4):
        gathered = jnp.take(extended, neighbours[face_index], axis=1)
        derivs = derivs + jnp.dot(
            recon_weight[face_index + 1], gathered, preferred_element_type=jnp.float32
        )
    components = metric_rows(derivs)
    work_est = jnp.repeat(work_count.astype(jnp.float32), block_len) * jnp.sqrt(
        determinant(components)
    )
    components, work_est = lax.optimization_barrier((components, work_est))
    stats = jnp.concatenate([components, work_est[None, :]], axis=0).reshape(
        7, block_count, block_len
    )
    wide_target = owner_device // narrow_size
    narrow_target = owner_device % narrow_size
    per_wide = max(1, block_count // wide_size)
    position = jnp.arange(block_count, dtype=jnp.int32)
    earlier = (wide_target[None, :] == wide_target[:, None]) & (
        position[None, :] < position[:, None]
    )
    rank_of = jnp.sum(earlier.astype(jnp.int32), axis=1)
    slot_total = wide_size * per_wide
    slot_ids = jnp.arange(slot_total, dtype=jnp.int32)
    filled, picked = first_slots(wide_target * per_wide + rank_of, slot_total, position)
    route_tag = jnp.where(filled, jnp.take(narrow_target, picked), -1)
    sent_stats = jnp.take(stats, picked, axis=1)
    sent_coeffs = jnp.take(blocked, picked, axis=1)
    stats_in, tags_in = (
        lax.all_to_all(sent_stats, "wide", split_axis=1, concat_axis=1, tiled=True),
        lax.all_to_all(
            route_tag.astype(jnp.float32)[None, :], "wide", split_axis=1, concat_axis=1, tiled=True
        ),
    )
    coeffs_in = lax.all_to_all(sent_coeffs, "wide", split_axis=1, concat_axis=1, tiled=True)
    route_values = tags_in[0].astype(jnp.int32)
    compact = jnp.argsort(jnp.where(route_values >= 0, 0, 1) * slot_total + slot_ids)[:block_count]
    grouping_route_values = jnp.take(route_values, compact)
    through = jnp.take(compact, jnp.argsort(grouping_route_values * block_count + position))
    relayed_coeffs = jnp.take(coeffs_in, through, axis=1)
    relayed_stats = jnp.take(stats_in, through, axis=1)
    new_coeffs = lax.all_to_all(relayed_coeffs, "narrow", split_axis=1, concat_axis=1, tiled=True)
    new_stats = lax.all_to_all(relayed_stats, "narrow", split_axis=1, concat_axis=1, tiled=True)
    flat_stats = new_stats.reshape(7, elem_count)
    return (new_coeffs.reshape(coeff_count, elem_count), flat_stats[:6], flat_stats[6])


def solution(mesh):
    return jax.shard_map(
        per_device,
        mesh=mesh,
        in_specs=(
            P(None, ("wide", "narrow")),
            P(None, ("wide", "narrow")),
            P(("wide", "narrow"), None, None),
            P(),
            P(("wide", "narrow")),
            P(("wide", "narrow")),
        ),
        out_specs=(P(None, ("wide", "narrow")), P(None, ("wide", "narrow")), P(("wide", "narrow"))),
        check_vma=False,
    )
```

profile of v0, /device:TPU:0, one launch (start us, length us, event | category | flops | bytes accessed | tf_op | source)
XLA Modules:
  0.0 172.5 jit_solution(7084079660594784279)
XLA Ops:
  0.6 1.0 slice_reduce_fusion.3
  1.7 1.3 copy.42
  4.1 3.0 %collective-permute-start = (bf16[100,2,128]{2,0,1:T(8,128)(2,1)S(1)}, bf16[100,2,128]{2,0,1:T(8,128)(2,1)S(1)}, u32[]{:S(2)}, u32[]{:S(2)}) collective-permute-start(bf16[100,2,128]{2,0,1:T(8,128)(2,1)S(1)} %select_bitcast_fusion.7), channel_id=1, source_target_pairs={{0,4},{4,8},{8,12},{12,16},{16,20},{20,24},{24,28},{28,0},{1,5},{5... | collective-permute-start | bytes 153608 | tf_op jit(solution)/shard_map/ppermute | solution.py:10
  7.8 3.1 %collective-permute-start.1 = (bf16[100,2,128]{2,0,1:T(8,128)(2,1)S(1)}, bf16[100,2,128]{2,0,1:T(8,128)(2,1)S(1)}, u32[]{:S(2)}, u32[]{:S(2)}) collective-permute-start(bf16[100,2,128]{2,0,1:T(8,128)(2,1)S(1)} %select_bitcast_fusion.6), channel_id=1, source_target_pairs={{0,28},{4,0},{8,4},{12,8},{16,12},{20,16},{24,20},{28,24},{1,29},{... | collective-permute-start | bytes 153608 | tf_op jit(solution)/shard_map/ppermute | solution.py:10
  12.8 1.7 collective-permute-start.3
  16.9 3.9 %all-to-all-start.1 = ((f32[1,8,4]{2,0,1:T(1,128)}), f32[1,8,4]{2,0,1:T(1,128)}, u32[]{:S(2)}, u32[]{:S(2)}) async-start(f32[1,8,4]{2,0,1:T(1,128)} %bitcast), calls=%async_computation.1 | async-start | bytes 8192 | tf_op jit(solution)/shard_map/all_to_all | solution.py:110
  23.7 1.4 copy.38
  25.1 1.8 %gather_fusion = bf16[32,100,128]{2,1,0:T(8,128)(2,1)} fusion(bf16[100,32,128]{2,0,1:T(8,128)(2,1)S(1)} %copy.31, s32[1024]{0:T(1024)} %copy-done.11), kind=kCustom, calls=%fused_computation.clone | custom fusion | bytes 1638528 | tf_op jit(solution)/shard_map/jit(_take)/gather | solution.py:107
  28.3 1.7 sort.31
  30.7 1.7 sort.32
  32.9 1.2 gather_fusion.3
  34.4 1.5 pad_maximum_fusion
  35.9 14.9 %gather_fusion.9 = bf16[4096,100]{1,0:T(8,128)(2,1)} fusion(bf16[100,5120]{0,1:T(8,128)(2,1)S(1)} %pad_maximum_fusion, s32[4096]{0:T(1024)S(1)} %fusion.33), kind=kCustom, calls=%fused_computation.3.clone | custom fusion | bytes 1654784 | tf_op jit(solution)/shard_map/jit(_take)/gather | solution.py:82
  50.8 14.9 %gather_fusion.10 = bf16[4096,100]{1,0:T(8,128)(2,1)} fusion(bf16[100,5120]{0,1:T(8,128)(2,1)S(1)} %pad_maximum_fusion, s32[4096]{0:T(1024)S(1)} %fusion.34), kind=kCustom, calls=%fused_computation.11.clone | custom fusion | bytes 1654784 | tf_op jit(solution)/shard_map/jit(_take)/gather | solution.py:82
  65.7 14.9 %gather_fusion.11 = bf16[4096,100]{1,0:T(8,128)(2,1)} fusion(bf16[100,5120]{0,1:T(8,128)(2,1)S(1)} %pad_maximum_fusion, s32[4096]{0:T(1024)S(1)} %fusion.35), kind=kCustom, calls=%fused_computation.12.clone | custom fusion | bytes 1654784 | tf_op jit(solution)/shard_map/jit(_take)/gather | solution.py:82
  80.6 14.9 %gather_fusion.12 = bf16[4096,100]{1,0:T(8,128)(2,1)} fusion(bf16[100,5120]{0,1:T(8,128)(2,1)S(1)} %pad_maximum_fusion, s32[4096]{0:T(1024)S(1)} %fusion.36), kind=kCustom, calls=%fused_computation.13.clone | custom fusion | bytes 1654784 | tf_op jit(solution)/shard_map/jit(_take)/gather | solution.py:82
  95.5 2.2 %fusion.3 = f32[75,4096]{1,0:T(8,128)S(1)} fusion(f32[75,4096]{1,0:T(8,128)S(1)} %fusion.24, bf16[4096,100]{1,0:T(8,128)(2,1)} %gather_fusion.9, pred[4096]{0:T(1024)(128)(4,1)S(1)} %copy-done.10, bf16[5,75,100]{2,1,0:T(8,128)(2,1)S(1)} %copy-done.5), kind=kOutput, calls=%fused_computation.22 | convolution fusion | flops 62156800 | bytes 3383296 | tf_op jit(solution)/shard_map/dot_general | solution.py:83
  97.7 0.8 fusion.2
  99.0 0.8 fusion.1
  100.2 0.8 fusion
  101.6 2.6 %multiply_reduce_fusion = (f32[4096]{0:T(1024)S(1)}, f32[4096]{0:T(1024)S(1)}, f32[4096]{0:T(1024)S(1)}, f32[4096]{0:T(1024)S(1)}, f32[4096]{0:T(1024)S(1)}, /*index=5*/f32[4096]{0:T(1024)S(1)}) fusion(f32[25,3,4096]{2,1,0:T(4,128)S(1)} %reshape.148), kind=kLoop, calls=%fused_computation.42 | loop fusion | flops 1204224 | bytes 1327104 | tf_op jit(solution)/shard_map/reduce_sum | solution.py:26
  105.9 5.9 %all-to-all-start.3 = ((f32[7,32,128]{2,0,1:T(8,128)}), f32[7,32,128]{2,0,1:T(8,128)S(1)}, u32[]{:S(2)}, u32[]{:S(2)}) async-start(f32[7,32,128]{2,0,1:T(8,128)} %select_bitcast_fusion.3), calls=%async_computation.3 | async-start | bytes 262144 | tf_op jit(solution)/shard_map/all_to_all | solution.py:109
  111.9 7.3 %all-to-all-done.3 = f32[7,32,128]{2,0,1:T(8,128)S(1)} async-done(((f32[7,32,128]{2,0,1:T(8,128)}), f32[7,32,128]{2,0,1:T(8,128)S(1)}, u32[]{:S(2)}, u32[]{:S(2)}) %all-to-all-start.3) | async-done | bytes 114720 | tf_op jit(solution)/shard_map/all_to_all | solution.py:109
  120.5 3.3 %all-to-all-start.4 = ((f32[7,32,128]{2,0,1:T(8,128)}), f32[7,32,128]{2,0,1:T(8,128)S(1)}, u32[]{:S(2)}, u32[]{:S(2)}) async-start(f32[7,32,128]{2,0,1:T(8,128)} %select_bitcast_fusion.2), calls=%async_computation.4 | async-start | bytes 262144 | tf_op jit(solution)/shard_map/all_to_all | solution.py:122
  123.9 1.0 select_bitcast_fusion.1
  124.9 3.5 %all-to-all-done.4 = f32[7,32,128]{2,0,1:T(8,128)S(1)} async-done(((f32[7,32,128]{2,0,1:T(8,128)}), f32[7,32,128]{2,0,1:T(8,128)S(1)}, u32[]{:S(2)}, u32[]{:S(2)}) %all-to-all-start.4) | async-done | bytes 114720 | tf_op jit(solution)/shard_map/all_to_all | solution.py:122
  128.4 3.6 %all-to-all-start = ((bf16[100,32,128]{2,0,1:T(8,128)(2,1)}), bf16[100,32,128]{2,0,1:T(8,128)(2,1)S(1)}, u32[]{:S(2)}, u32[]{:S(2)}) async-start(bf16[100,32,128]{2,0,1:T(8,128)(2,1)} %select_bitcast_fusion.1), calls=%async_computation | async-start | bytes 1703936 | tf_op jit(solution)/shard_map/all_to_all | solution.py:114
  132.6 20.9 %all-to-all-done = bf16[100,32,128]{2,0,1:T(8,128)(2,1)S(1)} async-done(((bf16[100,32,128]{2,0,1:T(8,128)(2,1)}), bf16[100,32,128]{2,0,1:T(8,128)(2,1)S(1)}, u32[]{:S(2)}, u32[]{:S(2)}) %all-to-all-start) | async-done | bytes 819232 | tf_op jit(solution)/shard_map/all_to_all | solution.py:114
  154.2 1.0 select_bitcast_fusion
  155.3 3.5 %all-to-all-start.2 = ((bf16[100,32,128]{2,0,1:T(8,128)(2,1)}), bf16[100,32,128]{2,0,1:T(8,128)(2,1)S(1)}, u32[]{:S(2)}, u32[]{:S(2)}) async-start(bf16[100,32,128]{2,0,1:T(8,128)(2,1)} %select_bitcast_fusion), calls=%async_computation.2 | async-start | bytes 1703936 | tf_op jit(solution)/shard_map/all_to_all | solution.py:121
  159.5 11.6 %all-to-all-done.2 = bf16[100,32,128]{2,0,1:T(8,128)(2,1)S(1)} async-done(((bf16[100,32,128]{2,0,1:T(8,128)(2,1)}), bf16[100,32,128]{2,0,1:T(8,128)(2,1)S(1)}, u32[]{:S(2)}, u32[]{:S(2)}) %all-to-all-start.2) | async-done | bytes 819232 | tf_op jit(solution)/shard_map/all_to_all | solution.py:121
  171.3 1.2 copy.43
  (115 shorter events, 18.3 us)
Async XLA Ops:
  3.1 11.5 %copy-start.17 = (s32[32]{0:T(128)S(1)}, s32[32]{0:T(128)}, u32[]{:S(2)}) copy-start(s32[32]{0:T(128)} %param.20) | copy-start | bytes 388
  3.1 17.7 %copy-start.6 = (s32[4,4096]{1,0:T(4,128)S(1)}, s32[4,4096]{1,0:T(4,128)}, u32[]{:S(2)}) copy-start(s32[4,4096]{1,0:T(4,128)} %param.17) | copy-start | bytes 196612
  3.4 19.9 %copy-start = (bf16[100,4096]{1,0:T(8,128)(2,1)S(1)}, bf16[100,4096]{1,0:T(8,128)(2,1)}, u32[]{:S(2)}) copy-start(bf16[100,4096]{1,0:T(8,128)(2,1)} %param.16) | copy-start | bytes 2457604
  3.5 19.9 %copy-start.5 = (bf16[5,75,100]{2,1,0:T(8,128)(2,1)S(1)}, bf16[5,75,100]{2,1,0:T(8,128)(2,1)}, u32[]{:S(2)}) copy-start(bf16[5,75,100]{2,1,0:T(8,128)(2,1)} %param.19) | copy-start | bytes 225004
  4.1 30.0 %collective-permute-start = (bf16[100,2,128]{2,0,1:T(8,128)(2,1)S(1)}, bf16[100,2,128]{2,0,1:T(8,128)(2,1)S(1)}, u32[]{:S(2)}, u32[]{:S(2)}) collective-permute-start(bf16[100,2,128]{2,0,1:T(8,128)(2,1)S(1)} %select_bitcast_fusion.7), channel_id=1, source_target_pairs={{0,4},{4,8},{8,12},{12,16},{16,20},{20,24},{24,28},{28,0},{1,5},{5... | collective-permute-start | bytes 153608 | tf_op jit(solution)/shard_map/ppermute | solution.py:10
  7.8 26.3 %collective-permute-start.1 = (bf16[100,2,128]{2,0,1:T(8,128)(2,1)S(1)}, bf16[100,2,128]{2,0,1:T(8,128)(2,1)S(1)}, u32[]{:S(2)}, u32[]{:S(2)}) collective-permute-start(bf16[100,2,128]{2,0,1:T(8,128)(2,1)S(1)} %select_bitcast_fusion.6), channel_id=1, source_target_pairs={{0,28},{4,0},{8,4},{12,8},{16,12},{20,16},{24,20},{28,24},{1,29},{... | collective-permute-start | bytes 153608 | tf_op jit(solution)/shard_map/ppermute | solution.py:10
  11.5 22.6 %collective-permute-start.2 = (bf16[100,2,128]{2,0,1:T(8,128)(2,1)S(1)}, bf16[100,2,128]{2,0,1:T(8,128)(2,1)S(1)}, u32[]{:S(2)}, u32[]{:S(2)}) collective-permute-start(bf16[100,2,128]{2,0,1:T(8,128)(2,1)S(1)} %select_bitcast_fusion.5), channel_id=1, source_target_pairs={{0,1},{1,2},{2,3},{3,0},{4,5},{5,6},{6,7},{7,4},{8,9},{9,10},{10,1... | collective-permute-start | bytes 153608 | tf_op jit(solution)/shard_map/ppermute | solution.py:10
  12.8 21.3 %collective-permute-start.3 = (bf16[100,2,128]{2,0,1:T(8,128)(2,1)}, bf16[100,2,128]{2,0,1:T(8,128)(2,1)S(1)}, u32[]{:S(2)}, u32[]{:S(2)}) collective-permute-start(bf16[100,2,128]{2,0,1:T(8,128)(2,1)} %select_bitcast_fusion.4), channel_id=1, source_target_pairs={{0,3},{1,0},{2,1},{3,2},{4,7},{5,4},{6,5},{7,6},{8,11},{9,8},{10,9... | collective-permute-start | bytes 153608 | tf_op jit(solution)/shard_map/ppermute | solution.py:10
  15.0 7.7 %copy-start.11 = (s32[1024]{0:T(1024)}, s32[1024]{0:T(1024)S(1)}, u32[]{:S(2)}) copy-start(s32[1024]{0:T(1024)S(1)} %pad_clamp_fusion.7) | copy-start | bytes 12292
  16.9 10.5 %all-to-all-start.1 = ((f32[1,8,4]{2,0,1:T(1,128)}), f32[1,8,4]{2,0,1:T(1,128)}, u32[]{:S(2)}, u32[]{:S(2)}) async-start(f32[1,8,4]{2,0,1:T(1,128)} %bitcast), calls=%async_computation.1 | async-start | bytes 8192 | tf_op jit(solution)/shard_map/all_to_all | solution.py:110
  25.1 1.8 %copy-start.18 = (s32[32]{0:T(128)S(1)}, s32[32]{0:T(128)}, u32[]{:S(2)}) copy-start(s32[32]{0:T(128)} %param.21) | copy-start | bytes 388
  32.4 0.5 copy-start.15
  80.6 14.9 %copy-start.10 = (pred[4096]{0:T(1024)(128)(4,1)S(1)}, pred[4096]{0:T(1024)(128)(4,1)}, u32[]{:S(2)}) copy-start(pred[4096]{0:T(1024)(128)(4,1)} %compare_and_fusion.3) | copy-start | bytes 12292
  95.5 2.2 %copy-start.3 = (bf16[4096,100]{1,0:T(8,128)(2,1)S(1)}, bf16[4096,100]{1,0:T(8,128)(2,1)}, u32[]{:S(2)}) copy-start(bf16[4096,100]{1,0:T(8,128)(2,1)} %gather_fusion.10) | copy-start | bytes 2457604
  95.5 2.2 %copy-start.9 = (pred[4096]{0:T(1024)(128)(4,1)S(1)}, pred[4096]{0:T(1024)(128)(4,1)}, u32[]{:S(2)}) copy-start(pred[4096]{0:T(1024)(128)(4,1)} %compare_and_fusion.2) | copy-start | bytes 12292
  97.7 1.2 copy-start.2
  97.7 1.2 copy-start.7
  99.0 1.2 copy-start.1
  99.0 1.2 copy-start.8
  101.5 2.6 %copy-start.14 = (f32[32]{0:T(128)S(1)}, f32[32]{0:T(128)}, u32[]{:S(2)}) copy-start(f32[32]{0:T(128)} %convert_element_type.19) | copy-start | bytes 388
  101.6 3.6 %copy-start.12 = (pred[32]{0:T(512)(128)(4,1)S(1)}, pred[32]{0:T(512)(128)(4,1)}, u32[]{:S(2)}) copy-start(pred[32]{0:T(512)(128)(4,1)} %get-tuple-element.29) | copy-start | bytes 100
  101.6 10.3 %copy-start.13 = (s32[32]{0:T(128)S(1)}, s32[32]{0:T(128)}, u32[]{:S(2)}) copy-start(s32[32]{0:T(128)} %gather_fusion.3) | copy-start | bytes 388
  101.6 10.3 %copy-start.16 = (s32[32]{0:T(128)S(1)}, s32[32]{0:T(128)}, u32[]{:S(2)}) copy-start(s32[32]{0:T(128)} %copy-done.15) | copy-start | bytes 388
  104.2 19.7 %copy-start.4 = (bf16[32,100,128]{2,1,0:T(8,128)(2,1)S(1)}, bf16[32,100,128]{2,1,0:T(8,128)(2,1)}, u32[]{:S(2)}) copy-start(bf16[32,100,128]{2,1,0:T(8,128)(2,1)} %gather_fusion) | copy-start | bytes 2457604
  105.9 13.2 %all-to-all-start.3 = ((f32[7,32,128]{2,0,1:T(8,128)}), f32[7,32,128]{2,0,1:T(8,128)S(1)}, u32[]{:S(2)}, u32[]{:S(2)}) async-start(f32[7,32,128]{2,0,1:T(8,128)} %select_bitcast_fusion.3), calls=%async_computation.3 | async-start | bytes 262144 | tf_op jit(solution)/shard_map/all_to_all | solution.py:109
  120.5 7.9 %all-to-all-start.4 = ((f32[7,32,128]{2,0,1:T(8,128)}), f32[7,32,128]{2,0,1:T(8,128)S(1)}, u32[]{:S(2)}, u32[]{:S(2)}) async-start(f32[7,32,128]{2,0,1:T(8,128)} %select_bitcast_fusion.2), calls=%async_computation.4 | async-start | bytes 262144 | tf_op jit(solution)/shard_map/all_to_all | solution.py:122
  128.4 25.1 %all-to-all-start = ((bf16[100,32,128]{2,0,1:T(8,128)(2,1)}), bf16[100,32,128]{2,0,1:T(8,128)(2,1)S(1)}, u32[]{:S(2)}, u32[]{:S(2)}) async-start(bf16[100,32,128]{2,0,1:T(8,128)(2,1)} %select_bitcast_fusion.1), calls=%async_computation | async-start | bytes 1703936 | tf_op jit(solution)/shard_map/all_to_all | solution.py:114
  155.3 15.8 %all-to-all-start.2 = ((bf16[100,32,128]{2,0,1:T(8,128)(2,1)}), bf16[100,32,128]{2,0,1:T(8,128)(2,1)S(1)}, u32[]{:S(2)}, u32[]{:S(2)}) async-start(bf16[100,32,128]{2,0,1:T(8,128)(2,1)} %select_bitcast_fusion), calls=%async_computation.2 | async-start | bytes 1703936 | tf_op jit(solution)/shard_map/all_to_all | solution.py:121
where the time goes:
time: 173 us
  local copies, waits for them, and re-layouts  78.2 us (45%)
  waiting for transfers between devices  43.3 us (25%)
  starting transfers between devices  27.9 us (16%)
  other arithmetic  16.9 us (10%)
  matrix products  5.01 us (3%)
    gather x4, local copies, waits for them, and re-layouts, per_device(): gathered = jnp.take(extended, neighbours[face_index], axis=1)  59.6 us
    all_to_all x1, waiting for transfers between devices, per_device(): lax.all_to_all(sent_coeffs, 'wide', split_axis=1, concat_axis=1, tiled=True)  20.9 us
    all_to_all x1, waiting for transfers between devices, per_device(): lax.all_to_all(relayed_coeffs, 'narrow', split_axis=1, concat_axis=1, til...  11.6 us
    ppermute x4, starting transfers between devices, passed_along(): return lax.ppermute(value, axis, pairs)  7.78 us
    all_to_all x1, waiting for transfers between devices, per_device(): lax.all_to_all(sent_stats, 'wide', split_axis=1, concat_axis=1, tiled=True)  7.3 us
    all_to_all x1, starting transfers between devices, per_device(): lax.all_to_all(sent_stats, 'wide', split_axis=1, concat_axis=1, tiled=True)  5.89 us
    unnamed x42, local copies, waits for them, and re-layouts  5.4 us
    dot_general x4, matrix products, per_device(): jnp.dot(recon_weight[face_index + 1], gathered, preferred_element_type=jn...  4.66 us
  transfers between devices with their start and end apart: 9, of which 4 were waited for; matrix products, arithmetic and copies ran while one was open for 11% of the time, Pallas kernels for 0%

commit v1 on v0

v1 whole, which is shorter than its diff:
```python
import jax
import jax.numpy as jnp
from jax import lax
from jax.experimental import pallas as pl
from jax.experimental.pallas import tpu as pltpu
from jax.sharding import PartitionSpec as P

f32 = jnp.float32
bf16 = jnp.bfloat16
LANES = 128
FACES = 4

SMEM = pl.BlockSpec(memory_space=pltpu.SMEM)
VMEM = pl.BlockSpec(memory_space=pltpu.VMEM)
HBM = pl.BlockSpec(memory_space=pl.ANY)


def passed_along(value, axis, steps):
    count = lax.axis_size(axis)
    pairs = [(source, (source + steps) % count) for source in range(count)]
    return lax.ppermute(value, axis, pairs)


def swapped(value, axis, flip):
    count = lax.axis_size(axis)
    return lax.ppermute(value, axis, [(source, source ^ flip) for source in range(count)])


def padded_rows(rows):
    return (rows // 8 + 1) * 8


def pack_kernel(wide, narrow, coef, halo_blocks, owner, *refs):
    halos, packed, slot, filled = refs[:4], refs[4], refs[5], refs[6]
    rows = coef.shape[0]
    slots, tall = packed.shape[0], packed.shape[1]
    blocks = owner.shape[0]
    per_wide = slots // wide
    for k in range(4):
        for h in range(halo_blocks.shape[2]):
            at = pl.multiple_of(halo_blocks[0, k, h] * LANES, LANES)
            halos[k][h] = coef[:, pl.ds(at, LANES)]

    def clear(w, _):
        filled[w] = 0
        return 0

    lax.fori_loop(0, wide, clear, 0)
    if slots > blocks:
        for t in range(slots):
            packed[t, rows:tall, :] = jnp.full((tall - rows, LANES), -1, bf16)
    for b in range(blocks):
        target = owner[b]
        w = target // narrow
        t = w * per_wide + filled[w]
        filled[w] = filled[w] + 1
        slot[b] = t
        packed[t, 0:rows, :] = coef[:, b * LANES : (b + 1) * LANES]
        packed[t, rows:tall, :] = jnp.full((tall - rows, LANES), (target % narrow).astype(f32)).astype(
            bf16
        )


def pack(coef, halo_blocks, owner, wide, narrow):
    rows, count = coef.shape
    blocks = owner.shape[0]
    slots = wide * max(1, blocks // wide)
    halo = jax.ShapeDtypeStruct((halo_blocks.shape[2], rows, LANES), bf16)
    return pl.pallas_call(
        lambda *refs: pack_kernel(wide, narrow, *refs),
        out_shape=[halo] * 4
        + [
            jax.ShapeDtypeStruct((slots, padded_rows(rows), LANES), bf16),
            jax.ShapeDtypeStruct((blocks,), jnp.int32),
        ],
        in_specs=[VMEM, SMEM, SMEM],
        out_specs=[VMEM] * 5 + [SMEM],
        scratch_shapes=[pltpu.SMEM((wide,), jnp.int32)],
        cost_estimate=pl.CostEstimate(flops=0, bytes_accessed=4 * rows * count, transcendentals=0),
        name="pack",
    )(coef, halo_blocks, owner)


def metric_kernel(nb, slot, count, coef, h0, h1, h2, h3, w, out, y0, y1, y2, y3, acc0, acc1, wp, idx, sem):
    tables = (y0, y1, y2, y3)
    accs = (acc0, acc1)
    rows = w.shape[1]
    third = rows // 3
    elems = coef.shape[1]
    blocks = elems // LANES
    contract = (((1,), (1,)), ((), ()))

    def fetch(b, place):
        at = pl.multiple_of(b * LANES, LANES)
        return pltpu.make_async_copy(nb.at[:, pl.ds(at, LANES)], idx.at[place], sem.at[place])

    fetch(0, 0).start()
    fetch(1, 1).start()
    lane = lax.broadcasted_iota(jnp.int32, (LANES, rows), 0)
    row = lax.broadcasted_iota(jnp.int32, (LANES, rows), 1)
    place = ((row == 3 * (lane % 32) + lane // 32) & (lane % 32 < third)).astype(bf16)
    for f in range(FACES + 1):
        wp[f] = jnp.dot(place, w[f], preferred_element_type=f32).astype(bf16)
    step = 512

    def project(i, _):
        at = pl.multiple_of(i * step, step)
        cols = coef[:, pl.ds(at, step)].T
        for f in range(FACES):
            tables[f][pl.ds(at, step), :] = lax.dot_general(
                cols, wp[f + 1], contract, preferred_element_type=f32
            )
        return 0

    lax.fori_loop(0, elems // step, project, 0)
    for k, halo in enumerate((h0, h1, h2, h3)):
        for h in range(halo.shape[0]):
            cols = halo[h].T
            at = elems + (k * halo.shape[0] + h) * LANES
            for f in range(FACES):
                tables[f][pl.ds(at, LANES), :] = lax.dot_general(
                    cols, wp[f + 1], contract, preferred_element_type=f32
                )

    def gather(place):
        for e in range(LANES):
            part = [tables[f][pl.ds(idx[place, f, e], 1), :] for f in range(FACES)]
            accs[place][pl.ds(e, 1), :] = (part[0] + part[1]) + (part[2] + part[3])

    def metric(b, place):
        at = pl.multiple_of(b * LANES, LANES)
        d = accs[place][...].T + jnp.dot(
            wp[0], coef[:, pl.ds(at, LANES)], preferred_element_type=f32
        )
        x, y, z = d[0:32], d[32:64], d[64:96]
        inverse = 1.0 / third

        def mean(p):
            return inverse * jnp.sum(p, axis=0, keepdims=True)

        xx, yy, zz = 1.0 + mean(x * x), 1.0 + mean(y * y), 1.0 + mean(z * z)
        xy, xz, yz = mean(x * y), mean(x * z), mean(y * z)
        det = xx * (yy * zz - yz * yz) - xy * (xy * zz - yz * xz) + xz * (xy * yz - yy * xz)
        work = count[b].astype(f32) * jnp.sqrt(det)
        out[slot[b]] = jnp.concatenate([xx, yy, zz, xy, xz, yz, work, work], axis=0)

    def pair(i, _):
        b = 2 * i
        fetch(b, 0).wait()
        gather(0)

        @pl.when(i + 1 < blocks // 2)
        def _():
            fetch(b + 2, 0).start()

        fetch(b + 1, 1).wait()
        metric(b, 0)
        gather(1)

        @pl.when(i + 1 < blocks // 2)
        def _():
            fetch(b + 3, 1).start()

        metric(b + 1, 1)
        return 0

    lax.fori_loop(0, blocks // 2, pair, 0)


def metrics(nb, slot, count, coef, halos, w, slots):
    elems = coef.shape[1]
    table = elems + sum(h.shape[0] for h in halos) * LANES
    return pl.pallas_call(
        metric_kernel,
        out_shape=jax.ShapeDtypeStruct((slots, 8, LANES), f32),
        in_specs=[HBM, SMEM, SMEM] + [VMEM] * 6,
        out_specs=VMEM,
        scratch_shapes=[pltpu.VMEM((table, LANES), f32)] * FACES
        + [
            pltpu.VMEM((LANES, LANES), f32),
            pltpu.VMEM((LANES, LANES), f32),
            pltpu.VMEM((FACES + 1, LANES, w.shape[2]), bf16),
            pltpu.SMEM((2, FACES, LANES), jnp.int32),
            pltpu.SemaphoreType.DMA((2,)),
        ],
        cost_estimate=pl.CostEstimate(
            flops=2 * table * 5 * LANES * LANES, bytes_accessed=30 * elems * LANES, transcendentals=elems
        ),
        name="metric",
    )(nb, slot, count, coef, *halos, w)


def relay_kernel(narrow, arrived, *refs):
    sends, order, words, tags, filled, sem = refs[:narrow], *refs[narrow:]
    slots, tall = arrived.shape[0], arrived.shape[1]
    per, rows = sends[0].shape[0], sends[0].shape[1]
    for t in range(slots):
        words[t : t + 1, :] = arrived[t, tall - 8 : tall, :].astype(f32)[7:8].astype(jnp.int32)
    copy = pltpu.make_async_copy(words, tags, sem)
    copy.start()
    copy.wait()
    for c in range(narrow + 1):
        filled[c] = c * per
    for t in range(slots):
        tag = tags[t, 0]
        c = jnp.where(tag < 0, narrow, tag)
        at = filled[c]
        order[at] = t
        filled[c] = at + 1
    mine = lax.axis_index("narrow")
    for k in range(narrow):
        for j in range(per):
            sends[k][j] = arrived[order[(mine ^ k) * per + j], 0:rows, :]


def relay(arrived, rows, narrow, blocks):
    slots = arrived.shape[0]
    per = blocks // narrow
    *sends, order = pl.pallas_call(
        lambda *refs: relay_kernel(narrow, *refs),
        out_shape=[jax.ShapeDtypeStruct((per, rows, LANES), bf16)] * narrow
        + [jax.ShapeDtypeStruct((blocks + slots,), jnp.int32)],
        in_specs=[VMEM],
        out_specs=[VMEM] * narrow + [SMEM],
        scratch_shapes=[
            pltpu.VMEM((slots, LANES), jnp.int32),
            pltpu.SMEM((slots, LANES), jnp.int32),
            pltpu.SMEM((narrow + 1,), jnp.int32),
            pltpu.SemaphoreType.DMA(()),
        ],
        cost_estimate=pl.CostEstimate(
            flops=0, bytes_accessed=4 * blocks * rows * LANES, transcendentals=0
        ),
        name="relay",
    )(arrived)
    return sends, order


def relay_stats_kernel(narrow, arrived, order, *sends):
    per = sends[0].shape[0]
    mine = lax.axis_index("narrow")
    for k in range(narrow):
        for j in range(per):
            sends[k][j] = arrived[order[(mine ^ k) * per + j]]


def relay_stats(arrived, order, narrow, blocks):
    per = blocks // narrow
    return pl.pallas_call(
        lambda *refs: relay_stats_kernel(narrow, *refs),
        out_shape=[jax.ShapeDtypeStruct((per, 8, LANES), f32)] * narrow,
        in_specs=[VMEM, SMEM],
        out_specs=[VMEM] * narrow,
        cost_estimate=pl.CostEstimate(flops=0, bytes_accessed=64 * blocks * LANES, transcendentals=0),
        name="relay_stats",
    )(arrived, order)


def place_kernel(*refs):
    parts, out = refs[:-1], refs[-1]
    per = parts[0].shape[0]
    mine = lax.axis_index("narrow")
    for k, part in enumerate(parts):
        for j in range(per):
            at = pl.multiple_of(((mine ^ k) * per + j) * LANES, LANES)
            out[:, pl.ds(at, LANES)] = part[j]


def place(parts):
    per, rows, _ = parts[0].shape
    return pl.pallas_call(
        place_kernel,
        out_shape=jax.ShapeDtypeStruct((rows, len(parts) * per * LANES), bf16),
        in_specs=[VMEM] * len(parts),
        out_specs=VMEM,
        name="place",
    )(*parts)


def place_stats_kernel(*refs):
    parts, metric, work = refs[:-2], refs[-2], refs[-1]
    per = parts[0].shape[0]
    mine = lax.axis_index("narrow")
    for k, part in enumerate(parts):
        for j in range(per):
            t = (mine ^ k) * per + j
            at = pl.multiple_of(t * LANES, LANES)
            metric[:, pl.ds(at, LANES)] = part[j, 0:6, :]
            work[pl.ds(t, 1), :] = part[j, 6:7, :]


def place_stats(parts):
    per = parts[0].shape[0]
    blocks = len(parts) * per
    return pl.pallas_call(
        place_stats_kernel,
        out_shape=[
            jax.ShapeDtypeStruct((6, blocks * LANES), f32),
            jax.ShapeDtypeStruct((blocks, LANES), f32),
        ],
        in_specs=[VMEM] * len(parts),
        out_specs=[VMEM] * 2,
        name="place_stats",
    )(*parts)


def per_device(coefficients, neighbours, halo_blocks, recon_weight, owner_device, work_count):
    wide = lax.axis_size("wide")
    narrow = lax.axis_size("narrow")
    rows, elems = coefficients.shape
    blocks = owner_device.shape[0]
    to0, to1, to2, to3, packed, slot = pack(coefficients, halo_blocks, owner_device, wide, narrow)
    halos = [
        passed_along(to1, "wide", 1),
        passed_along(to0, "wide", -1),
        passed_along(to3, "narrow", 1),
        passed_along(to2, "narrow", -1),
    ]
    arrived = lax.all_to_all(packed, "wide", 0, 0, tiled=True)
    stats = metrics(
        neighbours, slot, work_count, coefficients, halos, recon_weight, packed.shape[0]
    )
    stats_arrived = lax.all_to_all(stats, "wide", 0, 0, tiled=True)
    sends, order = relay(arrived, rows, narrow, blocks)
    parts = [sends[0]] + [swapped(sends[k], "narrow", k) for k in range(1, narrow)]
    stats_sends = relay_stats(stats_arrived, order, narrow, blocks)
    stats_parts = [stats_sends[0]] + [
        swapped(stats_sends[k], "narrow", k) for k in range(1, narrow)
    ]
    modal = place(parts)
    metric, work = place_stats(stats_parts)
    return modal, metric, work.reshape(-1)


def solution(mesh):
    return jax.shard_map(
        per_device,
        mesh=mesh,
        in_specs=(
            P(None, ("wide", "narrow")),
            P(None, ("wide", "narrow")),
            P(("wide", "narrow"), None, None),
            P(),
            P(("wide", "narrow")),
            P(("wide", "narrow")),
        ),
        out_specs=(P(None, ("wide", "narrow")), P(None, ("wide", "narrow")), P(("wide", "narrow"))),
        check_vma=False,
    )
```

time: 173 us -> 82.7 us (0.48)
  local copies, waits for them, and re-layouts: 78.2 us -> 4.06 us
  Pallas kernels: 0 us -> 32.5 us
  waiting for transfers between devices: 43.3 us -> 20.1 us
  other arithmetic: 16.9 us -> 0 us
  matrix products: 5.01 us -> 0 us
  starting transfers between devices: 27.9 us -> 24.1 us
    gather x15 -> x0, local copies, waits for them, and re-layouts: 68.3 us -> none  [the longest x4 59.6 us: per_device(): gathered = jnp.take(extended, neighbours[face_index], axis=1)]
    all_to_all x5 -> x2, waiting for transfers between devices: 43.3 us -> 2.28 us  [the longest x1 2.28 us: per_device(): stats_arrived = lax.all_to_all(stats, 'wide', 0, 0, tiled=True)]
    pallas_call x0 -> x6, Pallas kernels: none -> 32.5 us  [the longest x1 21.4 us: metrics(): pl.pallas_call(metric_kernel, out_shape=jax.ShapeDtypeStruct((slots, 8, L...]
    ppermute x4, waiting for transfers between devices: 0.01 us -> 13.4 us  [passed_along(): return lax.ppermute(value, axis, pairs)]
    all_to_all x5 -> x2, starting transfers between devices: 20.1 us -> 13 us  [the longest x1 7.45 us: per_device(): arrived = lax.all_to_all(packed, 'wide', 0, 0, tiled=True)]
    dot_general x5 -> x0, matrix products: 5.01 us -> none  [the longest x4 4.66 us: per_device(): jnp.dot(recon_weight[face_index + 1], gathered, preferred_element_type=jn...]
    ppermute x0 -> x6, starting transfers between devices: none -> 4.58 us  [swapped(): lax.ppermute(value, axis, [(source, source ^ flip) for source in range(co...]
    select_n x16 -> x0, other arithmetic: 4.58 us -> none  [the longest x1 1.05 us: per_device(): sent_coeffs = jnp.take(blocked, picked, axis=1)]
  transfers between devices with their start and end apart: 9 -> 12, of which waited for: 4 -> 3; matrix products, arithmetic and copies ran while one was open for 11% -> 0% of each run, Pallas kernels for 0% -> 34%
where the time goes in v1:
time: 82.7 us; the launch traced here: 81.7 us
  Pallas kernels  32.5 us (39%)
  starting transfers between devices  24.1 us (29%)
  waiting for transfers between devices  20.1 us (24%)
  local copies, waits for them, and re-layouts  4.06 us (5%)
    pallas_call x1, Pallas kernels, metrics(): pl.pallas_call(metric_kernel, out_shape=jax.ShapeDtypeStruct((slots, 8, L...  21.4 us
    ppermute x4, waiting for transfers between devices, passed_along(): return lax.ppermute(value, axis, pairs)  13.4 us
    all_to_all x1, starting transfers between devices, per_device(): arrived = lax.all_to_all(packed, 'wide', 0, 0, tiled=True)  7.45 us
    ppermute x4, starting transfers between devices, passed_along(): return lax.ppermute(value, axis, pairs)  6.53 us
    all_to_all x1, starting transfers between devices, per_device(): stats_arrived = lax.all_to_all(stats, 'wide', 0, 0, tiled=True)  5.58 us
    ppermute x6, starting transfers between devices, swapped(): lax.ppermute(value, axis, [(source, source ^ flip) for source in range(co...  4.58 us
    ppermute x6, waiting for transfers between devices, swapped(): lax.ppermute(value, axis, [(source, source ^ flip) for source in range(co...  4.45 us
    unnamed x33, local copies, waits for them, and re-layouts  4.06 us
  transfers between devices with their start and end apart: 12, of which 3 were waited for; matrix products, arithmetic and copies ran while one was open for 0% of the time, Pallas kernels for 34%

profile of v1, /device:TPU:0, one launch (start us, length us, event | category | flops | bytes accessed | tf_op | source)
XLA Modules:
  0.0 81.7 jit_solution(3233200443132448050)
XLA Ops:
  0.6 1.3 %copy.9.refs_1_ = s32[1,4,2]{2,1,0:T(4,128)} copy(s32[1,4,2]{1,2,0:T(2,128)} %param.8) | data formatting | bytes 64 | tf_op args[2]
  2.0 2.6 %pack.1 = (bf16[2,100,128]{2,1,0:T(8,128)(2,1)}, bf16[2,100,128]{2,1,0:T(8,128)(2,1)}, bf16[2,100,128]{2,1,0:T(8,128)(2,1)}, bf16[2,100,128]{2,1,0:T(8,128)(2,1)...) custom-call(bf16[100,4096]{1,0:T(8,128)(2,1)} %coef.1, s32[1,4,2]{2,1,0:T(4,128)} %copy.9.refs_1_, s32[32]{0:T(128)} %refs_2_.1), custom_call_target="tpu_custom_call" | custom-call | bytes 1638400 | tf_op jit(solution)/shard_map/pack/pallas_call | solution.py:69
  4.5 0.0 copy-start.10
  4.6 7.5 %all-to-all-start = ((bf16[32,104,128]{2,1,0:T(8,128)(2,1)}), bf16[32,104,128]{2,1,0:T(8,128)(2,1)S(1)}, u32[]{:S(2)}, u32[]{:S(2)}) async-start(bf16[32,104,128]{2,1,0:T(8,128)(2,1)} %get-tuple-element.20), calls=%async_computation | async-start | bytes 1703936 | tf_op jit(solution)/shard_map/all_to_all | solution.py:319
  12.0 2.0 %collective-permute-start.3 = (bf16[2,100,128]{2,1,0:T(8,128)(2,1)S(1)}, bf16[2,100,128]{2,1,0:T(8,128)(2,1)S(1)}, u32[]{:S(2)}, u32[]{:S(2)}) collective-permute-start(bf16[2,100,128]{2,1,0:T(8,128)(2,1)S(1)} %copy-done.12), channel_id=1, source_target_pairs={{0,4},{4,8},{8,12},{12,16},{16,20},{20,24},{24,28},{28,0},{1,5},{5... | collective-permute-start | bytes 153608 | tf_op jit(solution)/shard_map/ppermute | solution.py:21
  14.1 2.8 %collective-permute-start.4 = (bf16[2,100,128]{2,1,0:T(8,128)(2,1)S(1)}, bf16[2,100,128]{2,1,0:T(8,128)(2,1)S(1)}, u32[]{:S(2)}, u32[]{:S(2)}) collective-permute-start(bf16[2,100,128]{2,1,0:T(8,128)(2,1)S(1)} %copy-done.10), channel_id=1, source_target_pairs={{0,28},{4,0},{8,4},{12,8},{16,12},{20,16},{24,20},{28,24},{1,29},{... | collective-permute-start | bytes 153608 | tf_op jit(solution)/shard_map/ppermute | solution.py:21
  16.8 1.7 %collective-permute-start.6 = (bf16[2,100,128]{2,1,0:T(8,128)(2,1)S(1)}, bf16[2,100,128]{2,1,0:T(8,128)(2,1)S(1)}, u32[]{:S(2)}, u32[]{:S(2)}) collective-permute-start(bf16[2,100,128]{2,1,0:T(8,128)(2,1)S(1)} %copy-done.8), channel_id=1, source_target_pairs={{0,3},{1,0},{2,1},{3,2},{4,7},{5,4},{6,5},{7,6},{8,11},{9,8},{10,9... | collective-permute-start | bytes 153608 | tf_op jit(solution)/shard_map/ppermute | solution.py:21
  18.6 13.4 %collective-permute-done.3.h0 = bf16[2,100,128]{2,1,0:T(8,128)(2,1)S(1)} collective-permute-done((bf16[2,100,128]{2,1,0:T(8,128)(2,1)S(1)}, bf16[2,100,128]{2,1,0:T(8,128)(2,1)S(1)}, u32[]{:S(2)}, u32[]{:S(2)}) %collective-permute-start.3) | collective-permute-done | bytes 51232 | tf_op jit(solution)/shard_map/ppermute | solution.py:21
  32.0 0.6 copy-done.11
  32.6 0.0 copy-done.13
  32.6 0.0 copy-done.14
  32.6 0.0 copy-done.15
  32.6 21.4 %metric.1 = f32[32,8,128]{2,1,0:T(8,128)} custom-call(s32[4,4096]{1,0:T(4,128)} %nb.1, s32[32]{0:T(128)} %get-tuple-element.25.slot, s32[32]{0:T(128)} %count.1, bf16[100,4096]{1,0:T(8,128)(2,1)} %coef.1, bf16[2,100,128]{2,1,0:T(8,128)(2,1)} %copy-done.11, bf16[2,100,128]{2,1,0:T(8,128)(2,1)} %copy-done.13, bf16[2,100,128]{2,1,0:T(8,128)(2,1)} %copy-done.14, ...), custom_call_target="tpu_custom_call" | custom-call | flops 838860800 | bytes 15728640 | tf_op jit(solution)/shard_map/metric/pallas_call | solution.py:173
  54.0 0.0 copy-start
  54.1 5.6 %all-to-all-start.1 = ((f32[32,8,128]{2,1,0:T(8,128)}), f32[32,8,128]{2,1,0:T(8,128)S(1)}, u32[]{:S(2)}, u32[]{:S(2)}) async-start(f32[32,8,128]{2,1,0:T(8,128)} %metric.1), calls=%async_computation.1 | async-start | bytes 262144 | tf_op jit(solution)/shard_map/all_to_all | solution.py:323
  59.6 3.1 %relay.1 = (bf16[8,100,128]{2,1,0:T(8,128)(2,1)}, bf16[8,100,128]{2,1,0:T(8,128)(2,1)}, bf16[8,100,128]{2,1,0:T(8,128)(2,1)}, bf16[8,100,128]{2,1,0:T(8,128)(2,1)}, s32[64]{0:T(128)}) custom-call(bf16[32,104,128]{2,1,0:T(8,128)(2,1)} %copy-done), custom_call_target="tpu_custom_call" | custom-call | bytes 1638400 | tf_op jit(solution)/shard_map/relay/pallas_call | solution.py:219
  62.8 0.1 collective-permute-start
  62.9 1.5 %collective-permute-start.1 = (bf16[8,100,128]{2,1,0:T(8,128)(2,1)}, bf16[8,100,128]{2,1,0:T(8,128)(2,1)S(1)}, u32[]{:S(2)}, u32[]{:S(2)}) collective-permute-start(bf16[8,100,128]{2,1,0:T(8,128)(2,1)} %get-tuple-element.23), channel_id=1, source_target_pairs={{0,2},{1,3},{2,0},{3,1},{4,6},{5,7},{6,4},{7,5},{8,10},{9,11},{10,... | collective-permute-start | bytes 614408 | tf_op jit(solution)/shard_map/ppermute | solution.py:26
  64.4 0.3 collective-permute-start.2
  64.7 2.3 %all-to-all-done.1.refs_0_ = f32[32,8,128]{2,1,0:T(8,128)S(1)} async-done(((f32[32,8,128]{2,1,0:T(8,128)}), f32[32,8,128]{2,1,0:T(8,128)S(1)}, u32[]{:S(2)}, u32[]{:S(2)}) %all-to-all-start.1) | async-done | bytes 131104 | tf_op jit(solution)/shard_map/all_to_all | solution.py:323
  67.0 0.7 copy-done.1
  67.6 1.6 %relay_stats.1 = (f32[8,8,128]{2,1,0:T(8,128)}, f32[8,8,128]{2,1,0:T(8,128)}, f32[8,8,128]{2,1,0:T(8,128)}, f32[8,8,128]{2,1,0:T(8,128)}) custom-call(f32[32,8,128]{2,1,0:T(8,128)} %copy-done.1, s32[64]{0:T(128)} %get-tuple-element.30.refs_1_), custom_call_target="tpu_custom_call" | custom-call | bytes 262144 | tf_op jit(solution)/shard_map/relay_stats/pallas_call | solution.py:249
  69.2 1.5 %collective-permute-start.8 = (f32[8,8,128]{2,1,0:T(8,128)}, f32[8,8,128]{2,1,0:T(8,128)S(1)}, u32[]{:S(2)}, u32[]{:S(2)}) collective-permute-start(f32[8,8,128]{2,1,0:T(8,128)} %get-tuple-element.33), channel_id=1, source_target_pairs={{0,2},{1,3},{2,0},{3,1},{4,6},{5,7},{6,4},{7,5},{8,10},{9,11},{10,... | collective-permute-start | bytes 98312 | tf_op jit(solution)/shard_map/ppermute | solution.py:26
  70.7 1.2 %collective-permute-start.9 = (f32[8,8,128]{2,1,0:T(8,128)}, f32[8,8,128]{2,1,0:T(8,128)S(1)}, u32[]{:S(2)}, u32[]{:S(2)}) collective-permute-start(f32[8,8,128]{2,1,0:T(8,128)} %get-tuple-element.34), channel_id=1, source_target_pairs={{0,3},{1,2},{2,1},{3,0},{4,7},{5,6},{6,5},{7,4},{8,11},{9,10},{10,... | collective-permute-start | bytes 98312 | tf_op jit(solution)/shard_map/ppermute | solution.py:26
  71.9 4.4 %collective-permute-done.8.refs_2_ = f32[8,8,128]{2,1,0:T(8,128)S(1)} collective-permute-done((f32[8,8,128]{2,1,0:T(8,128)}, f32[8,8,128]{2,1,0:T(8,128)S(1)}, u32[]{:S(2)}, u32[]{:S(2)}) %collective-permute-start.8) | collective-permute-done | bytes 32800 | tf_op jit(solution)/shard_map/ppermute | solution.py:26
  76.4 0.6 copy-done.6
  76.9 0.0 copy-done.7
  77.0 1.5 %place_stats.1 = (f32[6,4096]{1,0:T(8,128)}, f32[32,128]{1,0:T(8,128)}) custom-call(f32[8,8,128]{2,1,0:T(8,128)} %get-tuple-element.31.refs_0_, f32[8,8,128]{2,1,0:T(8,128)} %copy-done.5, f32[8,8,128]{2,1,0:T(8,128)} %copy-done.6, f32[8,8,128]{2,1,0:T(8,128)} %copy-done.7), custom_call_target="tpu_custom_call" | custom-call | tf_op jit(solution)/shard_map/place_stats/pallas_call | solution.py:295
  78.5 0.6 copy-done.2
  79.1 0.1 copy-done.3
  79.2 0.1 copy-done.4
  79.3 2.4 %place.1 = bf16[100,4096]{1,0:T(8,128)(2,1)} custom-call(bf16[8,100,128]{2,1,0:T(8,128)(2,1)} %get-tuple-element.21.refs_0_, bf16[8,100,128]{2,1,0:T(8,128)(2,1)} %copy-done.2, bf16[8,100,128]{2,1,0:T(8,128)(2,1)} %copy-done.3, bf16[8,100,128]{2,1,0:T(8,128)(2,1)} %copy-done.4), custom_call_target="tpu_custom_call" | custom-call | tf_op jit(solution)/shard_map/place/pallas_call | solution.py:271
  (31 shorter events, 0.1 us)
Async XLA Ops:
  4.5 7.5 %copy-start.12 = (bf16[2,100,128]{2,1,0:T(8,128)(2,1)S(1)}, bf16[2,100,128]{2,1,0:T(8,128)(2,1)}, u32[]{:S(2)}) copy-start(bf16[2,100,128]{2,1,0:T(8,128)(2,1)} %get-tuple-element.26) | copy-start | bytes 153604
  4.5 9.5 %copy-start.10 = (bf16[2,100,128]{2,1,0:T(8,128)(2,1)S(1)}, bf16[2,100,128]{2,1,0:T(8,128)(2,1)}, u32[]{:S(2)}) copy-start(bf16[2,100,128]{2,1,0:T(8,128)(2,1)} %get-tuple-element.27) | copy-start | bytes 153604
  4.6 12.3 %copy-start.9 = (bf16[2,100,128]{2,1,0:T(8,128)(2,1)S(1)}, bf16[2,100,128]{2,1,0:T(8,128)(2,1)}, u32[]{:S(2)}) copy-start(bf16[2,100,128]{2,1,0:T(8,128)(2,1)} %get-tuple-element.28) | copy-start | bytes 153604
  4.6 12.3 %copy-start.8 = (bf16[2,100,128]{2,1,0:T(8,128)(2,1)S(1)}, bf16[2,100,128]{2,1,0:T(8,128)(2,1)}, u32[]{:S(2)}) copy-start(bf16[2,100,128]{2,1,0:T(8,128)(2,1)} %get-tuple-element.29) | copy-start | bytes 153604
  4.6 49.5 %all-to-all-start = ((bf16[32,104,128]{2,1,0:T(8,128)(2,1)}), bf16[32,104,128]{2,1,0:T(8,128)(2,1)S(1)}, u32[]{:S(2)}, u32[]{:S(2)}) async-start(bf16[32,104,128]{2,1,0:T(8,128)(2,1)} %get-tuple-element.20), calls=%async_computation | async-start | bytes 1703936 | tf_op jit(solution)/shard_map/all_to_all | solution.py:319
  12.0 19.9 %collective-permute-start.3 = (bf16[2,100,128]{2,1,0:T(8,128)(2,1)S(1)}, bf16[2,100,128]{2,1,0:T(8,128)(2,1)S(1)}, u32[]{:S(2)}, u32[]{:S(2)}) collective-permute-start(bf16[2,100,128]{2,1,0:T(8,128)(2,1)S(1)} %copy-done.12), channel_id=1, source_target_pairs={{0,4},{4,8},{8,12},{12,16},{16,20},{20,24},{24,28},{28,0},{1,5},{5... | collective-permute-start | bytes 153608 | tf_op jit(solution)/shard_map/ppermute | solution.py:21
  14.1 17.9 %collective-permute-start.4 = (bf16[2,100,128]{2,1,0:T(8,128)(2,1)S(1)}, bf16[2,100,128]{2,1,0:T(8,128)(2,1)S(1)}, u32[]{:S(2)}, u32[]{:S(2)}) collective-permute-start(bf16[2,100,128]{2,1,0:T(8,128)(2,1)S(1)} %copy-done.10), channel_id=1, source_target_pairs={{0,28},{4,0},{8,4},{12,8},{16,12},{20,16},{24,20},{28,24},{1,29},{... | collective-permute-start | bytes 153608 | tf_op jit(solution)/shard_map/ppermute | solution.py:21
  16.8 15.1 %collective-permute-start.5 = (bf16[2,100,128]{2,1,0:T(8,128)(2,1)S(1)}, bf16[2,100,128]{2,1,0:T(8,128)(2,1)S(1)}, u32[]{:S(2)}, u32[]{:S(2)}) collective-permute-start(bf16[2,100,128]{2,1,0:T(8,128)(2,1)S(1)} %copy-done.9), channel_id=1, source_target_pairs={{0,1},{1,2},{2,3},{3,0},{4,5},{5,6},{6,7},{7,4},{8,9},{9,10},{10,1... | collective-permute-start | bytes 153608 | tf_op jit(solution)/shard_map/ppermute | solution.py:21
  16.8 15.2 %collective-permute-start.6 = (bf16[2,100,128]{2,1,0:T(8,128)(2,1)S(1)}, bf16[2,100,128]{2,1,0:T(8,128)(2,1)S(1)}, u32[]{:S(2)}, u32[]{:S(2)}) collective-permute-start(bf16[2,100,128]{2,1,0:T(8,128)(2,1)S(1)} %copy-done.8), channel_id=1, source_target_pairs={{0,3},{1,0},{2,1},{3,2},{4,7},{5,4},{6,5},{7,6},{8,11},{9,8},{10,9... | collective-permute-start | bytes 153608 | tf_op jit(solution)/shard_map/ppermute | solution.py:21
  32.0 0.6 copy-start.11
  32.0 0.6 copy-start.13
  32.0 0.6 copy-start.14
  32.0 0.7 copy-start.15
  54.0 5.6 %copy-start = (bf16[32,104,128]{2,1,0:T(8,128)(2,1)}, bf16[32,104,128]{2,1,0:T(8,128)(2,1)S(1)}, u32[]{:S(2)}) copy-start(bf16[32,104,128]{2,1,0:T(8,128)(2,1)S(1)} %all-to-all-done.refs_0_) | copy-start | bytes 2555908
  54.1 12.9 %all-to-all-start.1 = ((f32[32,8,128]{2,1,0:T(8,128)}), f32[32,8,128]{2,1,0:T(8,128)S(1)}, u32[]{:S(2)}, u32[]{:S(2)}) async-start(f32[32,8,128]{2,1,0:T(8,128)} %metric.1), calls=%async_computation.1 | async-start | bytes 262144 | tf_op jit(solution)/shard_map/all_to_all | solution.py:323
  62.8 15.7 %collective-permute-start = (bf16[8,100,128]{2,1,0:T(8,128)(2,1)}, bf16[8,100,128]{2,1,0:T(8,128)(2,1)S(1)}, u32[]{:S(2)}, u32[]{:S(2)}) collective-permute-start(bf16[8,100,128]{2,1,0:T(8,128)(2,1)} %get-tuple-element.22), channel_id=1, source_target_pairs={{0,1},{1,0},{2,3},{3,2},{4,5},{5,4},{6,7},{7,6},{8,9},{9,8},{10,11... | collective-permute-start | bytes 614408 | tf_op jit(solution)/shard_map/ppermute | solution.py:26
  62.9 15.6 %collective-permute-start.1 = (bf16[8,100,128]{2,1,0:T(8,128)(2,1)}, bf16[8,100,128]{2,1,0:T(8,128)(2,1)S(1)}, u32[]{:S(2)}, u32[]{:S(2)}) collective-permute-start(bf16[8,100,128]{2,1,0:T(8,128)(2,1)} %get-tuple-element.23), channel_id=1, source_target_pairs={{0,2},{1,3},{2,0},{3,1},{4,6},{5,7},{6,4},{7,5},{8,10},{9,11},{10,... | collective-permute-start | bytes 614408 | tf_op jit(solution)/shard_map/ppermute | solution.py:26
  64.4 14.1 %collective-permute-start.2 = (bf16[8,100,128]{2,1,0:T(8,128)(2,1)}, bf16[8,100,128]{2,1,0:T(8,128)(2,1)S(1)}, u32[]{:S(2)}, u32[]{:S(2)}) collective-permute-start(bf16[8,100,128]{2,1,0:T(8,128)(2,1)} %get-tuple-element.24), channel_id=1, source_target_pairs={{0,3},{1,2},{2,1},{3,0},{4,7},{5,6},{6,5},{7,4},{8,11},{9,10},{10,... | collective-permute-start | bytes 614408 | tf_op jit(solution)/shard_map/ppermute | solution.py:26
  67.0 0.7 copy-start.1
  69.2 1.5 %collective-permute-start.7 = (f32[8,8,128]{2,1,0:T(8,128)}, f32[8,8,128]{2,1,0:T(8,128)S(1)}, u32[]{:S(2)}, u32[]{:S(2)}) collective-permute-start(f32[8,8,128]{2,1,0:T(8,128)} %get-tuple-element.32), channel_id=1, source_target_pairs={{0,1},{1,0},{2,3},{3,2},{4,5},{5,4},{6,7},{7,6},{8,9},{9,8},{10,11... | collective-permute-start | bytes 98312 | tf_op jit(solution)/shard_map/ppermute | solution.py:26
  69.2 7.1 %collective-permute-start.8 = (f32[8,8,128]{2,1,0:T(8,128)}, f32[8,8,128]{2,1,0:T(8,128)S(1)}, u32[]{:S(2)}, u32[]{:S(2)}) collective-permute-start(f32[8,8,128]{2,1,0:T(8,128)} %get-tuple-element.33), channel_id=1, source_target_pairs={{0,2},{1,3},{2,0},{3,1},{4,6},{5,7},{6,4},{7,5},{8,10},{9,11},{10,... | collective-permute-start | bytes 98312 | tf_op jit(solution)/shard_map/ppermute | solution.py:26
  70.7 5.6 %copy-start.5 = (f32[8,8,128]{2,1,0:T(8,128)}, f32[8,8,128]{2,1,0:T(8,128)S(1)}, u32[]{:S(2)}) copy-start(f32[8,8,128]{2,1,0:T(8,128)S(1)} %collective-permute-done.7.refs_1_) | copy-start | bytes 98308
  70.7 5.6 %collective-permute-start.9 = (f32[8,8,128]{2,1,0:T(8,128)}, f32[8,8,128]{2,1,0:T(8,128)S(1)}, u32[]{:S(2)}, u32[]{:S(2)}) collective-permute-start(f32[8,8,128]{2,1,0:T(8,128)} %get-tuple-element.34), channel_id=1, source_target_pairs={{0,3},{1,2},{2,1},{3,0},{4,7},{5,6},{6,5},{7,4},{8,11},{9,10},{10,... | collective-permute-start | bytes 98312 | tf_op jit(solution)/shard_map/ppermute | solution.py:26
  76.3 0.6 copy-start.6
  76.3 0.6 copy-start.7
  78.5 0.7 copy-start.2
  78.5 0.7 copy-start.3
  78.5 0.8 copy-start.4

commit v2 on v1

--- a/solution.py
+++ b/solution.py
@@ -9,10 +9,15 @@
 bf16 = jnp.bfloat16
 LANES = 128
 FACES = 4
+AHEAD = 4
 
 SMEM = pl.BlockSpec(memory_space=pltpu.SMEM)
 VMEM = pl.BlockSpec(memory_space=pltpu.VMEM)
 HBM = pl.BlockSpec(memory_space=pl.ANY)
+
+
+def grant(*shapes):
+    return pltpu.CompilerParams(vmem_limit_bytes=sum(shapes) + (1 << 20))
 
 
 def passed_along(value, axis, steps):
@@ -37,8 +42,8 @@
     blocks = owner.shape[0]
     per_wide = slots // wide
     for k in range(4):
-        for h in range(halo_blocks.shape[2]):
-            at = pl.multiple_of(halo_blocks[0, k, h] * LANES, LANES)
+        for h in range(halo_blocks.shape[0]):
+            at = pl.multiple_of(halo_blocks[h, k] * LANES, LANES)
             halos[k][h] = coef[:, pl.ds(at, LANES)]
 
     def clear(w, _):
@@ -65,7 +70,7 @@
     rows, count = coef.shape
     blocks = owner.shape[0]
     slots = wide * max(1, blocks // wide)
-    halo = jax.ShapeDtypeStruct((halo_blocks.shape[2], rows, LANES), bf16)
+    halo = jax.ShapeDtypeStruct((halo_blocks.shape[0], rows, LANES), bf16)
     return pl.pallas_call(
         lambda *refs: pack_kernel(wide, narrow, *refs),
         out_shape=[halo] * 4
@@ -77,6 +82,7 @@
         out_specs=[VMEM] * 5 + [SMEM],
         scratch_shapes=[pltpu.SMEM((wide,), jnp.int32)],
         cost_estimate=pl.CostEstimate(flops=0, bytes_accessed=4 * rows * count, transcendentals=0),
+        compiler_params=grant(2 * rows * count, 3 * (slots + 16) * padded_rows(rows) * LANES),
         name="pack",
     )(coef, halo_blocks, owner)
 
@@ -94,8 +100,8 @@
         at = pl.multiple_of(b * LANES, LANES)
         return pltpu.make_async_copy(nb.at[:, pl.ds(at, LANES)], idx.at[place], sem.at[place])
 
-    fetch(0, 0).start()
-    fetch(1, 1).start()
+    for p in range(AHEAD):
+        fetch(p, p).start()
     lane = lax.broadcasted_iota(jnp.int32, (LANES, rows), 0)
     row = lax.broadcasted_iota(jnp.int32, (LANES, rows), 1)
     place = ((row == 3 * (lane % 32) + lane // 32) & (lane % 32 < third)).astype(bf16)
@@ -122,14 +128,14 @@
                     cols, wp[f + 1], contract, preferred_element_type=f32
                 )
 
-    def gather(place):
+    def gather(p):
         for e in range(LANES):
-            part = [tables[f][pl.ds(idx[place, f, e], 1), :] for f in range(FACES)]
-            accs[place][pl.ds(e, 1), :] = (part[0] + part[1]) + (part[2] + part[3])
-
-    def metric(b, place):
+            part = [tables[f][pl.ds(idx[p, f, e], 1), :] for f in range(FACES)]
+            accs[p % 2][pl.ds(e, 1), :] = (part[0] + part[1]) + (part[2] + part[3])
+
+    def metric(b, p):
         at = pl.multiple_of(b * LANES, LANES)
-        d = accs[place][...].T + jnp.dot(
+        d = accs[p % 2][...].T + jnp.dot(
             wp[0], coef[:, pl.ds(at, LANES)], preferred_element_type=f32
         )
         x, y, z = d[0:32], d[32:64], d[64:96]
@@ -144,27 +150,20 @@
         work = count[b].astype(f32) * jnp.sqrt(det)
         out[slot[b]] = jnp.concatenate([xx, yy, zz, xy, xz, yz, work, work], axis=0)
 
-    def pair(i, _):
-        b = 2 * i
-        fetch(b, 0).wait()
-        gather(0)
-
-        @pl.when(i + 1 < blocks // 2)
-        def _():
-            fetch(b + 2, 0).start()
-
-        fetch(b + 1, 1).wait()
-        metric(b, 0)
-        gather(1)
-
-        @pl.when(i + 1 < blocks // 2)
-        def _():
-            fetch(b + 3, 1).start()
-
-        metric(b + 1, 1)
+    def group(i, _):
+        for p in range(AHEAD):
+            b = AHEAD * i + p
+            fetch(b, p).wait()
+            gather(p)
+
+            @pl.when(b + AHEAD < blocks)
+            def _():
+                fetch(b + AHEAD, p).start()
+
+            metric(b, p)
         return 0
 
-    lax.fori_loop(0, blocks // 2, pair, 0)
+    lax.fori_loop(0, blocks // AHEAD, group, 0)
 
 
 def metrics(nb, slot, count, coef, halos, w, slots):
@@ -180,12 +179,13 @@
             pltpu.VMEM((LANES, LANES), f32),
             pltpu.VMEM((LANES, LANES), f32),
             pltpu.VMEM((FACES + 1, LANES, w.shape[2]), bf16),
-            pltpu.SMEM((2, FACES, LANES), jnp.int32),
-            pltpu.SemaphoreType.DMA((2,)),
+            pltpu.SMEM((AHEAD, FACES, LANES), jnp.int32),
+            pltpu.SemaphoreType.DMA((AHEAD,)),
         ],
         cost_estimate=pl.CostEstimate(
             flops=2 * table * 5 * LANES * LANES, bytes_accessed=30 * elems * LANES, transcendentals=elems
         ),
+        compiler_params=grant(6 * FACES * table * LANES, 2 * 104 * elems),
         name="metric",
     )(nb, slot, count, coef, *halos, w)
 
@@ -231,6 +231,7 @@
         cost_estimate=pl.CostEstimate(
             flops=0, bytes_accessed=4 * blocks * rows * LANES, transcendentals=0
         ),
+        compiler_params=grant(3 * (slots + blocks) * padded_rows(rows) * LANES),
         name="relay",
     )(arrived)
     return sends, order
@@ -252,6 +253,7 @@
         in_specs=[VMEM, SMEM],
         out_specs=[VMEM] * narrow,
         cost_estimate=pl.CostEstimate(flops=0, bytes_accessed=64 * blocks * LANES, transcendentals=0),
+        compiler_params=grant(2 * 32 * blocks * LANES),
         name="relay_stats",
     )(arrived, order)
 
@@ -273,6 +275,7 @@
         out_shape=jax.ShapeDtypeStruct((rows, len(parts) * per * LANES), bf16),
         in_specs=[VMEM] * len(parts),
         out_specs=VMEM,
+        compiler_params=grant(6 * len(parts) * per * padded_rows(rows) * LANES),
         name="place",
     )(*parts)
 
@@ -300,6 +303,7 @@
         ],
         in_specs=[VMEM] * len(parts),
         out_specs=[VMEM] * 2,
+        compiler_params=grant(3 * 32 * blocks * LANES),
         name="place_stats",
     )(*parts)
 
@@ -307,9 +311,11 @@
 def per_device(coefficients, neighbours, halo_blocks, recon_weight, owner_device, work_count):
     wide = lax.axis_size("wide")
     narrow = lax.axis_size("narrow")
-    rows, elems = coefficients.shape
+    rows, _ = coefficients.shape
     blocks = owner_device.shape[0]
-    to0, to1, to2, to3, packed, slot = pack(coefficients, halo_blocks, owner_device, wide, narrow)
+    to0, to1, to2, to3, packed, slot = pack(
+        coefficients, halo_blocks[0].T, owner_device, wide, narrow
+    )
     halos = [
         passed_along(to1, "wide", 1),
         passed_along(to0, "wide", -1),

time: 82.7 us -> 72.7 us (0.88)
  Pallas kernels: 32.5 us -> 24 us
  local copies, waits for them, and re-layouts: 4.06 us -> 1.84 us
  waiting for transfers between devices: 20.1 us -> 21.8 us
    pallas_call x1, Pallas kernels: 21.4 us -> 18.1 us  [metrics(): pl.pallas_call(metric_kernel, out_shape=jax.ShapeDtypeStruct((slots, 8, L...]
    unnamed x33 -> x14, local copies, waits for them, and re-layouts: 4.06 us -> 1.84 us
    all_to_all x1, waiting for transfers between devices: 2.28 us -> 3.81 us  [per_device(): stats_arrived = lax.all_to_all(stats, 'wide', 0, 0, tiled=True)]
    pallas_call x1, Pallas kernels: 3.13 us -> 1.6 us  [relay(): pl.pallas_call(lambda *refs: relay_kernel(narrow, *refs), out_shape=[jax....]
    pallas_call x1, Pallas kernels: 2.36 us -> 1.12 us  [place(): pl.pallas_call(place_kernel, out_shape=jax.ShapeDtypeStruct((rows, len(pa...]
    pallas_call x1, Pallas kernels: 1.59 us -> 0.58 us  [relay_stats(): pl.pallas_call(lambda *refs: relay_stats_kernel(narrow, *refs), out_shape...]
  transfers between devices with their start and end apart: 12 -> 12, of which waited for: 3 -> 3; matrix products, arithmetic and copies ran while one was open for 0% -> 0% of each run, Pallas kernels for 34% -> 29%
where the time goes in v2:
time: 72.7 us; the launch traced here: 72.4 us
  Pallas kernels  24 us (33%)
  starting transfers between devices  23.9 us (33%)
  waiting for transfers between devices  21.8 us (30%)
  local copies, waits for them, and re-layouts  1.84 us (3%)
  between operations  0.78 us (1%)
    pallas_call x1, Pallas kernels, metrics(): pl.pallas_call(metric_kernel, out_shape=jax.ShapeDtypeStruct((slots, 8, L...  18.1 us
    ppermute x4, waiting for transfers between devices, passed_along(): return lax.ppermute(value, axis, pairs)  13.4 us
    all_to_all x1, starting transfers between devices, per_device(): arrived = lax.all_to_all(packed, 'wide', 0, 0, tiled=True)  7.45 us
    ppermute x4, starting transfers between devices, passed_along(): return lax.ppermute(value, axis, pairs)  6.49 us
    all_to_all x1, starting transfers between devices, per_device(): stats_arrived = lax.all_to_all(stats, 'wide', 0, 0, tiled=True)  5.58 us
    ppermute x6, waiting for transfers between devices, swapped(): lax.ppermute(value, axis, [(source, source ^ flip) for source in range(co...  4.54 us
    ppermute x6, starting transfers between devices, swapped(): lax.ppermute(value, axis, [(source, source ^ flip) for source in range(co...  4.41 us
    all_to_all x1, waiting for transfers between devices, per_device(): stats_arrived = lax.all_to_all(stats, 'wide', 0, 0, tiled=True)  3.81 us
  transfers between devices with their start and end apart: 12, of which 3 were waited for; matrix products, arithmetic and copies ran while one was open for 0% of the time, Pallas kernels for 29%

profile of v2, /device:TPU:0, one launch (start us, length us, event | category | flops | bytes accessed | tf_op | source)
XLA Modules:
  0.0 72.4 jit_solution(627414112241799056)
XLA Ops:
  0.7 0.7 copy-done.2
  1.3 1.2 %copy-done = bf16[100,4096]{1,0:T(8,128)(2,1)S(1)} copy-done((bf16[100,4096]{1,0:T(8,128)(2,1)S(1)}, bf16[100,4096]{1,0:T(8,128)(2,1)}, u32[]{:S(2)}) %copy-start) | copy-done | bytes 819224
  2.5 1.9 %pack.1 = (bf16[2,100,128]{2,1,0:T(8,128)(2,1)S(1)}, bf16[2,100,128]{2,1,0:T(8,128)(2,1)S(1)}, bf16[2,100,128]{2,1,0:T(8,128)(2,1)S(1)}, bf16[2,100,128]{2,1,0:T...) custom-call(bf16[100,4096]{1,0:T(8,128)(2,1)S(1)} %copy-done, s32[2,4]{1,0:T(2,128)S(1)} %bitcast.4, ...), custom_call_target="tpu_custom_call" | custom-call | bytes 1638400 | tf_op jit(solution)/shard_map/pack/pallas_call | solution.py:74
  4.4 0.0 copy-start.1
  4.4 0.0 copy-start.4
  4.4 0.0 copy-start.5
  4.5 7.5 %all-to-all-start = ((bf16[32,104,128]{2,1,0:T(8,128)(2,1)}), bf16[32,104,128]{2,1,0:T(8,128)(2,1)S(1)}, u32[]{:S(2)}, u32[]{:S(2)}) async-start(bf16[32,104,128]{2,1,0:T(8,128)(2,1)} %get-tuple-element.20), calls=%async_computation | async-start | bytes 1703936 | tf_op jit(solution)/shard_map/all_to_all | solution.py:325
  11.9 2.0 %collective-permute-start.3 = (bf16[2,100,128]{2,1,0:T(8,128)(2,1)S(1)}, bf16[2,100,128]{2,1,0:T(8,128)(2,1)S(1)}, u32[]{:S(2)}, u32[]{:S(2)}) collective-permute-start(bf16[2,100,128]{2,1,0:T(8,128)(2,1)S(1)} %get-tuple-element.26), channel_id=1, source_target_pairs={{0,4},{4,8},{8,12},{12,16},{16,20},{20,24},{24,28},{28,0},{1,5},{5... | collective-permute-start | bytes 153608 | tf_op jit(solution)/shard_map/ppermute | solution.py:26
  13.9 2.7 %collective-permute-start.4 = (bf16[2,100,128]{2,1,0:T(8,128)(2,1)S(1)}, bf16[2,100,128]{2,1,0:T(8,128)(2,1)S(1)}, u32[]{:S(2)}, u32[]{:S(2)}) collective-permute-start(bf16[2,100,128]{2,1,0:T(8,128)(2,1)S(1)} %get-tuple-element.27), channel_id=1, source_target_pairs={{0,28},{4,0},{8,4},{12,8},{16,12},{20,16},{24,20},{28,24},{1,29},{... | collective-permute-start | bytes 153608 | tf_op jit(solution)/shard_map/ppermute | solution.py:26
  16.7 0.0 collective-permute-start.5
  16.7 1.7 %collective-permute-start.6 = (bf16[2,100,128]{2,1,0:T(8,128)(2,1)S(1)}, bf16[2,100,128]{2,1,0:T(8,128)(2,1)S(1)}, u32[]{:S(2)}, u32[]{:S(2)}) collective-permute-start(bf16[2,100,128]{2,1,0:T(8,128)(2,1)S(1)} %get-tuple-element.29), channel_id=1, source_target_pairs={{0,3},{1,0},{2,1},{3,2},{4,7},{5,4},{6,5},{7,6},{8,11},{9,8},{10,9... | collective-permute-start | bytes 153608 | tf_op jit(solution)/shard_map/ppermute | solution.py:26
  18.4 13.4 %collective-permute-done.3.h0 = bf16[2,100,128]{2,1,0:T(8,128)(2,1)S(1)} collective-permute-done((bf16[2,100,128]{2,1,0:T(8,128)(2,1)S(1)}, bf16[2,100,128]{2,1,0:T(8,128)(2,1)S(1)}, u32[]{:S(2)}, u32[]{:S(2)}) %collective-permute-start.3) | collective-permute-done | bytes 51232 | tf_op jit(solution)/shard_map/ppermute | solution.py:26
  31.8 0.0 collective-permute-done.4.h1
  31.9 0.0 collective-permute-done.5.h2
  31.9 0.0 collective-permute-done.6.h3
  31.9 18.1 %metric.1 = f32[32,8,128]{2,1,0:T(8,128)} custom-call(s32[4,4096]{1,0:T(4,128)S(1)} %copy-done.5, s32[32]{0:T(128)S(1)} %get-tuple-element.25.slot, s32[32]{0:T(128)S(1)} %copy-done.6, bf16[100,4096]{1,0:T(8,128)(2,1)S(1)} %copy-done.1, bf16[2,100,128]{2,1,0:T(8,128)(2,1)S(1)} %collective-permute-done.3.h0, ...), custom_call_target="tpu_custom_call" | custom-call | flops 838860800 | bytes 15728640 | tf_op jit(solution)/shard_map/metric/pallas_call | solution.py:172
  50.0 0.0 all-to-all-done.refs_0_
  50.0 5.6 %all-to-all-start.1 = ((f32[32,8,128]{2,1,0:T(8,128)}), f32[32,8,128]{2,1,0:T(8,128)S(1)}, u32[]{:S(2)}, u32[]{:S(2)}) async-start(f32[32,8,128]{2,1,0:T(8,128)} %metric.1), calls=%async_computation.1 | async-start | bytes 262144 | tf_op jit(solution)/shard_map/all_to_all | solution.py:329
  55.6 1.6 %relay.1 = (bf16[8,100,128]{2,1,0:T(8,128)(2,1)S(1)}, bf16[8,100,128]{2,1,0:T(8,128)(2,1)S(1)}, bf16[8,100,128]{2,1,0:T(8,128)(2,1)S(1)}, bf16[8,100,128]{2,1,0:T(8,128)(2,1)S(1)}, s32[64]{0:T(128)S(1)}) custom-call(bf16[32,104,128]{2,1,0:T(8,128)(2,1)S(1)} %all-to-all-done.refs_0_), custom_call_target="tpu_custom_call" | custom-call | bytes 1638400 | tf_op jit(solution)/shard_map/relay/pallas_call | solution.py:219
  57.2 0.1 collective-permute-start
  57.3 1.5 %collective-permute-start.1 = (bf16[8,100,128]{2,1,0:T(8,128)(2,1)S(1)}, bf16[8,100,128]{2,1,0:T(8,128)(2,1)S(1)}, u32[]{:S(2)}, u32[]{:S(2)}) collective-permute-start(bf16[8,100,128]{2,1,0:T(8,128)(2,1)S(1)} %get-tuple-element.23), channel_id=1, source_target_pairs={{0,2},{1,3},{2,0},{3,1},{4,6},{5,7},{6,4},{7,5},{8,10},{9,11},{10,... | collective-permute-start | bytes 614408 | tf_op jit(solution)/shard_map/ppermute | solution.py:31
  58.8 0.3 collective-permute-start.2
  59.1 3.8 %all-to-all-done.1.refs_0_ = f32[32,8,128]{2,1,0:T(8,128)S(1)} async-done(((f32[32,8,128]{2,1,0:T(8,128)}), f32[32,8,128]{2,1,0:T(8,128)S(1)}, u32[]{:S(2)}, u32[]{:S(2)}) %all-to-all-start.1) | async-done | bytes 131104 | tf_op jit(solution)/shard_map/all_to_all | solution.py:329
  62.9 0.6 relay_stats.1
  63.5 0.1 collective-permute-start.7
  63.6 1.5 %collective-permute-start.8 = (f32[8,8,128]{2,1,0:T(8,128)S(1)}, f32[8,8,128]{2,1,0:T(8,128)S(1)}, u32[]{:S(2)}, u32[]{:S(2)}) collective-permute-start(f32[8,8,128]{2,1,0:T(8,128)S(1)} %get-tuple-element.33), channel_id=1, source_target_pairs={{0,2},{1,3},{2,0},{3,1},{4,6},{5,7},{6,4},{7,5},{8,10},{9,11},{10,... | collective-permute-start | bytes 98312 | tf_op jit(solution)/shard_map/ppermute | solution.py:31
  65.1 0.0 collective-permute-done.7.refs_1_
  65.1 0.9 %collective-permute-start.9 = (f32[8,8,128]{2,1,0:T(8,128)S(1)}, f32[8,8,128]{2,1,0:T(8,128)S(1)}, u32[]{:S(2)}, u32[]{:S(2)}) collective-permute-start(f32[8,8,128]{2,1,0:T(8,128)S(1)} %get-tuple-element.34), channel_id=1, source_target_pairs={{0,3},{1,2},{2,1},{3,0},{4,7},{5,6},{6,5},{7,4},{8,11},{9,10},{10,... | collective-permute-start | bytes 98312 | tf_op jit(solution)/shard_map/ppermute | solution.py:31
  66.0 4.5 %collective-permute-done.8.refs_2_ = f32[8,8,128]{2,1,0:T(8,128)S(1)} collective-permute-done((f32[8,8,128]{2,1,0:T(8,128)S(1)}, f32[8,8,128]{2,1,0:T(8,128)S(1)}, u32[]{:S(2)}, u32[]{:S(2)}) %collective-permute-start.8) | collective-permute-done | bytes 32800 | tf_op jit(solution)/shard_map/ppermute | solution.py:31
  70.5 0.7 place_stats.1
  71.2 0.0 collective-permute-done.2.refs_3_
  71.2 1.1 %place.1 = bf16[100,4096]{1,0:T(8,128)(2,1)} custom-call(bf16[8,100,128]{2,1,0:T(8,128)(2,1)S(1)} %get-tuple-element.21.refs_0_, bf16[8,100,128]{2,1,0:T(8,128)(2,1)S(1)} %collective-permute-done.refs_1_, bf16[8,100,128]{2,1,0:T(8,128)(2,1)S(1)} %collective-permute-done.1.refs_2_, bf16[8,100,128]{2,1,0:T(8,128)(2,1)S(1)} %collective-permute-done.2.refs_3_), custom_call_target="tpu_custom_call" | custom-call | tf_op jit(solution)/shard_map/place/pallas_call | solution.py:273
  (12 shorter events, 0.0 us)
Async XLA Ops:
  0.6 0.7 copy-start.2
  0.6 0.7 copy-start.3
  1.3 1.2 %copy-start = (bf16[100,4096]{1,0:T(8,128)(2,1)S(1)}, bf16[100,4096]{1,0:T(8,128)(2,1)}, u32[]{:S(2)}) copy-start(bf16[100,4096]{1,0:T(8,128)(2,1)} %coef.1) | copy-start | bytes 2457604
  4.4 27.4 %copy-start.1 = (bf16[100,4096]{1,0:T(8,128)(2,1)S(1)}, bf16[100,4096]{1,0:T(8,128)(2,1)}, u32[]{:S(2)}) copy-start(bf16[100,4096]{1,0:T(8,128)(2,1)} %coef.1) | copy-start | bytes 2457604
  4.4 27.4 %copy-start.4 = (bf16[5,75,100]{2,1,0:T(8,128)(2,1)S(1)}, bf16[5,75,100]{2,1,0:T(8,128)(2,1)}, u32[]{:S(2)}) copy-start(bf16[5,75,100]{2,1,0:T(8,128)(2,1)} %w.1) | copy-start | bytes 225004
  4.4 27.4 %copy-start.5 = (s32[4,4096]{1,0:T(4,128)S(1)}, s32[4,4096]{1,0:T(4,128)}, u32[]{:S(2)}) copy-start(s32[4,4096]{1,0:T(4,128)} %nb.1) | copy-start | bytes 196612
  4.5 45.5 %all-to-all-start = ((bf16[32,104,128]{2,1,0:T(8,128)(2,1)}), bf16[32,104,128]{2,1,0:T(8,128)(2,1)S(1)}, u32[]{:S(2)}, u32[]{:S(2)}) async-start(bf16[32,104,128]{2,1,0:T(8,128)(2,1)} %get-tuple-element.20), calls=%async_computation | async-start | bytes 1703936 | tf_op jit(solution)/shard_map/all_to_all | solution.py:325
  11.9 19.9 %collective-permute-start.3 = (bf16[2,100,128]{2,1,0:T(8,128)(2,1)S(1)}, bf16[2,100,128]{2,1,0:T(8,128)(2,1)S(1)}, u32[]{:S(2)}, u32[]{:S(2)}) collective-permute-start(bf16[2,100,128]{2,1,0:T(8,128)(2,1)S(1)} %get-tuple-element.26), channel_id=1, source_target_pairs={{0,4},{4,8},{8,12},{12,16},{16,20},{20,24},{24,28},{28,0},{1,5},{5... | collective-permute-start | bytes 153608 | tf_op jit(solution)/shard_map/ppermute | solution.py:26
  13.9 17.9 %collective-permute-start.4 = (bf16[2,100,128]{2,1,0:T(8,128)(2,1)S(1)}, bf16[2,100,128]{2,1,0:T(8,128)(2,1)S(1)}, u32[]{:S(2)}, u32[]{:S(2)}) collective-permute-start(bf16[2,100,128]{2,1,0:T(8,128)(2,1)S(1)} %get-tuple-element.27), channel_id=1, source_target_pairs={{0,28},{4,0},{8,4},{12,8},{16,12},{20,16},{24,20},{28,24},{1,29},{... | collective-permute-start | bytes 153608 | tf_op jit(solution)/shard_map/ppermute | solution.py:26
  16.7 15.2 %collective-permute-start.5 = (bf16[2,100,128]{2,1,0:T(8,128)(2,1)S(1)}, bf16[2,100,128]{2,1,0:T(8,128)(2,1)S(1)}, u32[]{:S(2)}, u32[]{:S(2)}) collective-permute-start(bf16[2,100,128]{2,1,0:T(8,128)(2,1)S(1)} %get-tuple-element.28), channel_id=1, source_target_pairs={{0,1},{1,2},{2,3},{3,0},{4,5},{5,6},{6,7},{7,4},{8,9},{9,10},{10,1... | collective-permute-start | bytes 153608 | tf_op jit(solution)/shard_map/ppermute | solution.py:26
  16.7 15.2 %copy-start.6 = (s32[32]{0:T(128)S(1)}, s32[32]{0:T(128)}, u32[]{:S(2)}) copy-start(s32[32]{0:T(128)} %count.1) | copy-start | bytes 388
  16.7 15.2 %collective-permute-start.6 = (bf16[2,100,128]{2,1,0:T(8,128)(2,1)S(1)}, bf16[2,100,128]{2,1,0:T(8,128)(2,1)S(1)}, u32[]{:S(2)}, u32[]{:S(2)}) collective-permute-start(bf16[2,100,128]{2,1,0:T(8,128)(2,1)S(1)} %get-tuple-element.29), channel_id=1, source_target_pairs={{0,3},{1,0},{2,1},{3,2},{4,7},{5,4},{6,5},{7,6},{8,11},{9,8},{10,9... | collective-permute-start | bytes 153608 | tf_op jit(solution)/shard_map/ppermute | solution.py:26
  50.0 12.9 %all-to-all-start.1 = ((f32[32,8,128]{2,1,0:T(8,128)}), f32[32,8,128]{2,1,0:T(8,128)S(1)}, u32[]{:S(2)}, u32[]{:S(2)}) async-start(f32[32,8,128]{2,1,0:T(8,128)} %metric.1), calls=%async_computation.1 | async-start | bytes 262144 | tf_op jit(solution)/shard_map/all_to_all | solution.py:329
  57.2 14.1 %collective-permute-start = (bf16[8,100,128]{2,1,0:T(8,128)(2,1)S(1)}, bf16[8,100,128]{2,1,0:T(8,128)(2,1)S(1)}, u32[]{:S(2)}, u32[]{:S(2)}) collective-permute-start(bf16[8,100,128]{2,1,0:T(8,128)(2,1)S(1)} %get-tuple-element.22), channel_id=1, source_target_pairs={{0,1},{1,0},{2,3},{3,2},{4,5},{5,4},{6,7},{7,6},{8,9},{9,8},{10,11... | collective-permute-start | bytes 614408 | tf_op jit(solution)/shard_map/ppermute | solution.py:31
  57.3 14.0 %collective-permute-start.1 = (bf16[8,100,128]{2,1,0:T(8,128)(2,1)S(1)}, bf16[8,100,128]{2,1,0:T(8,128)(2,1)S(1)}, u32[]{:S(2)}, u32[]{:S(2)}) collective-permute-start(bf16[8,100,128]{2,1,0:T(8,128)(2,1)S(1)} %get-tuple-element.23), channel_id=1, source_target_pairs={{0,2},{1,3},{2,0},{3,1},{4,6},{5,7},{6,4},{7,5},{8,10},{9,11},{10,... | collective-permute-start | bytes 614408 | tf_op jit(solution)/shard_map/ppermute | solution.py:31
  58.8 12.5 %collective-permute-start.2 = (bf16[8,100,128]{2,1,0:T(8,128)(2,1)S(1)}, bf16[8,100,128]{2,1,0:T(8,128)(2,1)S(1)}, u32[]{:S(2)}, u32[]{:S(2)}) collective-permute-start(bf16[8,100,128]{2,1,0:T(8,128)(2,1)S(1)} %get-tuple-element.24), channel_id=1, source_target_pairs={{0,3},{1,2},{2,1},{3,0},{4,7},{5,6},{6,5},{7,4},{8,11},{9,10},{10,... | collective-permute-start | bytes 614408 | tf_op jit(solution)/shard_map/ppermute | solution.py:31
  63.5 1.6 %collective-permute-start.7 = (f32[8,8,128]{2,1,0:T(8,128)S(1)}, f32[8,8,128]{2,1,0:T(8,128)S(1)}, u32[]{:S(2)}, u32[]{:S(2)}) collective-permute-start(f32[8,8,128]{2,1,0:T(8,128)S(1)} %get-tuple-element.32), channel_id=1, source_target_pairs={{0,1},{1,0},{2,3},{3,2},{4,5},{5,4},{6,7},{7,6},{8,9},{9,8},{10,11... | collective-permute-start | bytes 98312 | tf_op jit(solution)/shard_map/ppermute | solution.py:31
  63.6 6.9 %collective-permute-start.8 = (f32[8,8,128]{2,1,0:T(8,128)S(1)}, f32[8,8,128]{2,1,0:T(8,128)S(1)}, u32[]{:S(2)}, u32[]{:S(2)}) collective-permute-start(f32[8,8,128]{2,1,0:T(8,128)S(1)} %get-tuple-element.33), channel_id=1, source_target_pairs={{0,2},{1,3},{2,0},{3,1},{4,6},{5,7},{6,4},{7,5},{8,10},{9,11},{10,... | collective-permute-start | bytes 98312 | tf_op jit(solution)/shard_map/ppermute | solution.py:31
  65.1 5.4 %collective-permute-start.9 = (f32[8,8,128]{2,1,0:T(8,128)S(1)}, f32[8,8,128]{2,1,0:T(8,128)S(1)}, u32[]{:S(2)}, u32[]{:S(2)}) collective-permute-start(f32[8,8,128]{2,1,0:T(8,128)S(1)} %get-tuple-element.34), channel_id=1, source_target_pairs={{0,3},{1,2},{2,1},{3,0},{4,7},{5,6},{6,5},{7,4},{8,11},{9,10},{10,... | collective-permute-start | bytes 98312 | tf_op jit(solution)/shard_map/ppermute | solution.py:31

commit v3 on v2

v3 whole, which is shorter than its diff:
```python
import jax
import jax.numpy as jnp
from jax import lax
from jax.experimental import pallas as pl
from jax.experimental.pallas import tpu as pltpu
from jax.sharding import PartitionSpec as P

f32 = jnp.float32
bf16 = jnp.bfloat16
LANES = 128
FACES = 4
AHEAD = 4
THIRD = 32

SMEM = pl.BlockSpec(memory_space=pltpu.SMEM)
VMEM = pl.BlockSpec(memory_space=pltpu.VMEM)
HBM = pl.BlockSpec(memory_space=pltpu.HBM)


def grant(*shapes):
    return pltpu.CompilerParams(vmem_limit_bytes=sum(shapes) + (1 << 20))


def far_pairs(value, axis):
    count = lax.axis_size(axis)
    return lax.ppermute(
        value, axis, [(at, (at + (1 if at % 2 else -1)) % count) for at in range(count)]
    )


def swapped(value, axis, flip):
    count = lax.axis_size(axis)
    return lax.ppermute(value, axis, [(source, source ^ flip) for source in range(count)])


def padded_rows(rows):
    return (rows // 8 + 1) * 8


def sides():
    odd_wide = lax.axis_index("wide") % 2
    odd_narrow = lax.axis_index("narrow") % 2
    return odd_wide, 1 - odd_wide, 2 + odd_narrow, 3 - odd_narrow


def halo_kernel(coef, halo_blocks, *refs):
    outs, sems = refs[:4], refs[4]
    copies = []
    for k, side in enumerate(sides()):
        for h in range(outs[k].shape[0]):
            at = pl.multiple_of(halo_blocks[h, side] * LANES, LANES)
            copies.append(
                pltpu.make_async_copy(coef.at[:, pl.ds(at, LANES)], outs[k].at[h], sems.at[k, h])
            )
    for copy in copies:
        copy.start()
    for copy in copies:
        copy.wait()


def halo_pack(coef, halo_blocks):
    rows = coef.shape[0]
    count = halo_blocks.shape[0]
    return pl.pallas_call(
        halo_kernel,
        out_shape=[jax.ShapeDtypeStruct((count, rows, LANES), bf16)] * 4,
        in_specs=[HBM, SMEM],
        out_specs=[VMEM] * 4,
        scratch_shapes=[pltpu.SemaphoreType.DMA((4, count))],
        cost_estimate=pl.CostEstimate(
            flops=0, bytes_accessed=16 * count * rows * LANES, transcendentals=0
        ),
        compiler_params=grant(16 * count * padded_rows(rows) * LANES),
        name="halo_pack",
    )(coef, halo_blocks)


def stats_place(t, w, per_wide, slots):
    away = (w ^ lax.axis_index("wide")) % 2
    return away * (slots // 2) + (w // 2) * per_wide + t % per_wide


def pack_kernel(wide, narrow, coef, owner, count, packed, route, filled):
    rows = coef.shape[0]
    slots, tall = packed.shape[0], packed.shape[1]
    blocks = owner.shape[0]
    per_wide = slots // wide

    def clear(w, _):
        filled[w] = 0
        return 0

    lax.fori_loop(0, wide, clear, 0)
    if slots > blocks:
        for t in range(slots):
            packed[t, rows:tall, :] = jnp.full((tall - rows, LANES), -1, bf16)
    for b in range(blocks):
        target = owner[b]
        w = target // narrow
        t = w * per_wide + filled[w]
        filled[w] = filled[w] + 1
        route[0, b] = stats_place(t, w, per_wide, slots) if slots == blocks else t
        route[1, b] = count[b]
        packed[t, 0:rows, :] = coef[:, b * LANES : (b + 1) * LANES]
        packed[t, rows:tall, :] = jnp.full((tall - rows, LANES), (target % narrow).astype(f32)).astype(
            bf16
        )


def pack(coef, owner, count, wide, narrow):
    rows, elems = coef.shape
    blocks = owner.shape[0]
    slots = wide * max(1, blocks // wide)
    return pl.pallas_call(
        lambda *refs: pack_kernel(wide, narrow, *refs),
        out_shape=[
            jax.ShapeDtypeStruct((slots, padded_rows(rows), LANES), bf16),
            jax.ShapeDtypeStruct((2, blocks), jnp.int32),
        ],
        in_specs=[VMEM, SMEM, SMEM],
        out_specs=[VMEM, SMEM],
        scratch_shapes=[pltpu.SMEM((wide,), jnp.int32)],
        cost_estimate=pl.CostEstimate(flops=0, bytes_accessed=4 * rows * elems, transcendentals=0),
        compiler_params=grant(2 * rows * elems, 3 * slots * padded_rows(rows) * LANES),
        name="pack",
    )(coef, owner, count)


def metric_kernel(nb, routes, coef, h0, h1, h2, h3, w, *refs):
    *outs, table, accs, wp, idx, sem, stats, route, arrived = refs
    rows, depth = w.shape[1], w.shape[2]
    third = rows // 3
    elems = coef.shape[1]
    groups = elems // (AHEAD * LANES)

    def fetch(g, s):
        at = pl.multiple_of(g * (AHEAD * LANES), LANES)
        return pltpu.make_async_copy(nb.at[:, pl.ds(at, AHEAD * LANES)], idx.at[s], sem.at[s])

    fetch(0, 0).start()
    fetch(1, 1).start()
    routing = pltpu.make_async_copy(routes, route, arrived)
    routing.start()
    line = lax.broadcasted_iota(jnp.int32, (3 * THIRD, rows), 0)
    row = lax.broadcasted_iota(jnp.int32, (3 * THIRD, rows), 1)
    order = ((row == 3 * (line % THIRD) + line // THIRD) & (line % THIRD < third)).astype(bf16)
    spare = jnp.zeros((3 * THIRD, LANES - depth), bf16)
    for f in range(FACES + 1):
        ordered = jnp.dot(order, w[f], preferred_element_type=f32).astype(bf16)
        wp[:, f * LANES : (f + 1) * LANES] = jnp.concatenate([ordered, spare], axis=1)

    def by_element(cols):
        turned = cols.astype(f32).T
        return jnp.concatenate([turned, jnp.zeros((turned.shape[0], LANES - depth), f32)], axis=1)

    step = 512

    def fill(i, _):
        at = pl.multiple_of(i * step, step)
        table[pl.ds(at, step), :] = by_element(coef[:, pl.ds(at, step)])
        return 0

    lax.fori_loop(0, elems // step, fill, 0)
    for side, halo in zip(sides(), (h0, h1, h2, h3)):
        for h in range(halo.shape[0]):
            at = pl.multiple_of(elems + (side * halo.shape[0] + h) * LANES, LANES)
            table[pl.ds(at, LANES), :] = by_element(halo[h])

    def gather(s, p):
        for e in range(LANES):
            for f in range(FACES):
                accs[s * AHEAD + p, pl.ds(e, 1), f * LANES : (f + 1) * LANES] = table[
                    pl.ds(idx[s, f, p * LANES + e], 1), :
                ]

    def metric(b, s, p):
        at = pl.multiple_of(b * LANES, LANES)
        d = jnp.dot(
            wp[:, 0:depth], coef[:, pl.ds(at, LANES)], preferred_element_type=f32
        ) + lax.dot_general(
            wp[:, LANES:],
            accs[s * AHEAD + p].astype(bf16),
            (((1,), (1,)), ((), ())),
            preferred_element_type=f32,
        )
        x, y, z = d[0:THIRD], d[THIRD : 2 * THIRD], d[2 * THIRD :]
        inverse = 1.0 / third

        def mean(p):
            return inverse * jnp.sum(p, axis=0, keepdims=True)

        xx, yy, zz = 1.0 + mean(x * x), 1.0 + mean(y * y), 1.0 + mean(z * z)
        xy, xz, yz = mean(x * y), mean(x * z), mean(y * z)
        det = xx * (yy * zz - yz * yz) - xy * (xy * zz - yz * xz) + xz * (xy * yz - yy * xz)
        work = route[1, b].astype(f32) * jnp.sqrt(det)
        stats[route[0, b]] = jnp.concatenate([xx, yy, zz, xy, xz, yz, work, work], axis=0)

    routing.wait()

    def two_groups(i, _):
        for s in range(2):
            g = 2 * i + s
            earlier = jnp.maximum(g - 1, 0) if s == 0 else g - 1
            fetch(g, s).wait()
            for p in range(AHEAD):
                metric(earlier * AHEAD + p, 1 - s, p)
                gather(s, p)
            fetch(jnp.minimum(g + 2, groups - 1), s).start()
        return 0

    lax.fori_loop(0, groups // 2, two_groups, 0)
    for p in range(AHEAD):
        metric((groups - 1) * AHEAD + p, 1, p)
    for s in range(2):
        fetch(groups - 1, s).wait()
    size = outs[0].shape[0]
    for k, out in enumerate(outs):
        out[...] = stats[k * size : (k + 1) * size]


def metrics(nb, route, coef, halos, w, slots):
    elems = coef.shape[1]
    table = elems + sum(h.shape[0] for h in halos) * LANES
    parts = 2 if slots == elems // LANES else 1
    return pl.pallas_call(
        metric_kernel,
        out_shape=[jax.ShapeDtypeStruct((slots // parts, 8, LANES), f32)] * parts,
        in_specs=[HBM, HBM] + [VMEM] * 6,
        out_specs=[VMEM] * parts,
        scratch_shapes=[
            pltpu.VMEM((table, LANES), f32),
            pltpu.VMEM((2 * AHEAD, LANES, FACES * LANES), f32),
            pltpu.VMEM((3 * THIRD, (FACES + 1) * LANES), bf16),
            pltpu.SMEM((2, FACES, AHEAD * LANES), jnp.int32),
            pltpu.SemaphoreType.DMA((2,)),
            pltpu.VMEM((slots, 8, LANES), f32),
            pltpu.SMEM(route.shape, jnp.int32),
            pltpu.SemaphoreType.DMA(()),
        ],
        cost_estimate=pl.CostEstimate(
            flops=2 * elems * 5 * LANES * LANES, bytes_accessed=20 * elems * LANES, transcendentals=elems
        ),
        compiler_params=grant(4 * table * LANES, 3 * 104 * elems, 96 * slots * LANES, 5 << 20),
        name="metric",
    )(nb, route, coef, *halos, w)


def relay_kernel(narrow, arrived, *refs):
    sends, order, words, tags, filled, sem = refs[:narrow], *refs[narrow:]
    slots, tall = arrived.shape[0], arrived.shape[1]
    per, rows = sends[0].shape[0], sends[0].shape[1]
    for t in range(slots):
        words[t : t + 1, :] = arrived[t, tall - 8 : tall, :].astype(f32)[7:8].astype(jnp.int32)
    copy = pltpu.make_async_copy(words, tags, sem)
    copy.start()
    copy.wait()
    for c in range(narrow + 1):
        filled[c] = c * per
    for t in range(slots):
        tag = tags[t, 0]
        c = jnp.where(tag < 0, narrow, tag)
        at = filled[c]
        order[at] = t
        filled[c] = at + 1
    mine = lax.axis_index("narrow")
    for k in range(narrow):
        for j in range(per):
            sends[k][j] = arrived[order[(mine ^ k) * per + j], 0:rows, :]


def relay(arrived, rows, narrow, blocks):
    slots = arrived.shape[0]
    per = blocks // narrow
    *sends, order = pl.pallas_call(
        lambda *refs: relay_kernel(narrow, *refs),
        out_shape=[jax.ShapeDtypeStruct((per, rows, LANES), bf16)] * narrow
        + [jax.ShapeDtypeStruct((blocks + slots,), jnp.int32)],
        in_specs=[VMEM],
        out_specs=[VMEM] * narrow + [SMEM],
        scratch_shapes=[
            pltpu.VMEM((slots, LANES), jnp.int32),
            pltpu.SMEM((slots, LANES), jnp.int32),
            pltpu.SMEM((narrow + 1,), jnp.int32),
            pltpu.SemaphoreType.DMA(()),
        ],
        cost_estimate=pl.CostEstimate(
            flops=0, bytes_accessed=4 * blocks * rows * LANES, transcendentals=0
        ),
        compiler_params=grant(3 * (slots + blocks) * padded_rows(rows) * LANES),
        name="relay",
    )(arrived)
    return sends, order


def merge_kernel(kept, got, *sends):
    per = sends[0].shape[0] // 2
    mine = lax.axis_index("wide") // 2
    for j, send in enumerate(sends):
        at = (mine ^ j) * per
        for i in range(per):
            send[i] = kept[at + i]
            send[per + i] = got[at + i]


def merge(kept, got, wide):
    half = kept.shape[0]
    groups = wide // 2
    return pl.pallas_call(
        merge_kernel,
        out_shape=[jax.ShapeDtypeStruct((2 * half // groups, 8, LANES), f32)] * groups,
        in_specs=[VMEM] * 2,
        out_specs=[VMEM] * groups,
        cost_estimate=pl.CostEstimate(flops=0, bytes_accessed=128 * half * LANES, transcendentals=0),
        compiler_params=grant(4 * 64 * half * LANES),
        name="merge",
    )(kept, got)


def relay_stats_kernel(narrow, per_wide, *refs):
    parts, order, sends, held = refs[: -narrow - 2], refs[-narrow - 2], refs[-narrow - 1 : -1], refs[-1]
    per = sends[0].shape[0]
    mine = lax.axis_index("narrow")
    wide = lax.axis_index("wide")
    size = parts[0].shape[0]
    for j, part in enumerate(parts):
        held[j * size : (j + 1) * size] = part[...]
    for k in range(narrow):
        for j in range(per):
            t = order[(mine ^ k) * per + j]
            if len(parts) > 1:
                t = ((t // per_wide) ^ wide) * per_wide + t % per_wide
            sends[k][j] = held[t]


def relay_stats(parts, order, narrow, per_wide, blocks):
    per = blocks // narrow
    slots = len(parts) * parts[0].shape[0]
    return pl.pallas_call(
        lambda *refs: relay_stats_kernel(narrow, per_wide, *refs),
        out_shape=[jax.ShapeDtypeStruct((per, 8, LANES), f32)] * narrow,
        in_specs=[VMEM] * len(parts) + [SMEM],
        out_specs=[VMEM] * narrow,
        scratch_shapes=[pltpu.VMEM((slots, 8, LANES), f32)],
        cost_estimate=pl.CostEstimate(flops=0, bytes_accessed=64 * slots * LANES, transcendentals=0),
        compiler_params=grant(4 * 32 * (slots + blocks) * LANES),
        name="relay_stats",
    )(*parts, order)


def place_kernel(*refs):
    parts, out = refs[:-1], refs[-1]
    per = parts[0].shape[0]
    mine = lax.axis_index("narrow")
    for k, part in enumerate(parts):
        for j in range(per):
            at = pl.multiple_of(((mine ^ k) * per + j) * LANES, LANES)
            out[:, pl.ds(at, LANES)] = part[j]


def place(parts):
    per, rows, _ = parts[0].shape
    return pl.pallas_call(
        place_kernel,
        out_shape=jax.ShapeDtypeStruct((rows, len(parts) * per * LANES), bf16),
        in_specs=[VMEM] * len(parts),
        out_specs=VMEM,
        compiler_params=grant(6 * len(parts) * per * padded_rows(rows) * LANES),
        name="place",
    )(*parts)


def place_stats_kernel(*refs):
    parts, metric, work = refs[:-2], refs[-2], refs[-1]
    per = parts[0].shape[0]
    mine = lax.axis_index("narrow")
    for k, part in enumerate(parts):
        for j in range(per):
            t = (mine ^ k) * per + j
            at = pl.multiple_of(t * LANES, LANES)
            metric[:, pl.ds(at, LANES)] = part[j, 0:6, :]
            work[pl.ds(t, 1), :] = part[j, 6:7, :]


def place_stats(parts):
    per = parts[0].shape[0]
    blocks = len(parts) * per
    return pl.pallas_call(
        place_stats_kernel,
        out_shape=[
            jax.ShapeDtypeStruct((6, blocks * LANES), f32),
            jax.ShapeDtypeStruct((blocks, LANES), f32),
        ],
        in_specs=[VMEM] * len(parts),
        out_specs=[VMEM] * 2,
        compiler_params=grant(3 * 32 * blocks * LANES),
        name="place_stats",
    )(*parts)


def per_device(coefficients, neighbours, halo_blocks, recon_weight, owner_device, work_count):
    wide = lax.axis_size("wide")
    narrow = lax.axis_size("narrow")
    rows, _ = coefficients.shape
    blocks = owner_device.shape[0]
    sent = halo_pack(coefficients, halo_blocks[0].T)
    halos = [
        far_pairs(sent[0], "wide"),
        swapped(sent[1], "wide", 1),
        far_pairs(sent[2], "narrow"),
        swapped(sent[3], "narrow", 1),
    ]
    packed, route = pack(coefficients, owner_device, work_count, wide, narrow)
    slots = packed.shape[0]
    arrived = lax.all_to_all(packed, "wide", 0, 0, tiled=True)
    stats = metrics(neighbours, route, coefficients, halos, recon_weight, slots)
    if len(stats) == 1:
        stats_arrived = [lax.all_to_all(stats[0], "wide", 0, 0, tiled=True)]
    else:
        got = swapped(stats[1], "wide", 1)
        stats_arrived = list(merge(stats[0], got, wide))
        for j in range(1, wide // 2):
            stats_arrived[j] = swapped(stats_arrived[j], "wide", 2 * j)
    sends, order = relay(arrived, rows, narrow, blocks)
    parts = [sends[0]] + [swapped(sends[k], "narrow", k) for k in range(1, narrow)]
    stats_sends = relay_stats(stats_arrived, order, narrow, slots // wide, blocks)
    stats_parts = [stats_sends[0]] + [
        swapped(stats_sends[k], "narrow", k) for k in range(1, narrow)
    ]
    modal = place(parts)
    metric, work = place_stats(stats_parts)
    return modal, metric, work.reshape(-1)


def solution(mesh):
    return jax.shard_map(
        per_device,
        mesh=mesh,
        in_specs=(
            P(None, ("wide", "narrow")),
            P(None, ("wide", "narrow")),
            P(("wide", "narrow"), None, None),
            P(),
            P(("wide", "narrow")),
            P(("wide", "narrow")),
        ),
        out_specs=(P(None, ("wide", "narrow")), P(None, ("wide", "narrow")), P(("wide", "narrow"))),
        check_vma=False,
    )
```

time: 72.7 us -> 73.5 us (1.011)
  Pallas kernels: 24 us -> 19.9 us
  waiting for transfers between devices: 21.8 us -> 25.7 us
  local copies, waits for them, and re-layouts: 1.84 us -> 3.14 us
    all_to_all x1, waiting for transfers between devices: 0.01 us -> 14.4 us  [per_device(): arrived = lax.all_to_all(packed, 'wide', 0, 0, tiled=True)]
    ppermute x4 -> x2, waiting for transfers between devices: 13.4 us -> 0.01 us  [far_pairs(): lax.ppermute(value, axis, [(at, (at + (1 if at % 2 else -1)) % count) for...]
    ppermute x6 -> x12, starting transfers between devices: 4.41 us -> 11.4 us  [swapped(): lax.ppermute(value, axis, [(source, source ^ flip) for source in range(co...]
    ppermute x6 -> x12, waiting for transfers between devices: 4.54 us -> 11.3 us  [swapped(): lax.ppermute(value, axis, [(source, source ^ flip) for source in range(co...]
    all_to_all x1 -> x0, starting transfers between devices: 5.58 us -> none  [per_device(): stats_arrived = lax.all_to_all(stats, 'wide', 0, 0, tiled=True)]
    pallas_call x2 -> x4, Pallas kernels: 18.7 us -> 14.4 us  [the longest x1 12.9 us: metrics(): pl.pallas_call(metric_kernel, out_shape=[jax.ShapeDtypeStruct((slots // p...]
    all_to_all x1 -> x0, waiting for transfers between devices: 3.81 us -> none  [per_device(): stats_arrived = lax.all_to_all(stats, 'wide', 0, 0, tiled=True)]
    ppermute x4 -> x2, starting transfers between devices: 6.49 us -> 4.88 us  [far_pairs(): lax.ppermute(value, axis, [(at, (at + (1 if at % 2 else -1)) % count) for...]
  transfers between devices with their start and end apart: 12 -> 15, of which waited for: 3 -> 7; matrix products, arithmetic and copies ran while one was open for 0% -> 0% of each run, Pallas kernels for 29% -> 23%
where the time goes in v3:
time: 73.5 us; the launch traced here: 73.3 us
  waiting for transfers between devices  25.7 us (35%)
  starting transfers between devices  23.8 us (32%)
  Pallas kernels  19.9 us (27%)
  local copies, waits for them, and re-layouts  3.14 us (4%)
  between operations  0.76 us (1%)
    all_to_all x1, waiting for transfers between devices, per_device(): arrived = lax.all_to_all(packed, 'wide', 0, 0, tiled=True)  14.4 us
    pallas_call x1, Pallas kernels, metrics(): pl.pallas_call(metric_kernel, out_shape=[jax.ShapeDtypeStruct((slots // p...  12.9 us
    ppermute x12, starting transfers between devices, swapped(): lax.ppermute(value, axis, [(source, source ^ flip) for source in range(co...  11.4 us
    ppermute x12, waiting for transfers between devices, swapped(): lax.ppermute(value, axis, [(source, source ^ flip) for source in range(co...  11.3 us
    all_to_all x1, starting transfers between devices, per_device(): arrived = lax.all_to_all(packed, 'wide', 0, 0, tiled=True)  7.45 us
    ppermute x2, starting transfers between devices, far_pairs(): lax.ppermute(value, axis, [(at, (at + (1 if at % 2 else -1)) % count) for...  4.88 us
    unnamed x14, local copies, waits for them, and re-layouts  3.14 us
    pallas_call x1, Pallas kernels, pack(): pl.pallas_call(lambda *refs: pack_kernel(wide, narrow, *refs), out_shape=...  2.08 us
  transfers between devices with their start and end apart: 15, of which 7 were waited for; matrix products, arithmetic and copies ran while one was open for 0% of the time, Pallas kernels for 23%

profile of v3, /device:TPU:0, one launch (start us, length us, event | category | flops | bytes accessed | tf_op | source)
XLA Modules:
  0.0 73.3 jit_solution(12461259069639774473)
XLA Ops:
  0.6 1.1 %copy-done = bf16[100,4096]{1,0:T(8,128)(2,1)S(1)} copy-done((bf16[100,4096]{1,0:T(8,128)(2,1)S(1)}, bf16[100,4096]{1,0:T(8,128)(2,1)}, u32[]{:S(2)}) %copy-start) | copy-done | bytes 819224
  1.8 0.7 copy-done.3
  2.4 0.7 copy-done.4
  3.1 2.1 %pack.1 = (bf16[32,104,128]{2,1,0:T(8,128)(2,1)}, s32[2,32]{1,0:T(2,128)S(1)}) custom-call(bf16[100,4096]{1,0:T(8,128)(2,1)S(1)} %copy-done, s32[32]{0:T(128)S(1)} %copy-done.3, s32[32]{0:T(128)S(1)} %copy-done.4), custom_call_target="tpu_custom_call" | custom-call | bytes 1638400 | tf_op jit(solution)/shard_map/pack/pallas_call | solution.py:114
  5.2 7.5 %all-to-all-start = ((bf16[32,104,128]{2,1,0:T(8,128)(2,1)}), bf16[32,104,128]{2,1,0:T(8,128)(2,1)S(1)}, u32[]{:S(2)}, u32[]{:S(2)}) async-start(bf16[32,104,128]{2,1,0:T(8,128)(2,1)} %get-tuple-element.26), calls=%async_computation | async-start | bytes 1703936 | tf_op jit(solution)/shard_map/all_to_all | solution.py:414
  12.7 0.7 copy-done.2
  13.3 0.7 halo_pack.1
  14.1 4.8 %collective-permute-start.3 = (bf16[2,100,128]{2,1,0:T(8,128)(2,1)S(1)}, bf16[2,100,128]{2,1,0:T(8,128)(2,1)S(1)}, u32[]{:S(2)}, u32[]{:S(2)}) collective-permute-start(bf16[2,100,128]{2,1,0:T(8,128)(2,1)S(1)} %get-tuple-element.32), channel_id=1, source_target_pairs={{0,28},{4,8},{8,4},{12,16},{16,12},{20,24},{24,20},{28,0},{1,29},{... | collective-permute-start | bytes 153608 | tf_op jit(solution)/shard_map/ppermute | solution.py:26
  18.9 0.1 collective-permute-start.5
  19.0 1.5 %collective-permute-start.6 = (bf16[2,100,128]{2,1,0:T(8,128)(2,1)S(1)}, bf16[2,100,128]{2,1,0:T(8,128)(2,1)S(1)}, u32[]{:S(2)}, u32[]{:S(2)}) collective-permute-start(bf16[2,100,128]{2,1,0:T(8,128)(2,1)S(1)} %get-tuple-element.35), channel_id=1, source_target_pairs={{0,1},{1,0},{2,3},{3,2},{4,5},{5,4},{6,7},{7,6},{8,9},{9,8},{10,11... | collective-permute-start | bytes 153608 | tf_op jit(solution)/shard_map/ppermute | solution.py:33
  20.5 14.4 %all-to-all-done.refs_0_ = bf16[32,104,128]{2,1,0:T(8,128)(2,1)S(1)} async-done(((bf16[32,104,128]{2,1,0:T(8,128)(2,1)}), bf16[32,104,128]{2,1,0:T(8,128)(2,1)S(1)}, u32[]{:S(2)}, u32[]{:S(2)}) %all-to-all-start) | async-done | bytes 852000 | tf_op jit(solution)/shard_map/all_to_all | solution.py:414
  34.9 1.6 %relay.1 = (bf16[8,100,128]{2,1,0:T(8,128)(2,1)S(1)}, bf16[8,100,128]{2,1,0:T(8,128)(2,1)S(1)}, bf16[8,100,128]{2,1,0:T(8,128)(2,1)S(1)}, bf16[8,100,128]{2,1,0:T(8,128)(2,1)S(1)}, s32[64]{0:T(128)S(1)}) custom-call(bf16[32,104,128]{2,1,0:T(8,128)(2,1)S(1)} %all-to-all-done.refs_0_), custom_call_target="tpu_custom_call" | custom-call | bytes 1638400 | tf_op jit(solution)/shard_map/relay/pallas_call | solution.py:274
  36.5 0.1 collective-permute-start
  36.6 1.6 %collective-permute-start.1 = (bf16[8,100,128]{2,1,0:T(8,128)(2,1)S(1)}, bf16[8,100,128]{2,1,0:T(8,128)(2,1)S(1)}, u32[]{:S(2)}, u32[]{:S(2)}) collective-permute-start(bf16[8,100,128]{2,1,0:T(8,128)(2,1)S(1)} %get-tuple-element.29), channel_id=1, source_target_pairs={{0,2},{1,3},{2,0},{3,1},{4,6},{5,7},{6,4},{7,5},{8,10},{9,11},{10,... | collective-permute-start | bytes 614408 | tf_op jit(solution)/shard_map/ppermute | solution.py:33
  38.1 0.3 collective-permute-start.2
  38.4 12.9 %metric.1 = (f32[16,8,128]{2,1,0:T(8,128)S(1)}, f32[16,8,128]{2,1,0:T(8,128)S(1)}) custom-call(s32[4,4096]{1,0:T(4,128)S(1)} %copy-done.6, s32[2,32]{1,0:T(2,128)S(1)} %get-tuple-element.31.routes, bf16[100,4096]{1,0:T(8,128)(2,1)S(1)} %copy-done.1, bf16[2,100,128]{2,1,0:T(8,128)(2,1)S(1)} %collective-permute-done.3.h0, ...), custom_call_target="tpu_custom_call" | custom-call | flops 671088640 | bytes 10485760 | tf_op jit(solution)/shard_map/metric/pallas_call | solution.py:225
  51.3 2.0 %collective-permute-start.7 = (f32[16,8,128]{2,1,0:T(8,128)S(1)}, f32[16,8,128]{2,1,0:T(8,128)S(1)}, u32[]{:S(2)}, u32[]{:S(2)}) collective-permute-start(f32[16,8,128]{2,1,0:T(8,128)S(1)} %get-tuple-element.37), channel_id=1, source_target_pairs={{0,4},{4,0},{8,12},{12,8},{16,20},{20,16},{24,28},{28,24},{1,5},{5... | collective-permute-start | bytes 196616 | tf_op jit(solution)/shard_map/ppermute | solution.py:33
  53.3 2.6 %collective-permute-done.7.got = f32[16,8,128]{2,1,0:T(8,128)S(1)} collective-permute-done((f32[16,8,128]{2,1,0:T(8,128)S(1)}, f32[16,8,128]{2,1,0:T(8,128)S(1)}, u32[]{:S(2)}, u32[]{:S(2)}) %collective-permute-start.7) | collective-permute-done | bytes 65568 | tf_op jit(solution)/shard_map/ppermute | solution.py:33
  55.9 0.5 collective-permute-start.8
  56.5 1.6 %collective-permute-start.9 = (f32[8,8,128]{2,1,0:T(8,128)S(1)}, f32[8,8,128]{2,1,0:T(8,128)S(1)}, u32[]{:S(2)}, u32[]{:S(2)}) collective-permute-start(f32[8,8,128]{2,1,0:T(8,128)S(1)} %get-tuple-element.40), channel_id=1, source_target_pairs={{0,16},{4,20},{8,24},{12,28},{16,0},{20,4},{24,8},{28,12},{1,17},{... | collective-permute-start | bytes 98312 | tf_op jit(solution)/shard_map/ppermute | solution.py:33
  58.0 1.9 %collective-permute-done.8.refs_1_ = f32[8,8,128]{2,1,0:T(8,128)S(1)} collective-permute-done((f32[8,8,128]{2,1,0:T(8,128)S(1)}, f32[8,8,128]{2,1,0:T(8,128)S(1)}, u32[]{:S(2)}, u32[]{:S(2)}) %collective-permute-start.8) | collective-permute-done | bytes 32800 | tf_op jit(solution)/shard_map/ppermute | solution.py:33
  59.9 1.4 %collective-permute-start.10 = (f32[8,8,128]{2,1,0:T(8,128)S(1)}, f32[8,8,128]{2,1,0:T(8,128)S(1)}, u32[]{:S(2)}, u32[]{:S(2)}) collective-permute-start(f32[8,8,128]{2,1,0:T(8,128)S(1)} %get-tuple-element.41), channel_id=1, source_target_pairs={{0,24},{4,28},{8,16},{12,20},{16,8},{20,12},{24,0},{28,4},{1,25},{... | collective-permute-start | bytes 98312 | tf_op jit(solution)/shard_map/ppermute | solution.py:33
  61.4 0.1 collective-permute-done.9.refs_2_
  61.5 4.2 %collective-permute-done.10.refs_3_ = f32[8,8,128]{2,1,0:T(8,128)S(1)} collective-permute-done((f32[8,8,128]{2,1,0:T(8,128)S(1)}, f32[8,8,128]{2,1,0:T(8,128)S(1)}, u32[]{:S(2)}, u32[]{:S(2)}) %collective-permute-start.10) | collective-permute-done | bytes 32800 | tf_op jit(solution)/shard_map/ppermute | solution.py:33
  65.7 0.8 %relay_stats.1 = (f32[8,8,128]{2,1,0:T(8,128)S(1)}, f32[8,8,128]{2,1,0:T(8,128)S(1)}, f32[8,8,128]{2,1,0:T(8,128)S(1)}, f32[8,8,128]{2,1,0:T(8,128)S(1)}) custom-call(f32[8,8,128]{2,1,0:T(8,128)S(1)} %get-tuple-element.38.refs_0_, f32[8,8,128]{2,1,0:T(8,128)S(1)} %collective-permute-done.8.refs_1_, f32[8,8,128]{2,1,0:T(8,128)S(1)} %collective-permute-done.9.refs_2_, ...), custom_call_target="tpu_custom_call" | custom-call | bytes 262144 | tf_op jit(solution)/shard_map/relay_stats/pallas_call | solution.py:338
  66.4 0.1 collective-permute-start.11
  66.5 1.6 %collective-permute-start.12 = (f32[8,8,128]{2,1,0:T(8,128)S(1)}, f32[8,8,128]{2,1,0:T(8,128)S(1)}, u32[]{:S(2)}, u32[]{:S(2)}) collective-permute-start(f32[8,8,128]{2,1,0:T(8,128)S(1)} %get-tuple-element.45), channel_id=1, source_target_pairs={{0,2},{1,3},{2,0},{3,1},{4,6},{5,7},{6,4},{7,5},{8,10},{9,11},{10,... | collective-permute-start | bytes 98312 | tf_op jit(solution)/shard_map/ppermute | solution.py:33
  68.1 0.9 %collective-permute-start.13 = (f32[8,8,128]{2,1,0:T(8,128)S(1)}, f32[8,8,128]{2,1,0:T(8,128)S(1)}, u32[]{:S(2)}, u32[]{:S(2)}) collective-permute-start(f32[8,8,128]{2,1,0:T(8,128)S(1)} %get-tuple-element.46), channel_id=1, source_target_pairs={{0,3},{1,2},{2,1},{3,0},{4,7},{5,6},{6,5},{7,4},{8,11},{9,10},{10,... | collective-permute-start | bytes 98312 | tf_op jit(solution)/shard_map/ppermute | solution.py:33
  69.0 1.5 %collective-permute-done.12.refs_2_ = f32[8,8,128]{2,1,0:T(8,128)S(1)} collective-permute-done((f32[8,8,128]{2,1,0:T(8,128)S(1)}, f32[8,8,128]{2,1,0:T(8,128)S(1)}, u32[]{:S(2)}, u32[]{:S(2)}) %collective-permute-start.12) | collective-permute-done | bytes 32800 | tf_op jit(solution)/shard_map/ppermute | solution.py:33
  70.5 0.9 %collective-permute-done.13.refs_3_ = f32[8,8,128]{2,1,0:T(8,128)S(1)} collective-permute-done((f32[8,8,128]{2,1,0:T(8,128)S(1)}, f32[8,8,128]{2,1,0:T(8,128)S(1)}, u32[]{:S(2)}, u32[]{:S(2)}) %collective-permute-start.13) | collective-permute-done | bytes 32800 | tf_op jit(solution)/shard_map/ppermute | solution.py:33
  71.4 0.7 place_stats.1
  72.1 1.1 %place.1 = bf16[100,4096]{1,0:T(8,128)(2,1)} custom-call(bf16[8,100,128]{2,1,0:T(8,128)(2,1)S(1)} %get-tuple-element.27.refs_0_, bf16[8,100,128]{2,1,0:T(8,128)(2,1)S(1)} %collective-permute-done.refs_1_, bf16[8,100,128]{2,1,0:T(8,128)(2,1)S(1)} %collective-permute-done.1.refs_2_, bf16[8,100,128]{2,1,0:T(8,128)(2,1)S(1)} %collective-permute-done.2.refs_3_), custom_call_target="tpu_custom_call" | custom-call | tf_op jit(solution)/shard_map/place/pallas_call | solution.py:362
  (20 shorter events, 0.1 us)
Async XLA Ops:
  0.6 1.2 %copy-start = (bf16[100,4096]{1,0:T(8,128)(2,1)S(1)}, bf16[100,4096]{1,0:T(8,128)(2,1)}, u32[]{:S(2)}) copy-start(bf16[100,4096]{1,0:T(8,128)(2,1)} %coef.3) | copy-start | bytes 2457604
  1.8 0.7 copy-start.3
  2.4 0.7 copy-start.4
  5.2 7.5 %copy-start.1 = (bf16[100,4096]{1,0:T(8,128)(2,1)S(1)}, bf16[100,4096]{1,0:T(8,128)(2,1)}, u32[]{:S(2)}) copy-start(bf16[100,4096]{1,0:T(8,128)(2,1)} %coef.3) | copy-start | bytes 2457604
  5.2 29.7 %all-to-all-start = ((bf16[32,104,128]{2,1,0:T(8,128)(2,1)}), bf16[32,104,128]{2,1,0:T(8,128)(2,1)S(1)}, u32[]{:S(2)}, u32[]{:S(2)}) async-start(bf16[32,104,128]{2,1,0:T(8,128)(2,1)} %get-tuple-element.26), calls=%async_computation | async-start | bytes 1703936 | tf_op jit(solution)/shard_map/all_to_all | solution.py:414
  12.7 0.7 copy-start.2
  14.1 22.5 %collective-permute-start.3 = (bf16[2,100,128]{2,1,0:T(8,128)(2,1)S(1)}, bf16[2,100,128]{2,1,0:T(8,128)(2,1)S(1)}, u32[]{:S(2)}, u32[]{:S(2)}) collective-permute-start(bf16[2,100,128]{2,1,0:T(8,128)(2,1)S(1)} %get-tuple-element.32), channel_id=1, source_target_pairs={{0,28},{4,8},{8,4},{12,16},{16,12},{20,24},{24,20},{28,0},{1,29},{... | collective-permute-start | bytes 153608 | tf_op jit(solution)/shard_map/ppermute | solution.py:26
  18.9 19.3 %collective-permute-start.4 = (bf16[2,100,128]{2,1,0:T(8,128)(2,1)S(1)}, bf16[2,100,128]{2,1,0:T(8,128)(2,1)S(1)}, u32[]{:S(2)}, u32[]{:S(2)}) collective-permute-start(bf16[2,100,128]{2,1,0:T(8,128)(2,1)S(1)} %get-tuple-element.33), channel_id=1, source_target_pairs={{0,4},{4,0},{8,12},{12,8},{16,20},{20,16},{24,28},{28,24},{1,5},{5... | collective-permute-start | bytes 153608 | tf_op jit(solution)/shard_map/ppermute | solution.py:33
  18.9 19.6 %collective-permute-start.5 = (bf16[2,100,128]{2,1,0:T(8,128)(2,1)S(1)}, bf16[2,100,128]{2,1,0:T(8,128)(2,1)S(1)}, u32[]{:S(2)}, u32[]{:S(2)}) collective-permute-start(bf16[2,100,128]{2,1,0:T(8,128)(2,1)S(1)} %get-tuple-element.34), channel_id=1, source_target_pairs={{0,3},{1,2},{2,1},{3,0},{4,7},{5,6},{6,5},{7,4},{8,11},{9,10},{10,... | collective-permute-start | bytes 153608 | tf_op jit(solution)/shard_map/ppermute | solution.py:26
  19.0 19.5 %copy-start.5 = (bf16[5,75,100]{2,1,0:T(8,128)(2,1)S(1)}, bf16[5,75,100]{2,1,0:T(8,128)(2,1)}, u32[]{:S(2)}) copy-start(bf16[5,75,100]{2,1,0:T(8,128)(2,1)} %w.1) | copy-start | bytes 225004
  19.0 19.5 %copy-start.6 = (s32[4,4096]{1,0:T(4,128)S(1)}, s32[4,4096]{1,0:T(4,128)}, u32[]{:S(2)}) copy-start(s32[4,4096]{1,0:T(4,128)} %nb.1) | copy-start | bytes 196612
  19.0 19.5 %collective-permute-start.6 = (bf16[2,100,128]{2,1,0:T(8,128)(2,1)S(1)}, bf16[2,100,128]{2,1,0:T(8,128)(2,1)S(1)}, u32[]{:S(2)}, u32[]{:S(2)}) collective-permute-start(bf16[2,100,128]{2,1,0:T(8,128)(2,1)S(1)} %get-tuple-element.35), channel_id=1, source_target_pairs={{0,1},{1,0},{2,3},{3,2},{4,5},{5,4},{6,7},{7,6},{8,9},{9,8},{10,11... | collective-permute-start | bytes 153608 | tf_op jit(solution)/shard_map/ppermute | solution.py:33
  36.5 35.7 %collective-permute-start = (bf16[8,100,128]{2,1,0:T(8,128)(2,1)S(1)}, bf16[8,100,128]{2,1,0:T(8,128)(2,1)S(1)}, u32[]{:S(2)}, u32[]{:S(2)}) collective-permute-start(bf16[8,100,128]{2,1,0:T(8,128)(2,1)S(1)} %get-tuple-element.28), channel_id=1, source_target_pairs={{0,1},{1,0},{2,3},{3,2},{4,5},{5,4},{6,7},{7,6},{8,9},{9,8},{10,11... | collective-permute-start | bytes 614408 | tf_op jit(solution)/shard_map/ppermute | solution.py:33
  36.6 35.6 %collective-permute-start.1 = (bf16[8,100,128]{2,1,0:T(8,128)(2,1)S(1)}, bf16[8,100,128]{2,1,0:T(8,128)(2,1)S(1)}, u32[]{:S(2)}, u32[]{:S(2)}) collective-permute-start(bf16[8,100,128]{2,1,0:T(8,128)(2,1)S(1)} %get-tuple-element.29), channel_id=1, source_target_pairs={{0,2},{1,3},{2,0},{3,1},{4,6},{5,7},{6,4},{7,5},{8,10},{9,11},{10,... | collective-permute-start | bytes 614408 | tf_op jit(solution)/shard_map/ppermute | solution.py:33
  38.1 34.0 %collective-permute-start.2 = (bf16[8,100,128]{2,1,0:T(8,128)(2,1)S(1)}, bf16[8,100,128]{2,1,0:T(8,128)(2,1)S(1)}, u32[]{:S(2)}, u32[]{:S(2)}) collective-permute-start(bf16[8,100,128]{2,1,0:T(8,128)(2,1)S(1)} %get-tuple-element.30), channel_id=1, source_target_pairs={{0,3},{1,2},{2,1},{3,0},{4,7},{5,6},{6,5},{7,4},{8,11},{9,10},{10,... | collective-permute-start | bytes 614408 | tf_op jit(solution)/shard_map/ppermute | solution.py:33
  51.3 4.6 %collective-permute-start.7 = (f32[16,8,128]{2,1,0:T(8,128)S(1)}, f32[16,8,128]{2,1,0:T(8,128)S(1)}, u32[]{:S(2)}, u32[]{:S(2)}) collective-permute-start(f32[16,8,128]{2,1,0:T(8,128)S(1)} %get-tuple-element.37), channel_id=1, source_target_pairs={{0,4},{4,0},{8,12},{12,8},{16,20},{20,16},{24,28},{28,24},{1,5},{5... | collective-permute-start | bytes 196616 | tf_op jit(solution)/shard_map/ppermute | solution.py:33
  55.9 4.0 %collective-permute-start.8 = (f32[8,8,128]{2,1,0:T(8,128)S(1)}, f32[8,8,128]{2,1,0:T(8,128)S(1)}, u32[]{:S(2)}, u32[]{:S(2)}) collective-permute-start(f32[8,8,128]{2,1,0:T(8,128)S(1)} %get-tuple-element.39), channel_id=1, source_target_pairs={{0,8},{4,12},{8,0},{12,4},{16,24},{20,28},{24,16},{28,20},{1,9},{5... | collective-permute-start | bytes 98312 | tf_op jit(solution)/shard_map/ppermute | solution.py:33
  56.5 5.0 %collective-permute-start.9 = (f32[8,8,128]{2,1,0:T(8,128)S(1)}, f32[8,8,128]{2,1,0:T(8,128)S(1)}, u32[]{:S(2)}, u32[]{:S(2)}) collective-permute-start(f32[8,8,128]{2,1,0:T(8,128)S(1)} %get-tuple-element.40), channel_id=1, source_target_pairs={{0,16},{4,20},{8,24},{12,28},{16,0},{20,4},{24,8},{28,12},{1,17},{... | collective-permute-start | bytes 98312 | tf_op jit(solution)/shard_map/ppermute | solution.py:33
  59.9 5.7 %collective-permute-start.10 = (f32[8,8,128]{2,1,0:T(8,128)S(1)}, f32[8,8,128]{2,1,0:T(8,128)S(1)}, u32[]{:S(2)}, u32[]{:S(2)}) collective-permute-start(f32[8,8,128]{2,1,0:T(8,128)S(1)} %get-tuple-element.41), channel_id=1, source_target_pairs={{0,24},{4,28},{8,16},{12,20},{16,8},{20,12},{24,0},{28,4},{1,25},{... | collective-permute-start | bytes 98312 | tf_op jit(solution)/shard_map/ppermute | solution.py:33
  66.4 1.6 %collective-permute-start.11 = (f32[8,8,128]{2,1,0:T(8,128)S(1)}, f32[8,8,128]{2,1,0:T(8,128)S(1)}, u32[]{:S(2)}, u32[]{:S(2)}) collective-permute-start(f32[8,8,128]{2,1,0:T(8,128)S(1)} %get-tuple-element.44), channel_id=1, source_target_pairs={{0,1},{1,0},{2,3},{3,2},{4,5},{5,4},{6,7},{7,6},{8,9},{9,8},{10,11... | collective-permute-start | bytes 98312 | tf_op jit(solution)/shard_map/ppermute | solution.py:33
  66.5 4.0 %collective-permute-start.12 = (f32[8,8,128]{2,1,0:T(8,128)S(1)}, f32[8,8,128]{2,1,0:T(8,128)S(1)}, u32[]{:S(2)}, u32[]{:S(2)}) collective-permute-start(f32[8,8,128]{2,1,0:T(8,128)S(1)} %get-tuple-element.45), channel_id=1, source_target_pairs={{0,2},{1,3},{2,0},{3,1},{4,6},{5,7},{6,4},{7,5},{8,10},{9,11},{10,... | collective-permute-start | bytes 98312 | tf_op jit(solution)/shard_map/ppermute | solution.py:33
  68.1 3.4 %collective-permute-start.13 = (f32[8,8,128]{2,1,0:T(8,128)S(1)}, f32[8,8,128]{2,1,0:T(8,128)S(1)}, u32[]{:S(2)}, u32[]{:S(2)}) collective-permute-start(f32[8,8,128]{2,1,0:T(8,128)S(1)} %get-tuple-element.46), channel_id=1, source_target_pairs={{0,3},{1,2},{2,1},{3,0},{4,7},{5,6},{6,5},{7,4},{8,11},{9,10},{10,... | collective-permute-start | bytes 98312 | tf_op jit(solution)/shard_map/ppermute | solution.py:33

commit v4 on v3

--- a/solution.py
+++ b/solution.py
@@ -43,36 +43,44 @@
     return odd_wide, 1 - odd_wide, 2 + odd_narrow, 3 - odd_narrow
 
 
-def halo_kernel(coef, halo_blocks, *refs):
-    outs, sems = refs[:4], refs[4]
-    copies = []
-    for k, side in enumerate(sides()):
-        for h in range(outs[k].shape[0]):
-            at = pl.multiple_of(halo_blocks[h, side] * LANES, LANES)
-            copies.append(
-                pltpu.make_async_copy(coef.at[:, pl.ds(at, LANES)], outs[k].at[h], sems.at[k, h])
-            )
+def halo_kernel(coef, listed, *refs):
+    *outs, held, halo_blocks, sems = refs
+    copies = [
+        pltpu.make_async_copy(listed, halo_blocks, sems.at[0]),
+        pltpu.make_async_copy(coef, held, sems.at[1]),
+    ]
     for copy in copies:
         copy.start()
     for copy in copies:
         copy.wait()
+    for k, side in enumerate(sides()):
+        for h in range(outs[k].shape[0]):
+            at = pl.multiple_of(halo_blocks[h, side] * LANES, LANES)
+            outs[k][h] = held[:, pl.ds(at, LANES)]
 
 
 def halo_pack(coef, halo_blocks):
-    rows = coef.shape[0]
+    rows, elems = coef.shape
     count = halo_blocks.shape[0]
     return pl.pallas_call(
         halo_kernel,
-        out_shape=[jax.ShapeDtypeStruct((count, rows, LANES), bf16)] * 4,
-        in_specs=[HBM, SMEM],
-        out_specs=[VMEM] * 4,
-        scratch_shapes=[pltpu.SemaphoreType.DMA((4, count))],
+        out_shape=[jax.ShapeDtypeStruct((count, rows, LANES), bf16)] * 4
+        + [jax.ShapeDtypeStruct((rows, elems), bf16)],
+        in_specs=[HBM, HBM],
+        out_specs=[VMEM] * 5,
+        scratch_shapes=[
+            pltpu.SMEM(halo_blocks.shape, jnp.int32),
+            pltpu.SemaphoreType.DMA((2,)),
+        ],
         cost_estimate=pl.CostEstimate(
-            flops=0, bytes_accessed=16 * count * rows * LANES, transcendentals=0
+            flops=0, bytes_accessed=4 * rows * elems, transcendentals=0
         ),
-        compiler_params=grant(16 * count * padded_rows(rows) * LANES),
+        compiler_params=grant(4 * padded_rows(rows) * (elems + 4 * count * LANES)),
         name="halo_pack",
-    )(coef, halo_blocks)
+    )(
+        pltpu.with_memory_space_constraint(coef, pltpu.HBM),
+        pltpu.with_memory_space_constraint(halo_blocks, pltpu.HBM),
+    )
 
 
 def stats_place(t, w, per_wide, slots):
@@ -402,17 +410,17 @@
     narrow = lax.axis_size("narrow")
     rows, _ = coefficients.shape
     blocks = owner_device.shape[0]
-    sent = halo_pack(coefficients, halo_blocks[0].T)
+    *sent, held = halo_pack(coefficients, halo_blocks[0].T)
     halos = [
         far_pairs(sent[0], "wide"),
         swapped(sent[1], "wide", 1),
         far_pairs(sent[2], "narrow"),
         swapped(sent[3], "narrow", 1),
     ]
-    packed, route = pack(coefficients, owner_device, work_count, wide, narrow)
+    packed, route = pack(held, owner_device, work_count, wide, narrow)
     slots = packed.shape[0]
     arrived = lax.all_to_all(packed, "wide", 0, 0, tiled=True)
-    stats = metrics(neighbours, route, coefficients, halos, recon_weight, slots)
+    stats = metrics(neighbours, route, held, halos, recon_weight, slots)
     if len(stats) == 1:
         stats_arrived = [lax.all_to_all(stats[0], "wide", 0, 0, tiled=True)]
     else:

time: 73.5 us -> 72.8 us (level)
  local copies, waits for them, and re-layouts: 3.14 us -> 0.67 us
  waiting for transfers between devices: 25.7 us -> 27.2 us
    unnamed x14 -> x8, local copies, waits for them, and re-layouts: 3.14 us -> 0.67 us
    all_to_all x1, waiting for transfers between devices: 14.4 us -> 15.9 us  [per_device(): arrived = lax.all_to_all(packed, 'wide', 0, 0, tiled=True)]
  transfers between devices with their start and end apart: 15 -> 15, of which waited for: 7 -> 7; matrix products, arithmetic and copies ran while one was open for 0% -> 0% of each run, Pallas kernels for 23% -> 22%
where the time goes in v4:
time: 72.8 us; the launch traced here: 72.6 us
  waiting for transfers between devices  27.2 us (37%)
  starting transfers between devices  23.5 us (32%)
  Pallas kernels  20.4 us (28%)
  between operations  0.74 us (1%)
    all_to_all x1, waiting for transfers between devices, per_device(): arrived = lax.all_to_all(packed, 'wide', 0, 0, tiled=True)  15.9 us
    pallas_call x1, Pallas kernels, metrics(): pl.pallas_call(metric_kernel, out_shape=[jax.ShapeDtypeStruct((slots // p...  12.9 us
    ppermute x12, starting transfers between devices, swapped(): lax.ppermute(value, axis, [(source, source ^ flip) for source in range(co...  11.4 us
    ppermute x12, waiting for transfers between devices, swapped(): lax.ppermute(value, axis, [(source, source ^ flip) for source in range(co...  11.3 us
    all_to_all x1, starting transfers between devices, per_device(): arrived = lax.all_to_all(packed, 'wide', 0, 0, tiled=True)  7.32 us
    ppermute x2, starting transfers between devices, far_pairs(): lax.ppermute(value, axis, [(at, (at + (1 if at % 2 else -1)) % count) for...  4.81 us
    pallas_call x1, Pallas kernels, pack(): pl.pallas_call(lambda *refs: pack_kernel(wide, narrow, *refs), out_shape=...  2.08 us
    pallas_call x1, Pallas kernels, relay(): pl.pallas_call(lambda *refs: relay_kernel(narrow, *refs), out_shape=[jax....  1.6 us
  transfers between devices with their start and end apart: 15, of which 7 were waited for; matrix products, arithmetic and copies ran while one was open for 0% of the time, Pallas kernels for 22%

profile of v4, /device:TPU:0, one launch (start us, length us, event | category | flops | bytes accessed | tf_op | source)
XLA Modules:
  0.0 72.6 jit_solution(16881241392193674686)
XLA Ops:
  0.6 1.2 %halo_pack.1 = (bf16[2,100,128]{2,1,0:T(8,128)(2,1)S(1)}, bf16[2,100,128]{2,1,0:T(8,128)(2,1)S(1)}, bf16[2,100,128]{2,1,0:T(8,128)(2,1)S(1)}, bf16[2,100,128]{2,1,0:T(8,128)(2,1)S(1)}, bf16[100,4096]{1,0:T(8,128)(2,1)S(1)}) custom-call(bf16[100,4096]{1,0:T(8,128)(2,1)} %coef.1, s32[2,4]{1,0:T(2,128)} %bitcast.4), custom_call_target="tpu_custom_call" | custom-call | bytes 1638400 | tf_op jit(solution)/shard_map/halo_pack/pallas_call | solution.py:65
  1.9 0.0 copy-start
  1.9 0.0 copy-start.1
  1.9 0.6 copy-done
  2.5 0.0 copy-done.1
  2.5 2.1 %pack.1 = (bf16[32,104,128]{2,1,0:T(8,128)(2,1)}, s32[2,32]{1,0:T(2,128)S(1)}) custom-call(bf16[100,4096]{1,0:T(8,128)(2,1)S(1)} %get-tuple-element.27.refs_0_.coef, s32[32]{0:T(128)S(1)} %copy-done, s32[32]{0:T(128)S(1)} %copy-done.1), custom_call_target="tpu_custom_call" | custom-call | bytes 1638400 | tf_op jit(solution)/shard_map/pack/pallas_call | solution.py:122
  4.6 7.3 %all-to-all-start = ((bf16[32,104,128]{2,1,0:T(8,128)(2,1)}), bf16[32,104,128]{2,1,0:T(8,128)(2,1)S(1)}, u32[]{:S(2)}, u32[]{:S(2)}) async-start(bf16[32,104,128]{2,1,0:T(8,128)(2,1)} %get-tuple-element.28), calls=%async_computation | async-start | bytes 1703936 | tf_op jit(solution)/shard_map/all_to_all | solution.py:422
  12.0 4.7 %collective-permute-start.3 = (bf16[2,100,128]{2,1,0:T(8,128)(2,1)S(1)}, bf16[2,100,128]{2,1,0:T(8,128)(2,1)S(1)}, u32[]{:S(2)}, u32[]{:S(2)}) collective-permute-start(bf16[2,100,128]{2,1,0:T(8,128)(2,1)S(1)} %get-tuple-element.34), channel_id=1, source_target_pairs={{0,28},{4,8},{8,4},{12,16},{16,12},{20,24},{24,20},{28,0},{1,29},{... | collective-permute-start | bytes 153608 | tf_op jit(solution)/shard_map/ppermute | solution.py:26
  16.7 0.1 collective-permute-start.5
  16.8 1.5 %collective-permute-start.6 = (bf16[2,100,128]{2,1,0:T(8,128)(2,1)S(1)}, bf16[2,100,128]{2,1,0:T(8,128)(2,1)S(1)}, u32[]{:S(2)}, u32[]{:S(2)}) collective-permute-start(bf16[2,100,128]{2,1,0:T(8,128)(2,1)S(1)} %get-tuple-element.37), channel_id=1, source_target_pairs={{0,1},{1,0},{2,3},{3,2},{4,5},{5,4},{6,7},{7,6},{8,9},{9,8},{10,11... | collective-permute-start | bytes 153608 | tf_op jit(solution)/shard_map/ppermute | solution.py:33
  18.3 15.9 %all-to-all-done.refs_0_ = bf16[32,104,128]{2,1,0:T(8,128)(2,1)S(1)} async-done(((bf16[32,104,128]{2,1,0:T(8,128)(2,1)}), bf16[32,104,128]{2,1,0:T(8,128)(2,1)S(1)}, u32[]{:S(2)}, u32[]{:S(2)}) %all-to-all-start) | async-done | bytes 852000 | tf_op jit(solution)/shard_map/all_to_all | solution.py:422
  34.2 1.6 %relay.1 = (bf16[8,100,128]{2,1,0:T(8,128)(2,1)S(1)}, bf16[8,100,128]{2,1,0:T(8,128)(2,1)S(1)}, bf16[8,100,128]{2,1,0:T(8,128)(2,1)S(1)}, bf16[8,100,128]{2,1,0:T(8,128)(2,1)S(1)}, s32[64]{0:T(128)S(1)}) custom-call(bf16[32,104,128]{2,1,0:T(8,128)(2,1)S(1)} %all-to-all-done.refs_0_), custom_call_target="tpu_custom_call" | custom-call | bytes 1638400 | tf_op jit(solution)/shard_map/relay/pallas_call | solution.py:282
  35.8 0.1 collective-permute-start
  35.9 1.6 %collective-permute-start.1 = (bf16[8,100,128]{2,1,0:T(8,128)(2,1)S(1)}, bf16[8,100,128]{2,1,0:T(8,128)(2,1)S(1)}, u32[]{:S(2)}, u32[]{:S(2)}) collective-permute-start(bf16[8,100,128]{2,1,0:T(8,128)(2,1)S(1)} %get-tuple-element.31), channel_id=1, source_target_pairs={{0,2},{1,3},{2,0},{3,1},{4,6},{5,7},{6,4},{7,5},{8,10},{9,11},{10,... | collective-permute-start | bytes 614408 | tf_op jit(solution)/shard_map/ppermute | solution.py:33
  37.4 0.3 collective-permute-start.2
  37.7 12.9 %metric.1 = (f32[16,8,128]{2,1,0:T(8,128)S(1)}, f32[16,8,128]{2,1,0:T(8,128)S(1)}) custom-call(s32[4,4096]{1,0:T(4,128)S(1)} %copy-done.3, s32[2,32]{1,0:T(2,128)S(1)} %get-tuple-element.33.routes, bf16[100,4096]{1,0:T(8,128)(2,1)S(1)} %get-tuple-element.27.refs_0_.coef, bf16[2,100,128]{2,1,0:T(8,128)(2,1)S(1)} %collective-permute-done.3.h0, ...), custom_call_target="tpu_custom_call" | custom-call | flops 671088640 | bytes 10485760 | tf_op jit(solution)/shard_map/metric/pallas_call | solution.py:233
  50.6 2.0 %collective-permute-start.7 = (f32[16,8,128]{2,1,0:T(8,128)S(1)}, f32[16,8,128]{2,1,0:T(8,128)S(1)}, u32[]{:S(2)}, u32[]{:S(2)}) collective-permute-start(f32[16,8,128]{2,1,0:T(8,128)S(1)} %get-tuple-element.39), channel_id=1, source_target_pairs={{0,4},{4,0},{8,12},{12,8},{16,20},{20,16},{24,28},{28,24},{1,5},{5... | collective-permute-start | bytes 196616 | tf_op jit(solution)/shard_map/ppermute | solution.py:33
  52.6 2.6 %collective-permute-done.7.got = f32[16,8,128]{2,1,0:T(8,128)S(1)} collective-permute-done((f32[16,8,128]{2,1,0:T(8,128)S(1)}, f32[16,8,128]{2,1,0:T(8,128)S(1)}, u32[]{:S(2)}, u32[]{:S(2)}) %collective-permute-start.7) | collective-permute-done | bytes 65568 | tf_op jit(solution)/shard_map/ppermute | solution.py:33
  55.2 0.5 collective-permute-start.8
  55.8 1.6 %collective-permute-start.9 = (f32[8,8,128]{2,1,0:T(8,128)S(1)}, f32[8,8,128]{2,1,0:T(8,128)S(1)}, u32[]{:S(2)}, u32[]{:S(2)}) collective-permute-start(f32[8,8,128]{2,1,0:T(8,128)S(1)} %get-tuple-element.42), channel_id=1, source_target_pairs={{0,16},{4,20},{8,24},{12,28},{16,0},{20,4},{24,8},{28,12},{1,17},{... | collective-permute-start | bytes 98312 | tf_op jit(solution)/shard_map/ppermute | solution.py:33
  57.3 1.9 %collective-permute-done.8.refs_1_ = f32[8,8,128]{2,1,0:T(8,128)S(1)} collective-permute-done((f32[8,8,128]{2,1,0:T(8,128)S(1)}, f32[8,8,128]{2,1,0:T(8,128)S(1)}, u32[]{:S(2)}, u32[]{:S(2)}) %collective-permute-start.8) | collective-permute-done | bytes 32800 | tf_op jit(solution)/shard_map/ppermute | solution.py:33
  59.2 1.4 %collective-permute-start.10 = (f32[8,8,128]{2,1,0:T(8,128)S(1)}, f32[8,8,128]{2,1,0:T(8,128)S(1)}, u32[]{:S(2)}, u32[]{:S(2)}) collective-permute-start(f32[8,8,128]{2,1,0:T(8,128)S(1)} %get-tuple-element.43), channel_id=1, source_target_pairs={{0,24},{4,28},{8,16},{12,20},{16,8},{20,12},{24,0},{28,4},{1,25},{... | collective-permute-start | bytes 98312 | tf_op jit(solution)/shard_map/ppermute | solution.py:33
  60.7 0.1 collective-permute-done.9.refs_2_
  60.8 4.2 %collective-permute-done.10.refs_3_ = f32[8,8,128]{2,1,0:T(8,128)S(1)} collective-permute-done((f32[8,8,128]{2,1,0:T(8,128)S(1)}, f32[8,8,128]{2,1,0:T(8,128)S(1)}, u32[]{:S(2)}, u32[]{:S(2)}) %collective-permute-start.10) | collective-permute-done | bytes 32800 | tf_op jit(solution)/shard_map/ppermute | solution.py:33
  65.0 0.8 %relay_stats.1 = (f32[8,8,128]{2,1,0:T(8,128)S(1)}, f32[8,8,128]{2,1,0:T(8,128)S(1)}, f32[8,8,128]{2,1,0:T(8,128)S(1)}, f32[8,8,128]{2,1,0:T(8,128)S(1)}) custom-call(f32[8,8,128]{2,1,0:T(8,128)S(1)} %get-tuple-element.40.refs_0_, f32[8,8,128]{2,1,0:T(8,128)S(1)} %collective-permute-done.8.refs_1_, f32[8,8,128]{2,1,0:T(8,128)S(1)} %collective-permute-done.9.refs_2_, ...), custom_call_target="tpu_custom_call" | custom-call | bytes 262144 | tf_op jit(solution)/shard_map/relay_stats/pallas_call | solution.py:346
  65.7 0.1 collective-permute-start.11
  65.8 1.5 %collective-permute-start.12 = (f32[8,8,128]{2,1,0:T(8,128)S(1)}, f32[8,8,128]{2,1,0:T(8,128)S(1)}, u32[]{:S(2)}, u32[]{:S(2)}) collective-permute-start(f32[8,8,128]{2,1,0:T(8,128)S(1)} %get-tuple-element.47), channel_id=1, source_target_pairs={{0,2},{1,3},{2,0},{3,1},{4,6},{5,7},{6,4},{7,5},{8,10},{9,11},{10,... | collective-permute-start | bytes 98312 | tf_op jit(solution)/shard_map/ppermute | solution.py:33
  67.4 0.9 %collective-permute-start.13 = (f32[8,8,128]{2,1,0:T(8,128)S(1)}, f32[8,8,128]{2,1,0:T(8,128)S(1)}, u32[]{:S(2)}, u32[]{:S(2)}) collective-permute-start(f32[8,8,128]{2,1,0:T(8,128)S(1)} %get-tuple-element.48), channel_id=1, source_target_pairs={{0,3},{1,2},{2,1},{3,0},{4,7},{5,6},{6,5},{7,4},{8,11},{9,10},{10,... | collective-permute-start | bytes 98312 | tf_op jit(solution)/shard_map/ppermute | solution.py:33
  68.3 1.5 %collective-permute-done.12.refs_2_ = f32[8,8,128]{2,1,0:T(8,128)S(1)} collective-permute-done((f32[8,8,128]{2,1,0:T(8,128)S(1)}, f32[8,8,128]{2,1,0:T(8,128)S(1)}, u32[]{:S(2)}, u32[]{:S(2)}) %collective-permute-start.12) | collective-permute-done | bytes 32800 | tf_op jit(solution)/shard_map/ppermute | solution.py:33
  69.8 0.9 %collective-permute-done.13.refs_3_ = f32[8,8,128]{2,1,0:T(8,128)S(1)} collective-permute-done((f32[8,8,128]{2,1,0:T(8,128)S(1)}, f32[8,8,128]{2,1,0:T(8,128)S(1)}, u32[]{:S(2)}, u32[]{:S(2)}) %collective-permute-start.13) | collective-permute-done | bytes 32800 | tf_op jit(solution)/shard_map/ppermute | solution.py:33
  70.7 0.7 place_stats.1
  71.4 1.1 %place.1 = bf16[100,4096]{1,0:T(8,128)(2,1)} custom-call(bf16[8,100,128]{2,1,0:T(8,128)(2,1)S(1)} %get-tuple-element.29.refs_0_, bf16[8,100,128]{2,1,0:T(8,128)(2,1)S(1)} %collective-permute-done.refs_1_, bf16[8,100,128]{2,1,0:T(8,128)(2,1)S(1)} %collective-permute-done.1.refs_2_, bf16[8,100,128]{2,1,0:T(8,128)(2,1)S(1)} %collective-permute-done.2.refs_3_), custom_call_target="tpu_custom_call" | custom-call | tf_op jit(solution)/shard_map/place/pallas_call | solution.py:370
  (14 shorter events, 0.0 us)
Async XLA Ops:
  1.9 0.7 copy-start
  1.9 0.7 copy-start.1
  4.6 29.5 %all-to-all-start = ((bf16[32,104,128]{2,1,0:T(8,128)(2,1)}), bf16[32,104,128]{2,1,0:T(8,128)(2,1)S(1)}, u32[]{:S(2)}, u32[]{:S(2)}) async-start(bf16[32,104,128]{2,1,0:T(8,128)(2,1)} %get-tuple-element.28), calls=%async_computation | async-start | bytes 1703936 | tf_op jit(solution)/shard_map/all_to_all | solution.py:422
  12.0 23.9 %collective-permute-start.3 = (bf16[2,100,128]{2,1,0:T(8,128)(2,1)S(1)}, bf16[2,100,128]{2,1,0:T(8,128)(2,1)S(1)}, u32[]{:S(2)}, u32[]{:S(2)}) collective-permute-start(bf16[2,100,128]{2,1,0:T(8,128)(2,1)S(1)} %get-tuple-element.34), channel_id=1, source_target_pairs={{0,28},{4,8},{8,4},{12,16},{16,12},{20,24},{24,20},{28,0},{1,29},{... | collective-permute-start | bytes 153608 | tf_op jit(solution)/shard_map/ppermute | solution.py:26
  16.7 20.7 %collective-permute-start.4 = (bf16[2,100,128]{2,1,0:T(8,128)(2,1)S(1)}, bf16[2,100,128]{2,1,0:T(8,128)(2,1)S(1)}, u32[]{:S(2)}, u32[]{:S(2)}) collective-permute-start(bf16[2,100,128]{2,1,0:T(8,128)(2,1)S(1)} %get-tuple-element.35), channel_id=1, source_target_pairs={{0,4},{4,0},{8,12},{12,8},{16,20},{20,16},{24,28},{28,24},{1,5},{5... | collective-permute-start | bytes 153608 | tf_op jit(solution)/shard_map/ppermute | solution.py:33
  16.7 21.0 %collective-permute-start.5 = (bf16[2,100,128]{2,1,0:T(8,128)(2,1)S(1)}, bf16[2,100,128]{2,1,0:T(8,128)(2,1)S(1)}, u32[]{:S(2)}, u32[]{:S(2)}) collective-permute-start(bf16[2,100,128]{2,1,0:T(8,128)(2,1)S(1)} %get-tuple-element.36), channel_id=1, source_target_pairs={{0,3},{1,2},{2,1},{3,0},{4,7},{5,6},{6,5},{7,4},{8,11},{9,10},{10,... | collective-permute-start | bytes 153608 | tf_op jit(solution)/shard_map/ppermute | solution.py:26
  16.8 20.9 %copy-start.2 = (bf16[5,75,100]{2,1,0:T(8,128)(2,1)S(1)}, bf16[5,75,100]{2,1,0:T(8,128)(2,1)}, u32[]{:S(2)}) copy-start(bf16[5,75,100]{2,1,0:T(8,128)(2,1)} %w.1) | copy-start | bytes 225004
  16.8 21.0 %copy-start.3 = (s32[4,4096]{1,0:T(4,128)S(1)}, s32[4,4096]{1,0:T(4,128)}, u32[]{:S(2)}) copy-start(s32[4,4096]{1,0:T(4,128)} %nb.1) | copy-start | bytes 196612
  16.8 20.9 %collective-permute-start.6 = (bf16[2,100,128]{2,1,0:T(8,128)(2,1)S(1)}, bf16[2,100,128]{2,1,0:T(8,128)(2,1)S(1)}, u32[]{:S(2)}, u32[]{:S(2)}) collective-permute-start(bf16[2,100,128]{2,1,0:T(8,128)(2,1)S(1)} %get-tuple-element.37), channel_id=1, source_target_pairs={{0,1},{1,0},{2,3},{3,2},{4,5},{5,4},{6,7},{7,6},{8,9},{9,8},{10,11... | collective-permute-start | bytes 153608 | tf_op jit(solution)/shard_map/ppermute | solution.py:33
  35.8 35.7 %collective-permute-start = (bf16[8,100,128]{2,1,0:T(8,128)(2,1)S(1)}, bf16[8,100,128]{2,1,0:T(8,128)(2,1)S(1)}, u32[]{:S(2)}, u32[]{:S(2)}) collective-permute-start(bf16[8,100,128]{2,1,0:T(8,128)(2,1)S(1)} %get-tuple-element.30), channel_id=1, source_target_pairs={{0,1},{1,0},{2,3},{3,2},{4,5},{5,4},{6,7},{7,6},{8,9},{9,8},{10,11... | collective-permute-start | bytes 614408 | tf_op jit(solution)/shard_map/ppermute | solution.py:33
  35.9 35.6 %collective-permute-start.1 = (bf16[8,100,128]{2,1,0:T(8,128)(2,1)S(1)}, bf16[8,100,128]{2,1,0:T(8,128)(2,1)S(1)}, u32[]{:S(2)}, u32[]{:S(2)}) collective-permute-start(bf16[8,100,128]{2,1,0:T(8,128)(2,1)S(1)} %get-tuple-element.31), channel_id=1, source_target_pairs={{0,2},{1,3},{2,0},{3,1},{4,6},{5,7},{6,4},{7,5},{8,10},{9,11},{10,... | collective-permute-start | bytes 614408 | tf_op jit(solution)/shard_map/ppermute | solution.py:33
  37.4 34.0 %collective-permute-start.2 = (bf16[8,100,128]{2,1,0:T(8,128)(2,1)S(1)}, bf16[8,100,128]{2,1,0:T(8,128)(2,1)S(1)}, u32[]{:S(2)}, u32[]{:S(2)}) collective-permute-start(bf16[8,100,128]{2,1,0:T(8,128)(2,1)S(1)} %get-tuple-element.32), channel_id=1, source_target_pairs={{0,3},{1,2},{2,1},{3,0},{4,7},{5,6},{6,5},{7,4},{8,11},{9,10},{10,... | collective-permute-start | bytes 614408 | tf_op jit(solution)/shard_map/ppermute | solution.py:33
  50.6 4.6 %collective-permute-start.7 = (f32[16,8,128]{2,1,0:T(8,128)S(1)}, f32[16,8,128]{2,1,0:T(8,128)S(1)}, u32[]{:S(2)}, u32[]{:S(2)}) collective-permute-start(f32[16,8,128]{2,1,0:T(8,128)S(1)} %get-tuple-element.39), channel_id=1, source_target_pairs={{0,4},{4,0},{8,12},{12,8},{16,20},{20,16},{24,28},{28,24},{1,5},{5... | collective-permute-start | bytes 196616 | tf_op jit(solution)/shard_map/ppermute | solution.py:33
  55.2 4.0 %collective-permute-start.8 = (f32[8,8,128]{2,1,0:T(8,128)S(1)}, f32[8,8,128]{2,1,0:T(8,128)S(1)}, u32[]{:S(2)}, u32[]{:S(2)}) collective-permute-start(f32[8,8,128]{2,1,0:T(8,128)S(1)} %get-tuple-element.41), channel_id=1, source_target_pairs={{0,8},{4,12},{8,0},{12,4},{16,24},{20,28},{24,16},{28,20},{1,9},{5... | collective-permute-start | bytes 98312 | tf_op jit(solution)/shard_map/ppermute | solution.py:33
  55.8 5.0 %collective-permute-start.9 = (f32[8,8,128]{2,1,0:T(8,128)S(1)}, f32[8,8,128]{2,1,0:T(8,128)S(1)}, u32[]{:S(2)}, u32[]{:S(2)}) collective-permute-start(f32[8,8,128]{2,1,0:T(8,128)S(1)} %get-tuple-element.42), channel_id=1, source_target_pairs={{0,16},{4,20},{8,24},{12,28},{16,0},{20,4},{24,8},{28,12},{1,17},{... | collective-permute-start | bytes 98312 | tf_op jit(solution)/shard_map/ppermute | solution.py:33
  59.2 5.7 %collective-permute-start.10 = (f32[8,8,128]{2,1,0:T(8,128)S(1)}, f32[8,8,128]{2,1,0:T(8,128)S(1)}, u32[]{:S(2)}, u32[]{:S(2)}) collective-permute-start(f32[8,8,128]{2,1,0:T(8,128)S(1)} %get-tuple-element.43), channel_id=1, source_target_pairs={{0,24},{4,28},{8,16},{12,20},{16,8},{20,12},{24,0},{28,4},{1,25},{... | collective-permute-start | bytes 98312 | tf_op jit(solution)/shard_map/ppermute | solution.py:33
  65.7 1.6 %collective-permute-start.11 = (f32[8,8,128]{2,1,0:T(8,128)S(1)}, f32[8,8,128]{2,1,0:T(8,128)S(1)}, u32[]{:S(2)}, u32[]{:S(2)}) collective-permute-start(f32[8,8,128]{2,1,0:T(8,128)S(1)} %get-tuple-element.46), channel_id=1, source_target_pairs={{0,1},{1,0},{2,3},{3,2},{4,5},{5,4},{6,7},{7,6},{8,9},{9,8},{10,11... | collective-permute-start | bytes 98312 | tf_op jit(solution)/shard_map/ppermute | solution.py:33
  65.8 4.0 %collective-permute-start.12 = (f32[8,8,128]{2,1,0:T(8,128)S(1)}, f32[8,8,128]{2,1,0:T(8,128)S(1)}, u32[]{:S(2)}, u32[]{:S(2)}) collective-permute-start(f32[8,8,128]{2,1,0:T(8,128)S(1)} %get-tuple-element.47), channel_id=1, source_target_pairs={{0,2},{1,3},{2,0},{3,1},{4,6},{5,7},{6,4},{7,5},{8,10},{9,11},{10,... | collective-permute-start | bytes 98312 | tf_op jit(solution)/shard_map/ppermute | solution.py:33
  67.4 3.4 %collective-permute-start.13 = (f32[8,8,128]{2,1,0:T(8,128)S(1)}, f32[8,8,128]{2,1,0:T(8,128)S(1)}, u32[]{:S(2)}, u32[]{:S(2)}) collective-permute-start(f32[8,8,128]{2,1,0:T(8,128)S(1)} %get-tuple-element.48), channel_id=1, source_target_pairs={{0,3},{1,2},{2,1},{3,0},{4,7},{5,6},{6,5},{7,4},{8,11},{9,10},{10,... | collective-permute-start | bytes 98312 | tf_op jit(solution)/shard_map/ppermute | solution.py:33

commit v5 on v4

--- a/solution.py
+++ b/solution.py
@@ -37,9 +37,38 @@
     return (rows // 8 + 1) * 8
 
 
+def split(value, size):
+    if size & (size - 1) == 0:
+        return value >> (size.bit_length() - 1), value & (size - 1)
+    return lax.div(value, size), lax.rem(value, size)
+
+
+class Counters:
+    def __init__(self, labels, largest, memory):
+        self.packed = labels * 4 <= 32 and largest < 8
+        self.counts = jnp.int32(0)
+        self.memory = memory
+        if not self.packed:
+
+            def clear(w, _):
+                memory[w] = 0
+                return 0
+
+            lax.fori_loop(0, labels, clear, 0)
+
+    def next(self, label):
+        if self.packed:
+            seen = (self.counts >> (4 * label)) & 15
+            self.counts = self.counts + (jnp.int32(1) << (4 * label))
+        else:
+            seen = self.memory[label]
+            self.memory[label] = seen + 1
+        return seen
+
+
 def sides():
-    odd_wide = lax.axis_index("wide") % 2
-    odd_narrow = lax.axis_index("narrow") % 2
+    odd_wide = lax.axis_index("wide") & 1
+    odd_narrow = lax.axis_index("narrow") & 1
     return odd_wide, 1 - odd_wide, 2 + odd_narrow, 3 - odd_narrow
 
 
@@ -83,9 +112,9 @@
     )
 
 
-def stats_place(t, w, per_wide, slots):
-    away = (w ^ lax.axis_index("wide")) % 2
-    return away * (slots // 2) + (w // 2) * per_wide + t % per_wide
+def stats_place(w, rank, per_wide, slots):
+    away = (w ^ lax.axis_index("wide")) & 1
+    return away * (slots // 2) + (w >> 1) * per_wide + rank
 
 
 def pack_kernel(wide, narrow, coef, owner, count, packed, route, filled):
@@ -94,25 +123,18 @@
     blocks = owner.shape[0]
     per_wide = slots // wide
 
-    def clear(w, _):
-        filled[w] = 0
-        return 0
-
-    lax.fori_loop(0, wide, clear, 0)
     if slots > blocks:
         for t in range(slots):
             packed[t, rows:tall, :] = jnp.full((tall - rows, LANES), -1, bf16)
+    counters = Counters(wide, per_wide, filled)
     for b in range(blocks):
-        target = owner[b]
-        w = target // narrow
-        t = w * per_wide + filled[w]
-        filled[w] = filled[w] + 1
-        route[0, b] = stats_place(t, w, per_wide, slots) if slots == blocks else t
+        w, target = split(owner[b], narrow)
+        rank = counters.next(w)
+        t = w * per_wide + rank
+        route[0, b] = stats_place(w, rank, per_wide, slots) if slots == blocks else t
         route[1, b] = count[b]
         packed[t, 0:rows, :] = coef[:, b * LANES : (b + 1) * LANES]
-        packed[t, rows:tall, :] = jnp.full((tall - rows, LANES), (target % narrow).astype(f32)).astype(
-            bf16
-        )
+        packed[t, rows:tall, :] = jnp.full((tall - rows, LANES), target.astype(f32)).astype(bf16)
 
 
 def pack(coef, owner, count, wide, narrow):
@@ -262,14 +284,22 @@
     copy = pltpu.make_async_copy(words, tags, sem)
     copy.start()
     copy.wait()
-    for c in range(narrow + 1):
-        filled[c] = c * per
-    for t in range(slots):
-        tag = tags[t, 0]
-        c = jnp.where(tag < 0, narrow, tag)
-        at = filled[c]
-        order[at] = t
-        filled[c] = at + 1
+    blocks = narrow * per
+    if slots == blocks and per <= 8:
+        counts = jnp.int32(0)
+        for t in range(slots):
+            c = tags[t, 0]
+            order[c * per + ((counts >> (4 * c)) & 15)] = t
+            counts = counts + (jnp.int32(1) << (4 * c))
+    else:
+        for c in range(narrow + 1):
+            filled[c] = c * per
+        for t in range(slots):
+            tag = tags[t, 0]
+            c = jnp.where(tag < 0, narrow, tag)
+            at = filled[c]
+            order[at] = t
+            filled[c] = at + 1
     mine = lax.axis_index("narrow")
     for k in range(narrow):
         for j in range(per):
@@ -302,7 +332,7 @@
 
 def merge_kernel(kept, got, *sends):
     per = sends[0].shape[0] // 2
-    mine = lax.axis_index("wide") // 2
+    mine = lax.axis_index("wide") >> 1
     for j, send in enumerate(sends):
         at = (mine ^ j) * per
         for i in range(per):
@@ -336,7 +366,8 @@
         for j in range(per):
             t = order[(mine ^ k) * per + j]
             if len(parts) > 1:
-                t = ((t // per_wide) ^ wide) * per_wide + t % per_wide
+                at, rank = split(t, per_wide)
+                t = (at ^ wide) * per_wide + rank
             sends[k][j] = held[t]
 
 

time: 72.8 us -> 72.3 us (level)
  no operation moved by 1% of the time
where the time goes in v5:
time: 72.3 us; the launch traced here: 72.1 us
  waiting for transfers between devices  27.2 us (38%)
  starting transfers between devices  23.6 us (33%)
  Pallas kernels  19.9 us (28%)
  between operations  0.74 us (1%)
    all_to_all x1, waiting for transfers between devices, per_device(): arrived = lax.all_to_all(packed, 'wide', 0, 0, tiled=True)  15.9 us
    pallas_call x1, Pallas kernels, metrics(): pl.pallas_call(metric_kernel, out_shape=[jax.ShapeDtypeStruct((slots // p...  12.9 us
    ppermute x12, starting transfers between devices, swapped(): lax.ppermute(value, axis, [(source, source ^ flip) for source in range(co...  11.4 us
    ppermute x12, waiting for transfers between devices, swapped(): lax.ppermute(value, axis, [(source, source ^ flip) for source in range(co...  11.3 us
    all_to_all x1, starting transfers between devices, per_device(): arrived = lax.all_to_all(packed, 'wide', 0, 0, tiled=True)  7.32 us
    ppermute x2, starting transfers between devices, far_pairs(): lax.ppermute(value, axis, [(at, (at + (1 if at % 2 else -1)) % count) for...  4.81 us
    pallas_call x1, Pallas kernels, pack(): pl.pallas_call(lambda *refs: pack_kernel(wide, narrow, *refs), out_shape=...  1.82 us
    pallas_call x1, Pallas kernels, relay(): pl.pallas_call(lambda *refs: relay_kernel(narrow, *refs), out_shape=[jax....  1.52 us
  transfers between devices with their start and end apart: 15, of which 7 were waited for; matrix products, arithmetic and copies ran while one was open for 0% of the time, Pallas kernels for 22%

profile of v5, /device:TPU:0, one launch (start us, length us, event | category | flops | bytes accessed | tf_op | source)
XLA Modules:
  0.0 72.1 jit_solution(15031853535990661018)
XLA Ops:
  0.6 1.2 %halo_pack.1 = (bf16[2,100,128]{2,1,0:T(8,128)(2,1)S(1)}, bf16[2,100,128]{2,1,0:T(8,128)(2,1)S(1)}, bf16[2,100,128]{2,1,0:T(8,128)(2,1)S(1)}, bf16[2,100,128]{2,1,0:T(8,128)(2,1)S(1)}, bf16[100,4096]{1,0:T(8,128)(2,1)S(1)}) custom-call(bf16[100,4096]{1,0:T(8,128)(2,1)} %coef.1, s32[2,4]{1,0:T(2,128)} %bitcast.4), custom_call_target="tpu_custom_call" | custom-call | bytes 1638400 | tf_op jit(solution)/shard_map/halo_pack/pallas_call | solution.py:94
  1.9 0.0 copy-start
  1.9 0.0 copy-start.1
  1.9 0.6 copy-done
  2.5 0.0 copy-done.1
  2.5 1.8 %pack.1 = (bf16[32,104,128]{2,1,0:T(8,128)(2,1)}, s32[2,32]{1,0:T(2,128)S(1)}) custom-call(bf16[100,4096]{1,0:T(8,128)(2,1)S(1)} %get-tuple-element.27.refs_0_.coef, s32[32]{0:T(128)S(1)} %copy-done, s32[32]{0:T(128)S(1)} %copy-done.1), custom_call_target="tpu_custom_call" | custom-call | bytes 1638400 | tf_op jit(solution)/shard_map/pack/pallas_call | solution.py:144
  4.4 7.3 %all-to-all-start = ((bf16[32,104,128]{2,1,0:T(8,128)(2,1)}), bf16[32,104,128]{2,1,0:T(8,128)(2,1)S(1)}, u32[]{:S(2)}, u32[]{:S(2)}) async-start(bf16[32,104,128]{2,1,0:T(8,128)(2,1)} %get-tuple-element.28), calls=%async_computation | async-start | bytes 1703936 | tf_op jit(solution)/shard_map/all_to_all | solution.py:453
  11.7 4.7 %collective-permute-start.3 = (bf16[2,100,128]{2,1,0:T(8,128)(2,1)S(1)}, bf16[2,100,128]{2,1,0:T(8,128)(2,1)S(1)}, u32[]{:S(2)}, u32[]{:S(2)}) collective-permute-start(bf16[2,100,128]{2,1,0:T(8,128)(2,1)S(1)} %get-tuple-element.34), channel_id=1, source_target_pairs={{0,28},{4,8},{8,4},{12,16},{16,12},{20,24},{24,20},{28,0},{1,29},{... | collective-permute-start | bytes 153608 | tf_op jit(solution)/shard_map/ppermute | solution.py:26
  16.4 0.1 collective-permute-start.5
  16.5 1.5 %collective-permute-start.6 = (bf16[2,100,128]{2,1,0:T(8,128)(2,1)S(1)}, bf16[2,100,128]{2,1,0:T(8,128)(2,1)S(1)}, u32[]{:S(2)}, u32[]{:S(2)}) collective-permute-start(bf16[2,100,128]{2,1,0:T(8,128)(2,1)S(1)} %get-tuple-element.37), channel_id=1, source_target_pairs={{0,1},{1,0},{2,3},{3,2},{4,5},{5,4},{6,7},{7,6},{8,9},{9,8},{10,11... | collective-permute-start | bytes 153608 | tf_op jit(solution)/shard_map/ppermute | solution.py:33
  18.0 15.9 %all-to-all-done.refs_0_ = bf16[32,104,128]{2,1,0:T(8,128)(2,1)S(1)} async-done(((bf16[32,104,128]{2,1,0:T(8,128)(2,1)}), bf16[32,104,128]{2,1,0:T(8,128)(2,1)S(1)}, u32[]{:S(2)}, u32[]{:S(2)}) %all-to-all-start) | async-done | bytes 852000 | tf_op jit(solution)/shard_map/all_to_all | solution.py:453
  33.9 1.5 %relay.1 = (bf16[8,100,128]{2,1,0:T(8,128)(2,1)S(1)}, bf16[8,100,128]{2,1,0:T(8,128)(2,1)S(1)}, bf16[8,100,128]{2,1,0:T(8,128)(2,1)S(1)}, bf16[8,100,128]{2,1,0:T(8,128)(2,1)S(1)}, s32[64]{0:T(128)S(1)}) custom-call(bf16[32,104,128]{2,1,0:T(8,128)(2,1)S(1)} %all-to-all-done.refs_0_), custom_call_target="tpu_custom_call" | custom-call | bytes 1638400 | tf_op jit(solution)/shard_map/relay/pallas_call | solution.py:312
  35.4 0.1 collective-permute-start
  35.5 1.6 %collective-permute-start.1 = (bf16[8,100,128]{2,1,0:T(8,128)(2,1)S(1)}, bf16[8,100,128]{2,1,0:T(8,128)(2,1)S(1)}, u32[]{:S(2)}, u32[]{:S(2)}) collective-permute-start(bf16[8,100,128]{2,1,0:T(8,128)(2,1)S(1)} %get-tuple-element.31), channel_id=1, source_target_pairs={{0,2},{1,3},{2,0},{3,1},{4,6},{5,7},{6,4},{7,5},{8,10},{9,11},{10,... | collective-permute-start | bytes 614408 | tf_op jit(solution)/shard_map/ppermute | solution.py:33
  37.1 0.3 collective-permute-start.2
  37.4 12.9 %metric.1 = (f32[16,8,128]{2,1,0:T(8,128)S(1)}, f32[16,8,128]{2,1,0:T(8,128)S(1)}) custom-call(s32[4,4096]{1,0:T(4,128)S(1)} %copy-done.3, s32[2,32]{1,0:T(2,128)S(1)} %get-tuple-element.33.routes, bf16[100,4096]{1,0:T(8,128)(2,1)S(1)} %get-tuple-element.27.refs_0_.coef, bf16[2,100,128]{2,1,0:T(8,128)(2,1)S(1)} %collective-permute-done.3.h0, ...), custom_call_target="tpu_custom_call" | custom-call | flops 671088640 | bytes 10485760 | tf_op jit(solution)/shard_map/metric/pallas_call | solution.py:255
  50.3 2.0 %collective-permute-start.7 = (f32[16,8,128]{2,1,0:T(8,128)S(1)}, f32[16,8,128]{2,1,0:T(8,128)S(1)}, u32[]{:S(2)}, u32[]{:S(2)}) collective-permute-start(f32[16,8,128]{2,1,0:T(8,128)S(1)} %get-tuple-element.39), channel_id=1, source_target_pairs={{0,4},{4,0},{8,12},{12,8},{16,20},{20,16},{24,28},{28,24},{1,5},{5... | collective-permute-start | bytes 196616 | tf_op jit(solution)/shard_map/ppermute | solution.py:33
  52.3 2.6 %collective-permute-done.7.got = f32[16,8,128]{2,1,0:T(8,128)S(1)} collective-permute-done((f32[16,8,128]{2,1,0:T(8,128)S(1)}, f32[16,8,128]{2,1,0:T(8,128)S(1)}, u32[]{:S(2)}, u32[]{:S(2)}) %collective-permute-start.7) | collective-permute-done | bytes 65568 | tf_op jit(solution)/shard_map/ppermute | solution.py:33
  54.9 0.5 collective-permute-start.8
  55.4 1.6 %collective-permute-start.9 = (f32[8,8,128]{2,1,0:T(8,128)S(1)}, f32[8,8,128]{2,1,0:T(8,128)S(1)}, u32[]{:S(2)}, u32[]{:S(2)}) collective-permute-start(f32[8,8,128]{2,1,0:T(8,128)S(1)} %get-tuple-element.42), channel_id=1, source_target_pairs={{0,16},{4,20},{8,24},{12,28},{16,0},{20,4},{24,8},{28,12},{1,17},{... | collective-permute-start | bytes 98312 | tf_op jit(solution)/shard_map/ppermute | solution.py:33
  57.0 1.9 %collective-permute-done.8.refs_1_ = f32[8,8,128]{2,1,0:T(8,128)S(1)} collective-permute-done((f32[8,8,128]{2,1,0:T(8,128)S(1)}, f32[8,8,128]{2,1,0:T(8,128)S(1)}, u32[]{:S(2)}, u32[]{:S(2)}) %collective-permute-start.8) | collective-permute-done | bytes 32800 | tf_op jit(solution)/shard_map/ppermute | solution.py:33
  58.9 1.4 %collective-permute-start.10 = (f32[8,8,128]{2,1,0:T(8,128)S(1)}, f32[8,8,128]{2,1,0:T(8,128)S(1)}, u32[]{:S(2)}, u32[]{:S(2)}) collective-permute-start(f32[8,8,128]{2,1,0:T(8,128)S(1)} %get-tuple-element.43), channel_id=1, source_target_pairs={{0,24},{4,28},{8,16},{12,20},{16,8},{20,12},{24,0},{28,4},{1,25},{... | collective-permute-start | bytes 98312 | tf_op jit(solution)/shard_map/ppermute | solution.py:33
  60.3 0.1 collective-permute-done.9.refs_2_
  60.4 4.2 %collective-permute-done.10.refs_3_ = f32[8,8,128]{2,1,0:T(8,128)S(1)} collective-permute-done((f32[8,8,128]{2,1,0:T(8,128)S(1)}, f32[8,8,128]{2,1,0:T(8,128)S(1)}, u32[]{:S(2)}, u32[]{:S(2)}) %collective-permute-start.10) | collective-permute-done | bytes 32800 | tf_op jit(solution)/shard_map/ppermute | solution.py:33
  64.6 0.6 relay_stats.1
  65.2 0.1 collective-permute-start.11
  65.3 1.6 %collective-permute-start.12 = (f32[8,8,128]{2,1,0:T(8,128)S(1)}, f32[8,8,128]{2,1,0:T(8,128)S(1)}, u32[]{:S(2)}, u32[]{:S(2)}) collective-permute-start(f32[8,8,128]{2,1,0:T(8,128)S(1)} %get-tuple-element.47), channel_id=1, source_target_pairs={{0,2},{1,3},{2,0},{3,1},{4,6},{5,7},{6,4},{7,5},{8,10},{9,11},{10,... | collective-permute-start | bytes 98312 | tf_op jit(solution)/shard_map/ppermute | solution.py:33
  66.9 0.9 %collective-permute-start.13 = (f32[8,8,128]{2,1,0:T(8,128)S(1)}, f32[8,8,128]{2,1,0:T(8,128)S(1)}, u32[]{:S(2)}, u32[]{:S(2)}) collective-permute-start(f32[8,8,128]{2,1,0:T(8,128)S(1)} %get-tuple-element.48), channel_id=1, source_target_pairs={{0,3},{1,2},{2,1},{3,0},{4,7},{5,6},{6,5},{7,4},{8,11},{9,10},{10,... | collective-permute-start | bytes 98312 | tf_op jit(solution)/shard_map/ppermute | solution.py:33
  67.8 1.5 %collective-permute-done.12.refs_2_ = f32[8,8,128]{2,1,0:T(8,128)S(1)} collective-permute-done((f32[8,8,128]{2,1,0:T(8,128)S(1)}, f32[8,8,128]{2,1,0:T(8,128)S(1)}, u32[]{:S(2)}, u32[]{:S(2)}) %collective-permute-start.12) | collective-permute-done | bytes 32800 | tf_op jit(solution)/shard_map/ppermute | solution.py:33
  69.3 0.9 %collective-permute-done.13.refs_3_ = f32[8,8,128]{2,1,0:T(8,128)S(1)} collective-permute-done((f32[8,8,128]{2,1,0:T(8,128)S(1)}, f32[8,8,128]{2,1,0:T(8,128)S(1)}, u32[]{:S(2)}, u32[]{:S(2)}) %collective-permute-start.13) | collective-permute-done | bytes 32800 | tf_op jit(solution)/shard_map/ppermute | solution.py:33
  70.2 0.7 place_stats.1
  71.0 1.1 %place.1 = bf16[100,4096]{1,0:T(8,128)(2,1)} custom-call(bf16[8,100,128]{2,1,0:T(8,128)(2,1)S(1)} %get-tuple-element.29.refs_0_, bf16[8,100,128]{2,1,0:T(8,128)(2,1)S(1)} %collective-permute-done.refs_1_, bf16[8,100,128]{2,1,0:T(8,128)(2,1)S(1)} %collective-permute-done.1.refs_2_, bf16[8,100,128]{2,1,0:T(8,128)(2,1)S(1)} %collective-permute-done.2.refs_3_), custom_call_target="tpu_custom_call" | custom-call | tf_op jit(solution)/shard_map/place/pallas_call | solution.py:401
  (14 shorter events, 0.0 us)
Async XLA Ops:
  1.9 0.7 copy-start
  1.9 0.7 copy-start.1
  4.4 29.5 %all-to-all-start = ((bf16[32,104,128]{2,1,0:T(8,128)(2,1)}), bf16[32,104,128]{2,1,0:T(8,128)(2,1)S(1)}, u32[]{:S(2)}, u32[]{:S(2)}) async-start(bf16[32,104,128]{2,1,0:T(8,128)(2,1)} %get-tuple-element.28), calls=%async_computation | async-start | bytes 1703936 | tf_op jit(solution)/shard_map/all_to_all | solution.py:453
  11.7 23.8 %collective-permute-start.3 = (bf16[2,100,128]{2,1,0:T(8,128)(2,1)S(1)}, bf16[2,100,128]{2,1,0:T(8,128)(2,1)S(1)}, u32[]{:S(2)}, u32[]{:S(2)}) collective-permute-start(bf16[2,100,128]{2,1,0:T(8,128)(2,1)S(1)} %get-tuple-element.34), channel_id=1, source_target_pairs={{0,28},{4,8},{8,4},{12,16},{16,12},{20,24},{24,20},{28,0},{1,29},{... | collective-permute-start | bytes 153608 | tf_op jit(solution)/shard_map/ppermute | solution.py:26
  16.4 20.7 %collective-permute-start.4 = (bf16[2,100,128]{2,1,0:T(8,128)(2,1)S(1)}, bf16[2,100,128]{2,1,0:T(8,128)(2,1)S(1)}, u32[]{:S(2)}, u32[]{:S(2)}) collective-permute-start(bf16[2,100,128]{2,1,0:T(8,128)(2,1)S(1)} %get-tuple-element.35), channel_id=1, source_target_pairs={{0,4},{4,0},{8,12},{12,8},{16,20},{20,16},{24,28},{28,24},{1,5},{5... | collective-permute-start | bytes 153608 | tf_op jit(solution)/shard_map/ppermute | solution.py:33
  16.4 20.9 %collective-permute-start.5 = (bf16[2,100,128]{2,1,0:T(8,128)(2,1)S(1)}, bf16[2,100,128]{2,1,0:T(8,128)(2,1)S(1)}, u32[]{:S(2)}, u32[]{:S(2)}) collective-permute-start(bf16[2,100,128]{2,1,0:T(8,128)(2,1)S(1)} %get-tuple-element.36), channel_id=1, source_target_pairs={{0,3},{1,2},{2,1},{3,0},{4,7},{5,6},{6,5},{7,4},{8,11},{9,10},{10,... | collective-permute-start | bytes 153608 | tf_op jit(solution)/shard_map/ppermute | solution.py:26
  16.5 20.9 %copy-start.2 = (bf16[5,75,100]{2,1,0:T(8,128)(2,1)S(1)}, bf16[5,75,100]{2,1,0:T(8,128)(2,1)}, u32[]{:S(2)}) copy-start(bf16[5,75,100]{2,1,0:T(8,128)(2,1)} %w.1) | copy-start | bytes 225004
  16.5 20.9 %copy-start.3 = (s32[4,4096]{1,0:T(4,128)S(1)}, s32[4,4096]{1,0:T(4,128)}, u32[]{:S(2)}) copy-start(s32[4,4096]{1,0:T(4,128)} %nb.1) | copy-start | bytes 196612
  16.5 20.9 %collective-permute-start.6 = (bf16[2,100,128]{2,1,0:T(8,128)(2,1)S(1)}, bf16[2,100,128]{2,1,0:T(8,128)(2,1)S(1)}, u32[]{:S(2)}, u32[]{:S(2)}) collective-permute-start(bf16[2,100,128]{2,1,0:T(8,128)(2,1)S(1)} %get-tuple-element.37), channel_id=1, source_target_pairs={{0,1},{1,0},{2,3},{3,2},{4,5},{5,4},{6,7},{7,6},{8,9},{9,8},{10,11... | collective-permute-start | bytes 153608 | tf_op jit(solution)/shard_map/ppermute | solution.py:33
  35.4 35.5 %collective-permute-start = (bf16[8,100,128]{2,1,0:T(8,128)(2,1)S(1)}, bf16[8,100,128]{2,1,0:T(8,128)(2,1)S(1)}, u32[]{:S(2)}, u32[]{:S(2)}) collective-permute-start(bf16[8,100,128]{2,1,0:T(8,128)(2,1)S(1)} %get-tuple-element.30), channel_id=1, source_target_pairs={{0,1},{1,0},{2,3},{3,2},{4,5},{5,4},{6,7},{7,6},{8,9},{9,8},{10,11... | collective-permute-start | bytes 614408 | tf_op jit(solution)/shard_map/ppermute | solution.py:33
  35.5 35.4 %collective-permute-start.1 = (bf16[8,100,128]{2,1,0:T(8,128)(2,1)S(1)}, bf16[8,100,128]{2,1,0:T(8,128)(2,1)S(1)}, u32[]{:S(2)}, u32[]{:S(2)}) collective-permute-start(bf16[8,100,128]{2,1,0:T(8,128)(2,1)S(1)} %get-tuple-element.31), channel_id=1, source_target_pairs={{0,2},{1,3},{2,0},{3,1},{4,6},{5,7},{6,4},{7,5},{8,10},{9,11},{10,... | collective-permute-start | bytes 614408 | tf_op jit(solution)/shard_map/ppermute | solution.py:33
  37.1 33.9 %collective-permute-start.2 = (bf16[8,100,128]{2,1,0:T(8,128)(2,1)S(1)}, bf16[8,100,128]{2,1,0:T(8,128)(2,1)S(1)}, u32[]{:S(2)}, u32[]{:S(2)}) collective-permute-start(bf16[8,100,128]{2,1,0:T(8,128)(2,1)S(1)} %get-tuple-element.32), channel_id=1, source_target_pairs={{0,3},{1,2},{2,1},{3,0},{4,7},{5,6},{6,5},{7,4},{8,11},{9,10},{10,... | collective-permute-start | bytes 614408 | tf_op jit(solution)/shard_map/ppermute | solution.py:33
  50.3 4.6 %collective-permute-start.7 = (f32[16,8,128]{2,1,0:T(8,128)S(1)}, f32[16,8,128]{2,1,0:T(8,128)S(1)}, u32[]{:S(2)}, u32[]{:S(2)}) collective-permute-start(f32[16,8,128]{2,1,0:T(8,128)S(1)} %get-tuple-element.39), channel_id=1, source_target_pairs={{0,4},{4,0},{8,12},{12,8},{16,20},{20,16},{24,28},{28,24},{1,5},{5... | collective-permute-start | bytes 196616 | tf_op jit(solution)/shard_map/ppermute | solution.py:33
  54.9 4.0 %collective-permute-start.8 = (f32[8,8,128]{2,1,0:T(8,128)S(1)}, f32[8,8,128]{2,1,0:T(8,128)S(1)}, u32[]{:S(2)}, u32[]{:S(2)}) collective-permute-start(f32[8,8,128]{2,1,0:T(8,128)S(1)} %get-tuple-element.41), channel_id=1, source_target_pairs={{0,8},{4,12},{8,0},{12,4},{16,24},{20,28},{24,16},{28,20},{1,9},{5... | collective-permute-start | bytes 98312 | tf_op jit(solution)/shard_map/ppermute | solution.py:33
  55.4 5.0 %collective-permute-start.9 = (f32[8,8,128]{2,1,0:T(8,128)S(1)}, f32[8,8,128]{2,1,0:T(8,128)S(1)}, u32[]{:S(2)}, u32[]{:S(2)}) collective-permute-start(f32[8,8,128]{2,1,0:T(8,128)S(1)} %get-tuple-element.42), channel_id=1, source_target_pairs={{0,16},{4,20},{8,24},{12,28},{16,0},{20,4},{24,8},{28,12},{1,17},{... | collective-permute-start | bytes 98312 | tf_op jit(solution)/shard_map/ppermute | solution.py:33
  58.9 5.7 %collective-permute-start.10 = (f32[8,8,128]{2,1,0:T(8,128)S(1)}, f32[8,8,128]{2,1,0:T(8,128)S(1)}, u32[]{:S(2)}, u32[]{:S(2)}) collective-permute-start(f32[8,8,128]{2,1,0:T(8,128)S(1)} %get-tuple-element.43), channel_id=1, source_target_pairs={{0,24},{4,28},{8,16},{12,20},{16,8},{20,12},{24,0},{28,4},{1,25},{... | collective-permute-start | bytes 98312 | tf_op jit(solution)/shard_map/ppermute | solution.py:33
  65.2 1.6 %collective-permute-start.11 = (f32[8,8,128]{2,1,0:T(8,128)S(1)}, f32[8,8,128]{2,1,0:T(8,128)S(1)}, u32[]{:S(2)}, u32[]{:S(2)}) collective-permute-start(f32[8,8,128]{2,1,0:T(8,128)S(1)} %get-tuple-element.46), channel_id=1, source_target_pairs={{0,1},{1,0},{2,3},{3,2},{4,5},{5,4},{6,7},{7,6},{8,9},{9,8},{10,11... | collective-permute-start | bytes 98312 | tf_op jit(solution)/shard_map/ppermute | solution.py:33
  65.3 4.0 %collective-permute-start.12 = (f32[8,8,128]{2,1,0:T(8,128)S(1)}, f32[8,8,128]{2,1,0:T(8,128)S(1)}, u32[]{:S(2)}, u32[]{:S(2)}) collective-permute-start(f32[8,8,128]{2,1,0:T(8,128)S(1)} %get-tuple-element.47), channel_id=1, source_target_pairs={{0,2},{1,3},{2,0},{3,1},{4,6},{5,7},{6,4},{7,5},{8,10},{9,11},{10,... | collective-permute-start | bytes 98312 | tf_op jit(solution)/shard_map/ppermute | solution.py:33
  66.9 3.4 %collective-permute-start.13 = (f32[8,8,128]{2,1,0:T(8,128)S(1)}, f32[8,8,128]{2,1,0:T(8,128)S(1)}, u32[]{:S(2)}, u32[]{:S(2)}) collective-permute-start(f32[8,8,128]{2,1,0:T(8,128)S(1)} %get-tuple-element.48), channel_id=1, source_target_pairs={{0,3},{1,2},{2,1},{3,0},{4,7},{5,6},{6,5},{7,4},{8,11},{9,10},{10,... | collective-permute-start | bytes 98312 | tf_op jit(solution)/shard_map/ppermute | solution.py:33

commit v6 on v5

--- a/solution.py
+++ b/solution.py
@@ -386,26 +386,38 @@
     )(*parts, order)
 
 
-def place_kernel(*refs):
-    parts, out = refs[:-1], refs[-1]
+def place_kernel(flips, *refs):
+    parts, out, sems = refs[: len(flips)], refs[-2], refs[-1]
     per = parts[0].shape[0]
     mine = lax.axis_index("narrow")
-    for k, part in enumerate(parts):
+    copies = []
+    for i, part in enumerate(parts):
         for j in range(per):
-            at = pl.multiple_of(((mine ^ k) * per + j) * LANES, LANES)
-            out[:, pl.ds(at, LANES)] = part[j]
-
-
-def place(parts):
+            at = pl.multiple_of(((mine ^ flips[i]) * per + j) * LANES, LANES)
+            copies.append(
+                pltpu.make_async_copy(part.at[j], out.at[:, pl.ds(at, LANES)], sems.at[i, j])
+            )
+    for copy in copies:
+        copy.start()
+    for copy in copies:
+        copy.wait()
+
+
+def place(parts, flips, total, so_far=None):
     per, rows, _ = parts[0].shape
-    return pl.pallas_call(
-        place_kernel,
-        out_shape=jax.ShapeDtypeStruct((rows, len(parts) * per * LANES), bf16),
-        in_specs=[VMEM] * len(parts),
-        out_specs=VMEM,
+    earlier = [] if so_far is None else [so_far]
+    return pl.pallas_call(
+        lambda *refs: place_kernel(flips, *refs),
+        out_shape=jax.ShapeDtypeStruct((rows, total * per * LANES), bf16),
+        in_specs=[VMEM] * len(parts) + [HBM] * len(earlier),
+        out_specs=HBM,
+        scratch_shapes=[pltpu.SemaphoreType.DMA((len(parts), per))],
+        input_output_aliases={len(parts): 0} if earlier else {},
+        cost_estimate=pl.CostEstimate(
+            flops=0, bytes_accessed=4 * len(parts) * per * rows * LANES, transcendentals=0
+        ),
         compiler_params=grant(6 * len(parts) * per * padded_rows(rows) * LANES),
-        name="place",
-    )(*parts)
+    )(*parts, *earlier)
 
 
 def place_stats_kernel(*refs):
@@ -465,7 +477,8 @@
     stats_parts = [stats_sends[0]] + [
         swapped(stats_sends[k], "narrow", k) for k in range(1, narrow)
     ]
-    modal = place(parts)
+    modal = place(parts[:2], (0, 1), narrow)
+    modal = place(parts[2:], tuple(range(2, narrow)), narrow, modal)
     metric, work = place_stats(stats_parts)
     return modal, metric, work.reshape(-1)
 

time: 72.3 us -> 72.9 us (level)
    pallas_call x1 -> x2, Pallas kernels: 1.12 us -> 1.77 us  [place(): pl.pallas_call(lambda *refs: place_kernel(flips, *refs), out_shape=jax.Sh...]
  transfers between devices with their start and end apart: 15 -> 15, of which waited for: 7 -> 6; matrix products, arithmetic and copies ran while one was open for 0% -> 0% of each run, Pallas kernels for 22% -> 23%
where the time goes in v6:
time: 72.9 us; the launch traced here: 72.7 us
  waiting for transfers between devices  26.5 us (36%)
  starting transfers between devices  24.2 us (33%)
  Pallas kernels  20.6 us (28%)
  between operations  0.75 us (1%)
    all_to_all x1, waiting for transfers between devices, per_device(): arrived = lax.all_to_all(packed, 'wide', 0, 0, tiled=True)  15.9 us
    pallas_call x1, Pallas kernels, metrics(): pl.pallas_call(metric_kernel, out_shape=[jax.ShapeDtypeStruct((slots // p...  12.9 us
    ppermute x12, starting transfers between devices, swapped(): lax.ppermute(value, axis, [(source, source ^ flip) for source in range(co...  12.1 us
    ppermute x12, waiting for transfers between devices, swapped(): lax.ppermute(value, axis, [(source, source ^ flip) for source in range(co...  10.7 us
    all_to_all x1, starting transfers between devices, per_device(): arrived = lax.all_to_all(packed, 'wide', 0, 0, tiled=True)  7.32 us
    ppermute x2, starting transfers between devices, far_pairs(): lax.ppermute(value, axis, [(at, (at + (1 if at % 2 else -1)) % count) for...  4.81 us
    pallas_call x1, Pallas kernels, pack(): pl.pallas_call(lambda *refs: pack_kernel(wide, narrow, *refs), out_shape=...  1.82 us
    pallas_call x2, Pallas kernels, place(): pl.pallas_call(lambda *refs: place_kernel(flips, *refs), out_shape=jax.Sh...  1.77 us
  transfers between devices with their start and end apart: 15, of which 6 were waited for; matrix products, arithmetic and copies ran while one was open for 0% of the time, Pallas kernels for 23%

profile of v6, /device:TPU:0, one launch (start us, length us, event | category | flops | bytes accessed | tf_op | source)
XLA Modules:
  0.0 72.7 jit_solution(5914603301966303477)
XLA Ops:
  0.6 1.2 %halo_pack.1 = (bf16[2,100,128]{2,1,0:T(8,128)(2,1)S(1)}, bf16[2,100,128]{2,1,0:T(8,128)(2,1)S(1)}, bf16[2,100,128]{2,1,0:T(8,128)(2,1)S(1)}, bf16[2,100,128]{2,1,0:T(8,128)(2,1)S(1)}, bf16[100,4096]{1,0:T(8,128)(2,1)S(1)}) custom-call(bf16[100,4096]{1,0:T(8,128)(2,1)} %coef.1, s32[2,4]{1,0:T(2,128)} %bitcast.4), custom_call_target="tpu_custom_call" | custom-call | bytes 1638400 | tf_op jit(solution)/shard_map/halo_pack/pallas_call | solution.py:94
  1.9 0.0 copy-start
  1.9 0.0 copy-start.1
  1.9 0.6 copy-done
  2.5 0.0 copy-done.1
  2.5 1.8 %pack.1 = (bf16[32,104,128]{2,1,0:T(8,128)(2,1)}, s32[2,32]{1,0:T(2,128)S(1)}) custom-call(bf16[100,4096]{1,0:T(8,128)(2,1)S(1)} %get-tuple-element.27.refs_0_.coef, s32[32]{0:T(128)S(1)} %copy-done, s32[32]{0:T(128)S(1)} %copy-done.1), custom_call_target="tpu_custom_call" | custom-call | bytes 1638400 | tf_op jit(solution)/shard_map/pack/pallas_call | solution.py:144
  4.4 7.3 %all-to-all-start = ((bf16[32,104,128]{2,1,0:T(8,128)(2,1)}), bf16[32,104,128]{2,1,0:T(8,128)(2,1)S(1)}, u32[]{:S(2)}, u32[]{:S(2)}) async-start(bf16[32,104,128]{2,1,0:T(8,128)(2,1)} %get-tuple-element.28), calls=%async_computation | async-start | bytes 1703936 | tf_op jit(solution)/shard_map/all_to_all | solution.py:465
  11.7 4.7 %collective-permute-start.3 = (bf16[2,100,128]{2,1,0:T(8,128)(2,1)S(1)}, bf16[2,100,128]{2,1,0:T(8,128)(2,1)S(1)}, u32[]{:S(2)}, u32[]{:S(2)}) collective-permute-start(bf16[2,100,128]{2,1,0:T(8,128)(2,1)S(1)} %get-tuple-element.34), channel_id=1, source_target_pairs={{0,28},{4,8},{8,4},{12,16},{16,12},{20,24},{24,20},{28,0},{1,29},{... | collective-permute-start | bytes 153608 | tf_op jit(solution)/shard_map/ppermute | solution.py:26
  16.4 0.0 collective-permute-start.4
  16.4 0.1 collective-permute-start.5
  16.5 1.5 %collective-permute-start.6 = (bf16[2,100,128]{2,1,0:T(8,128)(2,1)S(1)}, bf16[2,100,128]{2,1,0:T(8,128)(2,1)S(1)}, u32[]{:S(2)}, u32[]{:S(2)}) collective-permute-start(bf16[2,100,128]{2,1,0:T(8,128)(2,1)S(1)} %get-tuple-element.37), channel_id=1, source_target_pairs={{0,1},{1,0},{2,3},{3,2},{4,5},{5,4},{6,7},{7,6},{8,9},{9,8},{10,11... | collective-permute-start | bytes 153608 | tf_op jit(solution)/shard_map/ppermute | solution.py:33
  18.0 15.9 %all-to-all-done.refs_0_ = bf16[32,104,128]{2,1,0:T(8,128)(2,1)S(1)} async-done(((bf16[32,104,128]{2,1,0:T(8,128)(2,1)}), bf16[32,104,128]{2,1,0:T(8,128)(2,1)S(1)}, u32[]{:S(2)}, u32[]{:S(2)}) %all-to-all-start) | async-done | bytes 852000 | tf_op jit(solution)/shard_map/all_to_all | solution.py:465
  33.9 1.5 %relay.1 = (bf16[8,100,128]{2,1,0:T(8,128)(2,1)S(1)}, bf16[8,100,128]{2,1,0:T(8,128)(2,1)S(1)}, bf16[8,100,128]{2,1,0:T(8,128)(2,1)S(1)}, bf16[8,100,128]{2,1,0:T(8,128)(2,1)S(1)}, s32[64]{0:T(128)S(1)}) custom-call(bf16[32,104,128]{2,1,0:T(8,128)(2,1)S(1)} %all-to-all-done.refs_0_), custom_call_target="tpu_custom_call" | custom-call | bytes 1638400 | tf_op jit(solution)/shard_map/relay/pallas_call | solution.py:312
  35.4 1.6 %collective-permute-start = (bf16[8,100,128]{2,1,0:T(8,128)(2,1)S(1)}, bf16[8,100,128]{2,1,0:T(8,128)(2,1)S(1)}, u32[]{:S(2)}, u32[]{:S(2)}) collective-permute-start(bf16[8,100,128]{2,1,0:T(8,128)(2,1)S(1)} %get-tuple-element.29), channel_id=1, source_target_pairs={{0,2},{1,3},{2,0},{3,1},{4,6},{5,7},{6,4},{7,5},{8,10},{9,11},{10,... | collective-permute-start | bytes 614408 | tf_op jit(solution)/shard_map/ppermute | solution.py:33
  37.0 0.6 collective-permute-start.2
  37.7 12.9 %metric.1 = (f32[16,8,128]{2,1,0:T(8,128)S(1)}, f32[16,8,128]{2,1,0:T(8,128)S(1)}) custom-call(s32[4,4096]{1,0:T(4,128)S(1)} %copy-done.3, s32[2,32]{1,0:T(2,128)S(1)} %get-tuple-element.33.routes, bf16[100,4096]{1,0:T(8,128)(2,1)S(1)} %get-tuple-element.27.refs_0_.coef, bf16[2,100,128]{2,1,0:T(8,128)(2,1)S(1)} %collective-permute-done.3.h0, ...), custom_call_target="tpu_custom_call" | custom-call | flops 671088640 | bytes 10485760 | tf_op jit(solution)/shard_map/metric/pallas_call | solution.py:255
  50.6 2.0 %collective-permute-start.7 = (f32[16,8,128]{2,1,0:T(8,128)S(1)}, f32[16,8,128]{2,1,0:T(8,128)S(1)}, u32[]{:S(2)}, u32[]{:S(2)}) collective-permute-start(f32[16,8,128]{2,1,0:T(8,128)S(1)} %get-tuple-element.39), channel_id=1, source_target_pairs={{0,4},{4,0},{8,12},{12,8},{16,20},{20,16},{24,28},{28,24},{1,5},{5... | collective-permute-start | bytes 196616 | tf_op jit(solution)/shard_map/ppermute | solution.py:33
  52.5 2.4 %collective-permute-done.7.got = f32[16,8,128]{2,1,0:T(8,128)S(1)} collective-permute-done((f32[16,8,128]{2,1,0:T(8,128)S(1)}, f32[16,8,128]{2,1,0:T(8,128)S(1)}, u32[]{:S(2)}, u32[]{:S(2)}) %collective-permute-start.7) | collective-permute-done | bytes 65568 | tf_op jit(solution)/shard_map/ppermute | solution.py:33
  54.9 0.7 collective-permute-start.8
  55.6 1.6 %collective-permute-start.9 = (f32[8,8,128]{2,1,0:T(8,128)S(1)}, f32[8,8,128]{2,1,0:T(8,128)S(1)}, u32[]{:S(2)}, u32[]{:S(2)}) collective-permute-start(f32[8,8,128]{2,1,0:T(8,128)S(1)} %get-tuple-element.42), channel_id=1, source_target_pairs={{0,16},{4,20},{8,24},{12,28},{16,0},{20,4},{24,8},{28,12},{1,17},{... | collective-permute-start | bytes 98312 | tf_op jit(solution)/shard_map/ppermute | solution.py:33
  57.2 1.7 %collective-permute-done.8.refs_1_ = f32[8,8,128]{2,1,0:T(8,128)S(1)} collective-permute-done((f32[8,8,128]{2,1,0:T(8,128)S(1)}, f32[8,8,128]{2,1,0:T(8,128)S(1)}, u32[]{:S(2)}, u32[]{:S(2)}) %collective-permute-start.8) | collective-permute-done | bytes 32800 | tf_op jit(solution)/shard_map/ppermute | solution.py:33
  58.9 1.6 %collective-permute-start.10 = (f32[8,8,128]{2,1,0:T(8,128)S(1)}, f32[8,8,128]{2,1,0:T(8,128)S(1)}, u32[]{:S(2)}, u32[]{:S(2)}) collective-permute-start(f32[8,8,128]{2,1,0:T(8,128)S(1)} %get-tuple-element.43), channel_id=1, source_target_pairs={{0,24},{4,28},{8,16},{12,20},{16,8},{20,12},{24,0},{28,4},{1,25},{... | collective-permute-start | bytes 98312 | tf_op jit(solution)/shard_map/ppermute | solution.py:33
  60.5 4.1 %collective-permute-done.10.refs_3_ = f32[8,8,128]{2,1,0:T(8,128)S(1)} collective-permute-done((f32[8,8,128]{2,1,0:T(8,128)S(1)}, f32[8,8,128]{2,1,0:T(8,128)S(1)}, u32[]{:S(2)}, u32[]{:S(2)}) %collective-permute-start.10) | collective-permute-done | bytes 32800 | tf_op jit(solution)/shard_map/ppermute | solution.py:33
  64.6 0.6 relay_stats.1
  65.2 0.1 collective-permute-start.11
  65.3 1.6 %collective-permute-start.12 = (f32[8,8,128]{2,1,0:T(8,128)S(1)}, f32[8,8,128]{2,1,0:T(8,128)S(1)}, u32[]{:S(2)}, u32[]{:S(2)}) collective-permute-start(f32[8,8,128]{2,1,0:T(8,128)S(1)} %get-tuple-element.47), channel_id=1, source_target_pairs={{0,2},{1,3},{2,0},{3,1},{4,6},{5,7},{6,4},{7,5},{8,10},{9,11},{10,... | collective-permute-start | bytes 98312 | tf_op jit(solution)/shard_map/ppermute | solution.py:33
  66.9 0.9 %collective-permute-start.13 = (f32[8,8,128]{2,1,0:T(8,128)S(1)}, f32[8,8,128]{2,1,0:T(8,128)S(1)}, u32[]{:S(2)}, u32[]{:S(2)}) collective-permute-start(f32[8,8,128]{2,1,0:T(8,128)S(1)} %get-tuple-element.48), channel_id=1, source_target_pairs={{0,3},{1,2},{2,1},{3,0},{4,7},{5,6},{6,5},{7,4},{8,11},{9,10},{10,... | collective-permute-start | bytes 98312 | tf_op jit(solution)/shard_map/ppermute | solution.py:33
  67.8 1.5 %collective-permute-done.12.refs_2_ = f32[8,8,128]{2,1,0:T(8,128)S(1)} collective-permute-done((f32[8,8,128]{2,1,0:T(8,128)S(1)}, f32[8,8,128]{2,1,0:T(8,128)S(1)}, u32[]{:S(2)}, u32[]{:S(2)}) %collective-permute-start.12) | collective-permute-done | bytes 32800 | tf_op jit(solution)/shard_map/ppermute | solution.py:33
  69.3 0.9 %collective-permute-done.13.refs_3_ = f32[8,8,128]{2,1,0:T(8,128)S(1)} collective-permute-done((f32[8,8,128]{2,1,0:T(8,128)S(1)}, f32[8,8,128]{2,1,0:T(8,128)S(1)}, u32[]{:S(2)}, u32[]{:S(2)}) %collective-permute-start.13) | collective-permute-done | bytes 32800 | tf_op jit(solution)/shard_map/ppermute | solution.py:33
  70.2 0.7 place_stats.1
  70.9 0.9 %shard_map.85.refs_2_ = bf16[100,4096]{1,0:T(8,128)(2,1)} custom-call(bf16[8,100,128]{2,1,0:T(8,128)(2,1)S(1)} %get-tuple-element.31.refs_0_, bf16[8,100,128]{2,1,0:T(8,128)(2,1)S(1)} %collective-permute-done.2.refs_1_), custom_call_target="tpu_custom_call" | custom-call | bytes 819200 | tf_op jit(solution)/shard_map/pallas_call | solution.py:409
  71.8 0.9 %shard_map.86 = bf16[100,4096]{1,0:T(8,128)(2,1)} custom-call(bf16[8,100,128]{2,1,0:T(8,128)(2,1)S(1)} %collective-permute-done.refs_0_, bf16[8,100,128]{2,1,0:T(8,128)(2,1)S(1)} %collective-permute-done.1.refs_1_, bf16[100,4096]{1,0:T(8,128)(2,1)} %shard_map.85.refs_2_), custom_call_target="tpu_custom_call", output_to_operand_aliasing={{}: (2, {})} | custom-call | bytes 819200 | tf_op jit(solution)/shard_map/pallas_call | solution.py:409
  (15 shorter events, 0.0 us)
Async XLA Ops:
  1.9 0.7 copy-start
  1.9 0.7 copy-start.1
  4.4 29.5 %all-to-all-start = ((bf16[32,104,128]{2,1,0:T(8,128)(2,1)}), bf16[32,104,128]{2,1,0:T(8,128)(2,1)S(1)}, u32[]{:S(2)}, u32[]{:S(2)}) async-start(bf16[32,104,128]{2,1,0:T(8,128)(2,1)} %get-tuple-element.28), calls=%async_computation | async-start | bytes 1703936 | tf_op jit(solution)/shard_map/all_to_all | solution.py:465
  11.7 25.3 %collective-permute-start.3 = (bf16[2,100,128]{2,1,0:T(8,128)(2,1)S(1)}, bf16[2,100,128]{2,1,0:T(8,128)(2,1)S(1)}, u32[]{:S(2)}, u32[]{:S(2)}) collective-permute-start(bf16[2,100,128]{2,1,0:T(8,128)(2,1)S(1)} %get-tuple-element.34), channel_id=1, source_target_pairs={{0,28},{4,8},{8,4},{12,16},{16,12},{20,24},{24,20},{28,0},{1,29},{... | collective-permute-start | bytes 153608 | tf_op jit(solution)/shard_map/ppermute | solution.py:26
  16.4 20.6 %collective-permute-start.4 = (bf16[2,100,128]{2,1,0:T(8,128)(2,1)S(1)}, bf16[2,100,128]{2,1,0:T(8,128)(2,1)S(1)}, u32[]{:S(2)}, u32[]{:S(2)}) collective-permute-start(bf16[2,100,128]{2,1,0:T(8,128)(2,1)S(1)} %get-tuple-element.35), channel_id=1, source_target_pairs={{0,4},{4,0},{8,12},{12,8},{16,20},{20,16},{24,28},{28,24},{1,5},{5... | collective-permute-start | bytes 153608 | tf_op jit(solution)/shard_map/ppermute | solution.py:33
  16.4 21.2 %collective-permute-start.5 = (bf16[2,100,128]{2,1,0:T(8,128)(2,1)S(1)}, bf16[2,100,128]{2,1,0:T(8,128)(2,1)S(1)}, u32[]{:S(2)}, u32[]{:S(2)}) collective-permute-start(bf16[2,100,128]{2,1,0:T(8,128)(2,1)S(1)} %get-tuple-element.36), channel_id=1, source_target_pairs={{0,3},{1,2},{2,1},{3,0},{4,7},{5,6},{6,5},{7,4},{8,11},{9,10},{10,... | collective-permute-start | bytes 153608 | tf_op jit(solution)/shard_map/ppermute | solution.py:26
  16.5 21.1 %copy-start.2 = (bf16[5,75,100]{2,1,0:T(8,128)(2,1)S(1)}, bf16[5,75,100]{2,1,0:T(8,128)(2,1)}, u32[]{:S(2)}) copy-start(bf16[5,75,100]{2,1,0:T(8,128)(2,1)} %w.1) | copy-start | bytes 225004
  16.5 21.1 %copy-start.3 = (s32[4,4096]{1,0:T(4,128)S(1)}, s32[4,4096]{1,0:T(4,128)}, u32[]{:S(2)}) copy-start(s32[4,4096]{1,0:T(4,128)} %nb.1) | copy-start | bytes 196612
  16.5 21.1 %collective-permute-start.6 = (bf16[2,100,128]{2,1,0:T(8,128)(2,1)S(1)}, bf16[2,100,128]{2,1,0:T(8,128)(2,1)S(1)}, u32[]{:S(2)}, u32[]{:S(2)}) collective-permute-start(bf16[2,100,128]{2,1,0:T(8,128)(2,1)S(1)} %get-tuple-element.37), channel_id=1, source_target_pairs={{0,1},{1,0},{2,3},{3,2},{4,5},{5,4},{6,7},{7,6},{8,9},{9,8},{10,11... | collective-permute-start | bytes 153608 | tf_op jit(solution)/shard_map/ppermute | solution.py:33
  35.4 36.4 %collective-permute-start = (bf16[8,100,128]{2,1,0:T(8,128)(2,1)S(1)}, bf16[8,100,128]{2,1,0:T(8,128)(2,1)S(1)}, u32[]{:S(2)}, u32[]{:S(2)}) collective-permute-start(bf16[8,100,128]{2,1,0:T(8,128)(2,1)S(1)} %get-tuple-element.29), channel_id=1, source_target_pairs={{0,2},{1,3},{2,0},{3,1},{4,6},{5,7},{6,4},{7,5},{8,10},{9,11},{10,... | collective-permute-start | bytes 614408 | tf_op jit(solution)/shard_map/ppermute | solution.py:33
  37.0 34.8 %collective-permute-start.1 = (bf16[8,100,128]{2,1,0:T(8,128)(2,1)S(1)}, bf16[8,100,128]{2,1,0:T(8,128)(2,1)S(1)}, u32[]{:S(2)}, u32[]{:S(2)}) collective-permute-start(bf16[8,100,128]{2,1,0:T(8,128)(2,1)S(1)} %get-tuple-element.30), channel_id=1, source_target_pairs={{0,3},{1,2},{2,1},{3,0},{4,7},{5,6},{6,5},{7,4},{8,11},{9,10},{10,... | collective-permute-start | bytes 614408 | tf_op jit(solution)/shard_map/ppermute | solution.py:33
  37.0 33.9 %collective-permute-start.2 = (bf16[8,100,128]{2,1,0:T(8,128)(2,1)S(1)}, bf16[8,100,128]{2,1,0:T(8,128)(2,1)S(1)}, u32[]{:S(2)}, u32[]{:S(2)}) collective-permute-start(bf16[8,100,128]{2,1,0:T(8,128)(2,1)S(1)} %get-tuple-element.32), channel_id=1, source_target_pairs={{0,1},{1,0},{2,3},{3,2},{4,5},{5,4},{6,7},{7,6},{8,9},{9,8},{10,11... | collective-permute-start | bytes 614408 | tf_op jit(solution)/shard_map/ppermute | solution.py:33
  50.6 4.3 %collective-permute-start.7 = (f32[16,8,128]{2,1,0:T(8,128)S(1)}, f32[16,8,128]{2,1,0:T(8,128)S(1)}, u32[]{:S(2)}, u32[]{:S(2)}) collective-permute-start(f32[16,8,128]{2,1,0:T(8,128)S(1)} %get-tuple-element.39), channel_id=1, source_target_pairs={{0,4},{4,0},{8,12},{12,8},{16,20},{20,16},{24,28},{28,24},{1,5},{5... | collective-permute-start | bytes 196616 | tf_op jit(solution)/shard_map/ppermute | solution.py:33
  54.9 4.0 %collective-permute-start.8 = (f32[8,8,128]{2,1,0:T(8,128)S(1)}, f32[8,8,128]{2,1,0:T(8,128)S(1)}, u32[]{:S(2)}, u32[]{:S(2)}) collective-permute-start(f32[8,8,128]{2,1,0:T(8,128)S(1)} %get-tuple-element.41), channel_id=1, source_target_pairs={{0,8},{4,12},{8,0},{12,4},{16,24},{20,28},{24,16},{28,20},{1,9},{5... | collective-permute-start | bytes 98312 | tf_op jit(solution)/shard_map/ppermute | solution.py:33
  55.6 4.9 %collective-permute-start.9 = (f32[8,8,128]{2,1,0:T(8,128)S(1)}, f32[8,8,128]{2,1,0:T(8,128)S(1)}, u32[]{:S(2)}, u32[]{:S(2)}) collective-permute-start(f32[8,8,128]{2,1,0:T(8,128)S(1)} %get-tuple-element.42), channel_id=1, source_target_pairs={{0,16},{4,20},{8,24},{12,28},{16,0},{20,4},{24,8},{28,12},{1,17},{... | collective-permute-start | bytes 98312 | tf_op jit(solution)/shard_map/ppermute | solution.py:33
  58.9 5.7 %collective-permute-start.10 = (f32[8,8,128]{2,1,0:T(8,128)S(1)}, f32[8,8,128]{2,1,0:T(8,128)S(1)}, u32[]{:S(2)}, u32[]{:S(2)}) collective-permute-start(f32[8,8,128]{2,1,0:T(8,128)S(1)} %get-tuple-element.43), channel_id=1, source_target_pairs={{0,24},{4,28},{8,16},{12,20},{16,8},{20,12},{24,0},{28,4},{1,25},{... | collective-permute-start | bytes 98312 | tf_op jit(solution)/shard_map/ppermute | solution.py:33
  65.2 1.6 %collective-permute-start.11 = (f32[8,8,128]{2,1,0:T(8,128)S(1)}, f32[8,8,128]{2,1,0:T(8,128)S(1)}, u32[]{:S(2)}, u32[]{:S(2)}) collective-permute-start(f32[8,8,128]{2,1,0:T(8,128)S(1)} %get-tuple-element.46), channel_id=1, source_target_pairs={{0,1},{1,0},{2,3},{3,2},{4,5},{5,4},{6,7},{7,6},{8,9},{9,8},{10,11... | collective-permute-start | bytes 98312 | tf_op jit(solution)/shard_map/ppermute | solution.py:33
  65.3 4.0 %collective-permute-start.12 = (f32[8,8,128]{2,1,0:T(8,128)S(1)}, f32[8,8,128]{2,1,0:T(8,128)S(1)}, u32[]{:S(2)}, u32[]{:S(2)}) collective-permute-start(f32[8,8,128]{2,1,0:T(8,128)S(1)} %get-tuple-element.47), channel_id=1, source_target_pairs={{0,2},{1,3},{2,0},{3,1},{4,6},{5,7},{6,4},{7,5},{8,10},{9,11},{10,... | collective-permute-start | bytes 98312 | tf_op jit(solution)/shard_map/ppermute | solution.py:33
  66.9 3.4 %collective-permute-start.13 = (f32[8,8,128]{2,1,0:T(8,128)S(1)}, f32[8,8,128]{2,1,0:T(8,128)S(1)}, u32[]{:S(2)}, u32[]{:S(2)}) collective-permute-start(f32[8,8,128]{2,1,0:T(8,128)S(1)} %get-tuple-element.48), channel_id=1, source_target_pairs={{0,3},{1,2},{2,1},{3,0},{4,7},{5,6},{6,5},{7,4},{8,11},{9,10},{10,... | collective-permute-start | bytes 98312 | tf_op jit(solution)/shard_map/ppermute | solution.py:33
